TPU v7x, 128 devices: a whole 4x4x4 slice. The times are simulated.
128 devices in a mesh: row: 16 (over y, z), col: 8 (over x, core).
Axes of the slice: x: 4, y: 4, z: 4, core: 2. Of those that a mesh axis runs over, the one named last changes fastest.
Arguments:
- grad_window: float32 [8192, 14336], P('row', 'col'), may hold values from -6 to 6
- rows_first: float32 [8192, 256], P('row'), may hold values from -0.0625 to 0.0625
- cols_first: float32 [14336, 256], P('col'), may hold values from -0.046875 to 0.046875
- rows_second: float32 [8192, 256], P('row'), may hold values from -0.0625 to 0.0625
- cols_second: float32 [14336, 256], P('col'), may hold values from -0.046875 to 0.046875
- inverse_first: float32 [256, 256], replicated, may hold values from -2 to 2, as said below
- inverse_second: float32 [256, 256], replicated, may hold values from -2 to 2, as said below
Outputs:
- panel_second: float32 [8192, 256], P('row')
- pivot_second: float32 [14336, 256], P('col')
- panel_first: float32 [8192, 256], P('row')
- pivot_first: float32 [14336, 256], P('col')
Inputs may be any that keep to these rules, and one draw needn't show every extreme that they name: `inverse_first`: lower triangular, diagonal entries between 1 and 2. `inverse_second`: lower triangular, diagonal entries between 1 and 2.
All inputs are finite; a program needn't handle non-finite values.
Results may differ from a plain program's by a relative error of at most 0.000071.
Values sent between devices are 32-bit elements; how exact they have to be, the bound alone decides.
No kernel may reach another device: no remote copies, remote signals or barrier semaphores. Data moves between devices by JAX's collectives and lax.ppermute only.
A program may use at most 64 MiB of HBM per device.

v0:
```python
import jax
import jax.numpy as jnp
from jax import lax
from jax.sharding import PartitionSpec as P


def matmul(left, right):
    return jnp.dot(left, right, precision=lax.Precision.HIGHEST, preferred_element_type=jnp.float32)


def tmatmul(left, right):
    return lax.dot_general(
        left,
        right,
        (((0,), (0,)), ((), ())),
        precision=lax.Precision.HIGHEST,
        preferred_element_type=jnp.float32,
    )


def local(
    grad_window, rows_first, cols_first, rows_second, cols_second, inverse_first, inverse_second
):
    col_count = lax.axis_size("col")
    is_last = lax.axis_index("col") == col_count - 1
    tile_cols = grad_window.shape[1]
    width = inverse_first.shape[0]
    left_sum = lax.psum(matmul(grad_window, cols_second), "col")
    panel_second = matmul(-left_sum, inverse_second)
    pivot_sum = lax.psum(tmatmul(grad_window, rows_second), "row")
    pivot_second = matmul(-pivot_sum, inverse_second)
    grad_next = grad_window.at[:, tile_cols - width :].add(jnp.where(is_last, panel_second, 0.0))
    left_next = lax.psum(matmul(grad_next, cols_first), "col")
    panel_first = matmul(-left_next, inverse_first)
    pivot_next = lax.psum(tmatmul(grad_next, rows_first), "row")
    pivot_first = matmul(-pivot_next, inverse_first)
    return (panel_second, pivot_second, panel_first, pivot_first)


def solution(mesh):
    in_specs = (
        P("row", "col"),
        P("row", None),
        P("col", None),
        P("row", None),
        P("col", None),
        P(),
        P(),
    )
    out_specs = (P("row", None), P("col", None), P("row", None), P("col", None))
    return jax.shard_map(local, mesh=mesh, in_specs=in_specs, out_specs=out_specs, check_vma=False)
```

profile of v0, /device:TPU:0, one launch (start us, length us, event | category | flops | bytes accessed | tf_op | source)
XLA Modules:
  0.0 263.5 jit_solution(18278489078048997041)
XLA Ops:
  7.2 0.0 copy-start
  7.2 0.0 all-reduce.5.cloned.1.call-start
  7.2 2.2 copy.17
  9.4 0.0 copy-start.1
  9.4 1.8 copy-done.1
  11.2 0.0 copy-done
  11.2 0.0 copy-start.6
  11.2 3.8 %fusion.8 = f32[512,256]{1,0:T(8,128)} fusion(f32[512,1792]{1,0:T(8,128)S(1)} %copy.17, f32[1792,256]{1,0:T(8,128)S(1)} %copy-done), kind=kOutput, calls=%fused_computation.9 | convolution fusion | flops 2818572288 | bytes 6029312 | tf_op jit(solution)/shard_map/dot_general | solution.py:8
  15.0 0.0 all-reduce.5.cloned.1.call-update
  15.1 0.2 all-reduce.7.cloned.1.call-start
  15.3 0.0 copy-done.6
  15.3 0.0 copy-start.4
  15.3 9.2 %fusion.9 = f32[1792,256]{1,0:T(8,128)} fusion(f32[512,1792]{1,0:T(8,128)} %copy-done.1, f32[512,256]{1,0:T(8,128)S(1)} %copy-done.6), kind=kOutput, calls=%fused_computation.10 | convolution fusion | flops 2818572288 | bytes 6029312 | tf_op jit(solution)/shard_map/dot_general | solution.py:12
  24.5 53.7 %all-reduce.5.cloned.1.call-done = f32[512,256]{1,0:T(8,128)} async-done(((f32[512,256]{1,0:T(8,128)}), f32[512,256]{1,0:T(8,128)}) %all-reduce.5.cloned.1.call-update) | async-done | bytes 524304 | tf_op jit(solution)/shard_map/psum | solution.py:28
  78.2 0.0 copy-done.4
  78.2 0.0 copy-start.2
  78.2 2.9 %add_dynamic-update-slice_fusion = (f32[512,1792]{1,0:T(8,128)}, f32[512,256]{1,0:T(8,128)}) fusion(f32[512,1792]{1,0:T(8,128)} %copy-done.1, pred[]{:T(512)S(6)} %eq.3, f32[256,256]{1,0:T(8,128)S(1)} %copy-done.4, f32[512,256]{1,0:T(8,128)} %all-reduce.5.cloned.1.call-done), kind=kOutput, calls=%fused_computation.6 | convolution fusion | flops 403046400 | bytes 2359297 | tf_op jit(solution)/shard_map/dot_general | solution.py:8
  81.2 0.0 copy-done.2
  81.2 0.0 copy-start.7
  81.2 5.9 %fusion.10 = f32[512,256]{1,0:T(8,128)} fusion(f32[512,1792]{1,0:T(8,128)} %get-tuple-element.18, f32[1792,256]{1,0:T(8,128)S(1)} %copy-done.2), kind=kOutput, calls=%fused_computation.11 | convolution fusion | flops 2818572288 | bytes 6029312 | tf_op jit(solution)/shard_map/dot_general | solution.py:8
  87.1 0.0 all-reduce.7.cloned.1.call-update
  87.1 0.3 all-reduce.9.cloned.1.call-start
  87.4 0.0 copy-done.7
  87.4 9.1 %fusion.11 = f32[1792,256]{1,0:T(8,128)} fusion(f32[512,1792]{1,0:T(8,128)} %get-tuple-element.18, f32[512,256]{1,0:T(8,128)S(1)} %copy-done.7), kind=kOutput, calls=%fused_computation.12 | convolution fusion | flops 2818572288 | bytes 6029312 | tf_op jit(solution)/shard_map/dot_general | solution.py:12
  96.6 0.0 copy-start.5
  96.6 0.0 all-reduce.9.cloned.1.call-update
  96.6 50.5 %all-reduce.7.cloned.1.call-done = f32[512,256]{1,0:T(8,128)} async-done(((f32[512,256]{1,0:T(8,128)}), f32[512,256]{1,0:T(8,128)}) %all-reduce.7.cloned.1.call-update) | async-done | bytes 524304 | tf_op jit(solution)/shard_map/psum | solution.py:33
  147.1 0.0 copy-done.5
  147.1 2.4 fusion.4
  149.5 100.2 %all-reduce.9.cloned.1.call-done = (f32[1792,256]{1,0:T(8,128)}, f32[1792,256]{1,0:T(8,128)}) async-done(((f32[1792,256]{1,0:T(8,128)}, f32[1792,256]{1,0:T(8,128)}), (f32[1792,256]{1,0:T(8,128)}, f32[1792,256]{1,0:T(8,128)})) %all-reduce.9.cloned.1.call-update) | async-done | bytes 3670032 | tf_op jit(solution)/shard_map/psum | solution.py:30
  249.7 0.0 copy-start.3
  249.7 4.5 %fusion.2 = f32[1792,256]{1,0:T(8,128)} fusion(f32[256,256]{1,0:T(8,128)S(1)} %copy-done.4, f32[1792,256]{1,0:T(8,128)} %get-tuple-element.16), kind=kOutput, calls=%fused_computation.2 | convolution fusion | flops 1409744896 | bytes 3932160 | tf_op jit(solution)/shard_map/dot_general | solution.py:8
  254.2 0.0 copy-done.3
  254.2 2.8 %fusion = f32[1792,256]{1,0:T(8,128)} fusion(f32[256,256]{1,0:T(8,128)S(1)} %copy-done.5, f32[1792,256]{1,0:T(8,128)S(1)} %copy-done.3), kind=kOutput, calls=%fused_computation | convolution fusion | flops 1409744896 | bytes 3932160 | tf_op jit(solution)/shard_map/dot_general | solution.py:8
Async XLA Ops:
  7.2 4.0 %copy-start = (f32[1792,256]{1,0:T(8,128)S(1)}, f32[1792,256]{1,0:T(8,128)}, u32[]{:S(2)}) copy-start(f32[1792,256]{1,0:T(8,128)} %param.13) | copy-start | bytes 5505028
  7.2 71.1 %all-reduce.5.cloned.1.call-start = ((), (), s32[]{:S(2)}) async-start(), calls=%async_computation | async-start | bytes 1048576 | tf_op jit(solution)/shard_map/psum | solution.py:28
  9.4 1.8 copy-start.1
  11.2 4.1 %copy-start.6 = (f32[512,256]{1,0:T(8,128)S(1)}, f32[512,256]{1,0:T(8,128)}, u32[]{:S(2)}) copy-start(f32[512,256]{1,0:T(8,128)} %param.12) | copy-start | bytes 1572868
  15.1 132.0 %all-reduce.7.cloned.1.call-start = ((), (), s32[]{:S(2)}) async-start(), calls=%async_computation.1 | async-start | bytes 1048576 | tf_op jit(solution)/shard_map/psum | solution.py:33
  15.3 62.9 %copy-start.4 = (f32[256,256]{1,0:T(8,128)S(1)}, f32[256,256]{1,0:T(8,128)}, u32[]{:S(2)}) copy-start(f32[256,256]{1,0:T(8,128)} %param.15) | copy-start | bytes 786436
  78.2 2.9 %copy-start.2 = (f32[1792,256]{1,0:T(8,128)S(1)}, f32[1792,256]{1,0:T(8,128)}, u32[]{:S(2)}) copy-start(f32[1792,256]{1,0:T(8,128)} %param.11) | copy-start | bytes 5505028
  81.2 6.2 %copy-start.7 = (f32[512,256]{1,0:T(8,128)S(1)}, f32[512,256]{1,0:T(8,128)}, u32[]{:S(2)}) copy-start(f32[512,256]{1,0:T(8,128)} %param.10) | copy-start | bytes 1572868
  87.1 162.6 %all-reduce.9.cloned.1.call-start = ((), (), s32[]{:S(2)}) async-start(), calls=%async_computation.2 | async-start | bytes 7340032 | tf_op jit(solution)/shard_map/psum | solution.py:30
  96.6 50.5 %copy-start.5 = (f32[256,256]{1,0:T(8,128)S(1)}, f32[256,256]{1,0:T(8,128)}, u32[]{:S(2)}) copy-start(f32[256,256]{1,0:T(8,128)} %param.14) | copy-start | bytes 786436
  249.7 4.5 %copy-start.3 = (f32[1792,256]{1,0:T(8,128)S(1)}, f32[1792,256]{1,0:T(8,128)}, u32[]{:S(2)}) copy-start(f32[1792,256]{1,0:T(8,128)} %get-tuple-element.17) | copy-start | bytes 5505028
Sparse Core Ops, SparseCore 0:
  15.2 63.0 all-reduce.4
  87.3 59.7 all-reduce.6
  151.1 98.5 all-reduce.8
where the time goes:
time: 264 us
  waiting for transfers between devices  204 us (77%)
  matrix products  40.8 us (15%)
  between operations  13.8 us (5%)
  local copies, waits for them, and re-layouts  4 us (2%)
    psum x1, waiting for transfers between devices, local(): pivot_sum = lax.psum(tmatmul(grad_window, rows_second), 'row')  100 us
    psum x1, waiting for transfers between devices, local(): left_sum = lax.psum(matmul(grad_window, cols_second), 'col')  53.7 us
    psum x1, waiting for transfers between devices, local(): left_next = lax.psum(matmul(grad_next, cols_first), 'col')  50.5 us
    dot_general x6, matrix products, matmul(): jnp.dot(left, right, precision=lax.Precision.HIGHEST, preferred_element_t...  22.4 us
    dot_general x2, matrix products, tmatmul(): lax.dot_general(left, right, (((0,), (0,)), ((), ())), precision=lax.Prec...  18.3 us
  transfers between devices with their start and end apart: 3, of which 3 were waited for; matrix products, arithmetic and copies ran while one was open for 8% of the time, Pallas kernels for 0%

commit v1 on v0

v1 whole, which is shorter than its diff:
```python
import jax
import jax.numpy as jnp
from jax import lax
from jax.sharding import PartitionSpec as P

SIDE = 4


def matmul(left, right):
    return jnp.dot(left, right, precision=lax.Precision.HIGH, preferred_element_type=jnp.float32)


def tmatmul(left, right):
    return lax.dot_general(
        left,
        right,
        (((0,), (0,)), ((), ())),
        precision=lax.Precision.HIGH,
        preferred_element_type=jnp.float32,
    )


def row_pairs(dy, dz):
    return [
        (y * SIDE + z, ((y + dy) % SIDE) * SIDE + (z + dz) % SIDE)
        for y in range(SIDE)
        for z in range(SIDE)
    ]


def shift_y(value, step):
    return lax.ppermute(value, "row", row_pairs(step, 0))


def shift_z(value, step):
    return lax.ppermute(value, "row", row_pairs(0, step))


def shift_x(value, step):
    pairs = [(x * 2 + k, ((x + step) % SIDE) * 2 + k) for x in range(SIDE) for k in range(2)]
    return lax.ppermute(value, "col", pairs)


def swap_core(value):
    return lax.ppermute(value, "col", [(c, c ^ 1) for c in range(2 * SIDE)])


def block(value, index):
    return lax.dynamic_index_in_dim(value, index, 0, keepdims=False)


STEPS = (2, 1, 3)


def scatter_stage(parts):
    got = [[] for _ in parts]
    for step in STEPS:
        for i, (blocks, place, shift) in enumerate(parts):
            got[i].append(shift(block(blocks, (place + step) % SIDE), step))
    return [
        block(blocks, place) + got[i][0] + got[i][1] + got[i][2]
        for i, (blocks, place, _) in enumerate(parts)
    ]


def gather_stage(parts):
    out = [
        lax.dynamic_update_index_in_dim(jnp.zeros((SIDE,) + own.shape, own.dtype), own, place, 0)
        for own, place, _ in parts
    ]
    for step in STEPS:
        for i, (own, place, shift) in enumerate(parts):
            got = shift(own, step)
            out[i] = lax.dynamic_update_index_in_dim(out[i], got, (place - step) % SIDE, 0)
    return out


def row_sum(partial, y, z, finish):
    rows, width = partial.shape
    half, quarter, piece = rows // 2, rows // 8, rows // 32
    first = partial[:half].reshape(SIDE, quarter, width)
    second = partial[half:].reshape(SIDE, quarter, width)
    first, second = scatter_stage([(first, y, shift_y), (second, z, shift_z)])
    first, second = scatter_stage(
        [
            (first.reshape(SIDE, piece, width), z, shift_z),
            (second.reshape(SIDE, piece, width), y, shift_y),
        ]
    )
    done = finish(jnp.concatenate([first, second], 0))
    first, second = gather_stage([(done[:piece], z, shift_z), (done[piece:], y, shift_y)])
    first, second = gather_stage(
        [(first.reshape(quarter, width), y, shift_y), (second.reshape(quarter, width), z, shift_z)]
    )
    return jnp.concatenate([first.reshape(half, width), second.reshape(half, width)], 0)


def local(
    grad_window, rows_first, cols_first, rows_second, cols_second, inverse_first, inverse_second
):
    row = lax.axis_index("row")
    col = lax.axis_index("col")
    y, z = row // SIDE, row % SIDE
    x, core = col // 2, col % 2
    last = 2 * SIDE - 1
    is_last = col == last
    tile_cols = grad_window.shape[1]
    tile_rows = grad_window.shape[0]
    width = inverse_first.shape[0]

    tail = cols_first[tile_cols - width :]
    held = jnp.where(is_last, tail, 0.0)
    for target in (1, 5, 3):
        held = held + lax.ppermute(tail, "col", [(last, target)])
    other = lax.ppermute(held, "col", [(2 * i + 1, 2 * i) for i in range(SIDE)])
    tail = jnp.where(core == 1, held, other)

    left = matmul(grad_window, jnp.concatenate([cols_second, cols_first], 1))
    left = left.reshape(2, tile_rows // 2, 2 * width)
    left = block(left, core) + swap_core(block(left, 1 - core))
    (left,) = scatter_stage([(left.reshape(SIDE, tile_rows // 8, 2 * width), x, shift_x)])
    share_second = matmul(-left[:, :width], inverse_second)
    share_first = matmul(-(left[:, width:] + matmul(share_second, tail)), inverse_first)
    share = jnp.concatenate([share_second, share_first], 1)
    (half,) = gather_stage([(share, x, shift_x)])
    half = half.reshape(tile_rows // 2, 2 * width)
    both = jnp.stack([half, swap_core(half)])
    panels = jnp.concatenate([block(both, core), block(both, 1 - core)], 0)
    panel_second, panel_first = panels[:, :width], panels[:, width:]

    pivot_second = row_sum(
        tmatmul(grad_window, rows_second), y, z, lambda total: matmul(-total, inverse_second)
    )
    end = grad_window[:, tile_cols - width :] + jnp.where(is_last, panel_second, 0.0)
    partial = jnp.concatenate(
        [tmatmul(grad_window[:, : tile_cols - width], rows_first), tmatmul(end, rows_first)], 0
    )
    pivot_first = row_sum(partial, y, z, lambda total: matmul(-total, inverse_first))
    return (panel_second, pivot_second, panel_first, pivot_first)


def solution(mesh):
    in_specs = (
        P("row", "col"),
        P("row", None),
        P("col", None),
        P("row", None),
        P("col", None),
        P(),
        P(),
    )
    out_specs = (P("row", None), P("col", None), P("row", None), P("col", None))
    return jax.shard_map(local, mesh=mesh, in_specs=in_specs, out_specs=out_specs, check_vma=False)
```

time: 264 us -> 159 us (0.60)
  waiting for transfers between devices: 204 us -> 39.6 us
  starting transfers between devices: 0.52 us -> 81.8 us
  matrix products: 40.8 us -> 18.7 us
  between operations: 13.8 us -> 1.69 us
  other arithmetic: 0 us -> 8.81 us
  local copies, waits for them, and re-layouts: 4 us -> 8.19 us
    psum x3 -> x0, waiting for transfers between devices: 204 us -> none  [the longest x1 100 us: local(): pivot_sum = lax.psum(tmatmul(grad_window, rows_second), 'row')]
    ppermute x0 -> x60, starting transfers between devices: none -> 81.8 us  [the longest x24 35.3 us: shift_y(): return lax.ppermute(value, 'row', row_pairs(step, 0))]
    ppermute x0 -> x60, waiting for transfers between devices: none -> 39.6 us  [the longest x24 20.3 us: shift_z(): return lax.ppermute(value, 'row', row_pairs(0, step))]
    dot_general x6, matrix products: 22.4 us -> 7.33 us  [matmul(): jnp.dot(left, right, precision=lax.Precision.HIGH, preferred_element_type...]
    dot_general x2 -> x3, matrix products: 18.3 us -> 11.4 us  [tmatmul(): lax.dot_general(left, right, (((0,), (0,)), ((), ())), precision=lax.Prec...]
    add x0 -> x9, other arithmetic: none -> 3.8 us  [the longest x7 2.69 us: scatter_stage(): block(blocks, place) + got[i][0] + got[i][1] + got[i][2]]
    concatenate x0 -> x4, other arithmetic: none -> 3.59 us  [the longest x2 2.7 us: row_sum(): jnp.concatenate([first.reshape(half, width), second.reshape(half, width)]...]
    squeeze x0 -> x10, local copies, waits for them, and re-layouts: none -> 2.85 us  [block(): return lax.dynamic_index_in_dim(value, index, 0, keepdims=False)]
  transfers between devices with their start and end apart: 3 -> 60, of which waited for: 3 -> 16; matrix products, arithmetic and copies ran while one was open for 8% -> 16% of each run, Pallas kernels for 0% -> 0%
where the time goes in v1:
time: 159 us
  starting transfers between devices  81.8 us (51%)
  waiting for transfers between devices  39.6 us (25%)
  matrix products  18.7 us (12%)
  other arithmetic  8.81 us (6%)
  local copies, waits for them, and re-layouts  8.19 us (5%)
  between operations  1.69 us (1%)
    ppermute x24, starting transfers between devices, shift_y(): return lax.ppermute(value, 'row', row_pairs(step, 0))  35.3 us
    ppermute x24, starting transfers between devices, shift_z(): return lax.ppermute(value, 'row', row_pairs(0, step))  31.8 us
    ppermute x24, waiting for transfers between devices, shift_z(): return lax.ppermute(value, 'row', row_pairs(0, step))  20.3 us
    ppermute x24, waiting for transfers between devices, shift_y(): return lax.ppermute(value, 'row', row_pairs(step, 0))  12.3 us
    dot_general x3, matrix products, tmatmul(): lax.dot_general(left, right, (((0,), (0,)), ((), ())), precision=lax.Prec...  11.4 us
    ppermute x6, starting transfers between devices, shift_x(): return lax.ppermute(value, 'col', pairs)  11.1 us
    dot_general x6, matrix products, matmul(): jnp.dot(left, right, precision=lax.Precision.HIGH, preferred_element_type...  7.33 us
    ppermute x6, waiting for transfers between devices, shift_x(): return lax.ppermute(value, 'col', pairs)  6.93 us
  transfers between devices with their start and end apart: 60, of which 16 were waited for; matrix products, arithmetic and copies ran while one was open for 16% of the time, Pallas kernels for 0%

profile of v1, /device:TPU:0, one launch (start us, length us, event | category | flops | bytes accessed | tf_op | source)
XLA Modules:
  0.0 158.7 jit_solution(7193626715064540008)
XLA Ops:
  0.7 6.2 %fusion = f32[512,512]{0,1:T(8,128)S(1)} fusion(f32[512,1792]{1,0:T(8,128)} %param.7, f32[1792,256]{1,0:T(8,128)} %param.9, f32[1792,256]{1,0:T(8,128)} %param.11), kind=kOutput, calls=%fused_computation | convolution fusion | flops 2819489792 | bytes 8388608 | tf_op jit(solution)/shard_map/dot_general | solution.py:10
  7.1 1.7 %slice.47 = f32[256,256]{1,0:T(8,128)} slice(f32[1792,256]{1,0:T(8,128)} %param.9), slice={[1536:1792], [0:256]} | slice | bytes 524288 | tf_op jit(solution)/shard_map/slice | solution.py:111
  10.9 5.1 %fusion.56 = f32[1792,256]{1,0:T(8,128)S(1)} fusion(f32[512,1792]{1,0:T(8,128)} %param.7, f32[512,256]{1,0:T(8,128)S(1)} %copy-done), kind=kOutput, calls=%fused_computation.145 | convolution fusion | flops 1409286144 | bytes 6029312 | tf_op jit(solution)/shard_map/dot_general | solution.py:14
  16.2 3.2 %collective-permute-start.1 = (f32[64,512]{1,0:T(8,128)S(1)}, f32[64,512]{1,0:T(8,128)S(1)}, u32[]{:S(2)}, u32[]{:S(2)}) collective-permute-start(f32[64,512]{1,0:T(8,128)S(1)} %get-tuple-element.24), channel_id=1, source_target_pairs={{0,4},{1,5},{2,6},{3,7},{4,0},{5,1},{6,2},{7,3},{8,12},{9,13},{10,... | collective-permute-start | bytes 393224 | tf_op jit(solution)/shard_map/ppermute | solution.py:41
  20.0 2.6 %collective-permute-start.3 = (f32[64,512]{1,0:T(8,128)S(1)}, f32[64,512]{1,0:T(8,128)S(1)}, u32[]{:S(2)}, u32[]{:S(2)}) collective-permute-start(f32[64,512]{1,0:T(8,128)S(1)} %get-tuple-element.25), channel_id=1, source_target_pairs={{0,6},{1,7},{2,0},{3,1},{4,2},{5,3},{6,4},{7,5},{8,14},{9,15},{10,... | collective-permute-start | bytes 393224 | tf_op jit(solution)/shard_map/ppermute | solution.py:41
  23.7 1.3 collective-permute-start.7
  25.0 2.0 %collective-permute-done.2 = f32[64,512]{1,0:T(8,128)S(1)} collective-permute-done((f32[64,512]{1,0:T(8,128)S(1)}, f32[64,512]{1,0:T(8,128)S(1)}, u32[]{:S(2)}, u32[]{:S(2)}) %collective-permute-start.2) | collective-permute-done | bytes 131104 | tf_op jit(solution)/shard_map/ppermute | solution.py:41
  27.9 1.4 collective-permute-start.8
  29.5 3.3 %collective-permute-start.9 = (f32[64,512]{1,0:T(8,128)S(1)}, f32[64,512]{1,0:T(8,128)S(1)}, u32[]{:S(2)}, u32[]{:S(2)}) collective-permute-start(f32[64,512]{1,0:T(8,128)S(1)} %pad_maximum_fusion.4), channel_id=1, source_target_pairs={{0,2},{1,3},{2,4},{3,5},{4,6},{5,7},{6,0},{7,1},{8,10},{9,11},{10,... | collective-permute-start | bytes 393224 | tf_op jit(solution)/shard_map/ppermute | solution.py:41
  33.0 2.9 %collective-permute-done.8 = f32[64,512]{1,0:T(8,128)} collective-permute-done((f32[64,512]{1,0:T(8,128)S(1)}, f32[64,512]{1,0:T(8,128)}, u32[]{:S(2)}, u32[]{:S(2)}) %collective-permute-start.8) | collective-permute-done | bytes 131104 | tf_op jit(solution)/shard_map/ppermute | solution.py:41
  36.8 1.3 collective-permute-done.9
  39.6 3.2 %collective-permute-start.12 = (f32[224,256]{1,0:T(8,128)}, f32[224,256]{1,0:T(8,128)}, u32[]{:S(2)}, u32[]{:S(2)}) collective-permute-start(f32[224,256]{1,0:T(8,128)} %get-tuple-element.18), channel_id=1, source_target_pairs={{0,64},{8,72},{16,80},{24,88},{32,96},{40,104},{48,112},{56,120},{... | collective-permute-start | bytes 688136 | tf_op jit(solution)/shard_map/ppermute | solution.py:32
  43.5 2.6 %collective-permute-start.14 = (f32[224,256]{1,0:T(8,128)}, f32[224,256]{1,0:T(8,128)}, u32[]{:S(2)}, u32[]{:S(2)}) collective-permute-start(f32[224,256]{1,0:T(8,128)} %get-tuple-element.19), channel_id=1, source_target_pairs={{0,96},{8,104},{16,112},{24,120},{32,0},{40,8},{48,16},{56,24},{64... | collective-permute-start | bytes 688136 | tf_op jit(solution)/shard_map/ppermute | solution.py:32
  47.0 3.9 %collective-permute-start.18 = (f32[224,256]{1,0:T(8,128)}, f32[224,256]{1,0:T(8,128)}, u32[]{:S(2)}, u32[]{:S(2)}) collective-permute-start(f32[224,256]{1,0:T(8,128)} %get-tuple-element.21), channel_id=1, source_target_pairs={{0,16},{8,24},{16,0},{24,8},{32,48},{40,56},{48,32},{56,40},{64,80... | collective-permute-start | bytes 688136 | tf_op jit(solution)/shard_map/ppermute | solution.py:36
  50.9 4.6 %fusion.4 = f32[1536,256]{1,0:T(8,128)S(1)} fusion(f32[512,256]{1,0:T(8,128)S(1)} %copy-done.2, f32[512,1792]{1,0:T(8,128)} %param.7), kind=kOutput, calls=%fused_computation.4 | convolution fusion | flops 1207959552 | bytes 5242880 | tf_op jit(solution)/shard_map/dot_general | solution.py:14
  55.5 1.3 fusion.8
  58.4 1.6 %fusion.11 = f32[256,256]{1,0:T(8,128)S(1)} fusion(f32[512,256]{1,0:T(8,128)S(1)} %copy-done.2, f32[512,256]{1,0:T(8,128)S(1)} %get-tuple-element.9, f32[512,1792]{1,0:T(8,128)} %param.7, pred[]{:T(512)S(6)} %eq.64), kind=kOutput, calls=%fused_computation.22 | convolution fusion | flops 201588736 | bytes 1835009 | tf_op jit(solution)/shard_map/dot_general | solution.py:14
  62.9 2.4 %collective-permute-start.38 = (f32[224,256]{1,0:T(8,128)}, f32[224,256]{1,0:T(8,128)}, u32[]{:S(2)}, u32[]{:S(2)}) collective-permute-start(f32[224,256]{1,0:T(8,128)} %get-tuple-element.13), channel_id=1, source_target_pairs={{0,96},{8,104},{16,112},{24,120},{32,0},{40,8},{48,16},{56,24},{64... | collective-permute-start | bytes 688136 | tf_op jit(solution)/shard_map/ppermute | solution.py:32
  66.4 2.2 %collective-permute-start.20 = (f32[224,256]{1,0:T(8,128)}, f32[224,256]{1,0:T(8,128)S(1)}, u32[]{:S(2)}, u32[]{:S(2)}) collective-permute-start(f32[224,256]{1,0:T(8,128)} %get-tuple-element.22), channel_id=1, source_target_pairs={{0,24},{8,0},{16,8},{24,16},{32,56},{40,32},{48,40},{56,48},{64,88... | collective-permute-start | bytes 688136 | tf_op jit(solution)/shard_map/ppermute | solution.py:36
  68.7 3.6 %collective-permute-done.36 = f32[224,256]{1,0:T(8,128)S(1)} collective-permute-done((f32[224,256]{1,0:T(8,128)}, f32[224,256]{1,0:T(8,128)S(1)}, u32[]{:S(2)}, u32[]{:S(2)}) %collective-permute-start.36) | collective-permute-done | bytes 229408 | tf_op jit(solution)/shard_map/ppermute | solution.py:32
  72.3 3.1 %collective-permute-done.37 = f32[224,256]{1,0:T(8,128)} collective-permute-done((f32[224,256]{1,0:T(8,128)}, f32[224,256]{1,0:T(8,128)}, u32[]{:S(2)}, u32[]{:S(2)}) %collective-permute-start.37) | collective-permute-done | bytes 229408 | tf_op jit(solution)/shard_map/ppermute | solution.py:32
  76.4 2.2 %collective-permute-start.44 = (f32[224,256]{1,0:T(8,128)S(1)}, f32[224,256]{1,0:T(8,128)S(1)}, u32[]{:S(2)}, u32[]{:S(2)}) collective-permute-start(f32[224,256]{1,0:T(8,128)S(1)} %get-tuple-element.16), channel_id=1, source_target_pairs={{0,24},{8,0},{16,8},{24,16},{32,56},{40,32},{48,40},{56,48},{64,88... | collective-permute-start | bytes 688136 | tf_op jit(solution)/shard_map/ppermute | solution.py:36
  78.6 1.5 fusion.22
  81.9 1.7 %collective-permute-start.41 = (f32[56,256]{1,0:T(8,128)S(1)}, f32[56,256]{1,0:T(8,128)S(1)}, u32[]{:S(2)}, u32[]{:S(2)}) collective-permute-start(f32[56,256]{1,0:T(8,128)S(1)} %get-tuple-element.28), channel_id=1, source_target_pairs={{0,24},{8,0},{16,8},{24,16},{32,56},{40,32},{48,40},{56,48},{64,88... | collective-permute-start | bytes 172040 | tf_op jit(solution)/shard_map/ppermute | solution.py:36
  83.6 3.5 %collective-permute-done.43 = f32[224,256]{1,0:T(8,128)S(1)} collective-permute-done((f32[224,256]{1,0:T(8,128)S(1)}, f32[224,256]{1,0:T(8,128)S(1)}, u32[]{:S(2)}, u32[]{:S(2)}) %collective-permute-start.43) | collective-permute-done | bytes 229408 | tf_op jit(solution)/shard_map/ppermute | solution.py:36
  89.2 2.6 %collective-permute-start.47 = (f32[56,256]{1,0:T(8,128)S(1)}, f32[56,256]{1,0:T(8,128)S(1)}, u32[]{:S(2)}, u32[]{:S(2)}) collective-permute-start(f32[56,256]{1,0:T(8,128)S(1)} %get-tuple-element.31), channel_id=1, source_target_pairs={{0,96},{8,104},{16,112},{24,120},{32,0},{40,8},{48,16},{56,24},{64... | collective-permute-start | bytes 172040 | tf_op jit(solution)/shard_map/ppermute | solution.py:32
  92.0 3.2 %collective-permute-start.16 = (f32[56,256]{1,0:T(8,128)S(1)}, f32[56,256]{1,0:T(8,128)S(1)}, u32[]{:S(2)}, u32[]{:S(2)}) collective-permute-start(f32[56,256]{1,0:T(8,128)S(1)} %get-tuple-element.35), channel_id=1, source_target_pairs={{0,8},{8,16},{16,24},{24,0},{32,40},{40,48},{48,56},{56,32},{64,72... | collective-permute-start | bytes 172040 | tf_op jit(solution)/shard_map/ppermute | solution.py:36
  95.4 2.2 %collective-permute-start.21 = (f32[56,256]{1,0:T(8,128)S(1)}, f32[56,256]{1,0:T(8,128)S(1)}, u32[]{:S(2)}, u32[]{:S(2)}) collective-permute-start(f32[56,256]{1,0:T(8,128)S(1)} %get-tuple-element.36), channel_id=1, source_target_pairs={{0,64},{8,72},{16,80},{24,88},{32,96},{40,104},{48,112},{56,120},{... | collective-permute-start | bytes 172040 | tf_op jit(solution)/shard_map/ppermute | solution.py:32
  97.9 3.3 %collective-permute-start.23 = (f32[56,256]{1,0:T(8,128)S(1)}, f32[56,256]{1,0:T(8,128)S(1)}, u32[]{:S(2)}, u32[]{:S(2)}) collective-permute-start(f32[56,256]{1,0:T(8,128)S(1)} %get-tuple-element.37), channel_id=1, source_target_pairs={{0,96},{8,104},{16,112},{24,120},{32,0},{40,8},{48,16},{56,24},{64... | collective-permute-start | bytes 172040 | tf_op jit(solution)/shard_map/ppermute | solution.py:32
  101.3 2.1 %collective-permute-start.48 = (f32[56,256]{1,0:T(8,128)S(1)}, f32[56,256]{1,0:T(8,128)S(1)}, u32[]{:S(2)}, u32[]{:S(2)}) collective-permute-start(f32[56,256]{1,0:T(8,128)S(1)} %get-tuple-element.39), channel_id=1, source_target_pairs={{0,16},{8,24},{16,0},{24,8},{32,48},{40,56},{48,32},{56,40},{64,80... | collective-permute-start | bytes 172040 | tf_op jit(solution)/shard_map/ppermute | solution.py:36
  103.4 3.3 %collective-permute-start.50 = (f32[56,256]{1,0:T(8,128)S(1)}, f32[56,256]{1,0:T(8,128)S(1)}, u32[]{:S(2)}, u32[]{:S(2)}) collective-permute-start(f32[56,256]{1,0:T(8,128)S(1)} %get-tuple-element.39), channel_id=1, source_target_pairs={{0,24},{8,0},{16,8},{24,16},{32,56},{40,32},{48,40},{56,48},{64,88... | collective-permute-start | bytes 172040 | tf_op jit(solution)/shard_map/ppermute | solution.py:36
  109.1 5.1 %collective-permute-done.24 = f32[56,256]{1,0:T(8,128)S(1)} collective-permute-done((f32[56,256]{1,0:T(8,128)S(1)}, f32[56,256]{1,0:T(8,128)S(1)}, u32[]{:S(2)}, u32[]{:S(2)}) %collective-permute-start.24) | collective-permute-done | bytes 57376 | tf_op jit(solution)/shard_map/ppermute | solution.py:36
  114.2 2.0 %collective-permute-start.56 = (f32[56,256]{1,0:T(8,128)S(1)}, f32[56,256]{1,0:T(8,128)S(1)}, u32[]{:S(2)}, u32[]{:S(2)}) collective-permute-start(f32[56,256]{1,0:T(8,128)S(1)} %get-tuple-element.40), channel_id=1, source_target_pairs={{0,96},{8,104},{16,112},{24,120},{32,0},{40,8},{48,16},{56,24},{64... | collective-permute-start | bytes 172040 | tf_op jit(solution)/shard_map/ppermute | solution.py:32
  116.3 5.4 %collective-permute-done.25 = f32[56,256]{1,0:T(8,128)S(1)} collective-permute-done((f32[56,256]{1,0:T(8,128)S(1)}, f32[56,256]{1,0:T(8,128)S(1)}, u32[]{:S(2)}, u32[]{:S(2)}) %collective-permute-start.25) | collective-permute-done | bytes 57376 | tf_op jit(solution)/shard_map/ppermute | solution.py:36
  121.8 2.2 %collective-permute-start.30 = (f32[56,256]{1,0:T(8,128)S(1)}, f32[56,256]{1,0:T(8,128)S(1)}, u32[]{:S(2)}, u32[]{:S(2)}) collective-permute-start(f32[56,256]{1,0:T(8,128)S(1)} %get-tuple-element.42), channel_id=1, source_target_pairs={{0,64},{8,72},{16,80},{24,88},{32,96},{40,104},{48,112},{56,120},{... | collective-permute-start | bytes 172040 | tf_op jit(solution)/shard_map/ppermute | solution.py:32
  124.0 1.8 %collective-permute-done.26 = f32[56,256]{1,0:T(8,128)S(1)} collective-permute-done((f32[56,256]{1,0:T(8,128)S(1)}, f32[56,256]{1,0:T(8,128)S(1)}, u32[]{:S(2)}, u32[]{:S(2)}) %collective-permute-start.26) | collective-permute-done | bytes 57376 | tf_op jit(solution)/shard_map/ppermute | solution.py:36
  126.0 3.1 %collective-permute-start.32 = (f32[56,256]{1,0:T(8,128)S(1)}, f32[56,256]{1,0:T(8,128)S(1)}, u32[]{:S(2)}, u32[]{:S(2)}) collective-permute-start(f32[56,256]{1,0:T(8,128)S(1)} %get-tuple-element.42), channel_id=1, source_target_pairs={{0,96},{8,104},{16,112},{24,120},{32,0},{40,8},{48,16},{56,24},{64... | collective-permute-start | bytes 172040 | tf_op jit(solution)/shard_map/ppermute | solution.py:32
  130.4 3.3 %collective-permute-start.53 = (f32[224,256]{1,0:T(8,128)S(1)}, f32[224,256]{1,0:T(8,128)S(1)}, u32[]{:S(2)}, u32[]{:S(2)}) collective-permute-start(f32[224,256]{1,0:T(8,128)S(1)} %bitcast.261), channel_id=1, source_target_pairs={{0,96},{8,104},{16,112},{24,120},{32,0},{40,8},{48,16},{56,24},{64... | collective-permute-start | bytes 688136 | tf_op jit(solution)/shard_map/ppermute | solution.py:32
  136.3 2.9 %collective-permute-done.51 = f32[224,256]{1,0:T(8,128)S(1)} collective-permute-done((f32[224,256]{1,0:T(8,128)S(1)}, f32[224,256]{1,0:T(8,128)S(1)}, u32[]{:S(2)}, u32[]{:S(2)}) %collective-permute-start.51) | collective-permute-done | bytes 229408 | tf_op jit(solution)/shard_map/ppermute | solution.py:32
  139.2 1.3 collective-permute-start.59
  140.6 2.7 %collective-permute-done.52 = f32[224,256]{1,0:T(8,128)S(1)} collective-permute-done((f32[224,256]{1,0:T(8,128)S(1)}, f32[224,256]{1,0:T(8,128)S(1)}, u32[]{:S(2)}, u32[]{:S(2)}) %collective-permute-start.52) | collective-permute-done | bytes 229408 | tf_op jit(solution)/shard_map/ppermute | solution.py:32
  144.9 2.3 %collective-permute-start.29 = (f32[224,256]{1,0:T(8,128)S(1)}, f32[224,256]{1,0:T(8,128)S(1)}, u32[]{:S(2)}, u32[]{:S(2)}) collective-permute-start(f32[224,256]{1,0:T(8,128)S(1)} %bitcast.266), channel_id=1, source_target_pairs={{0,96},{8,104},{16,112},{24,120},{32,0},{40,8},{48,16},{56,24},{64... | collective-permute-start | bytes 688136 | tf_op jit(solution)/shard_map/ppermute | solution.py:32
  147.2 1.6 collective-permute-start.33
  149.8 1.4 pad_maximum_fusion.1
  151.2 2.3 %collective-permute-start.35 = (f32[224,256]{1,0:T(8,128)S(1)}, f32[224,256]{1,0:T(8,128)S(1)}, u32[]{:S(2)}, u32[]{:S(2)}) collective-permute-start(f32[224,256]{1,0:T(8,128)S(1)} %bitcast.258), channel_id=1, source_target_pairs={{0,24},{8,0},{16,8},{24,16},{32,56},{40,32},{48,40},{56,48},{64,88... | collective-permute-start | bytes 688136 | tf_op jit(solution)/shard_map/ppermute | solution.py:36
  153.6 1.3 collective-permute-done.33
  155.0 2.3 %collective-permute-done.34 = f32[224,256]{1,0:T(8,128)S(1)} collective-permute-done((f32[224,256]{1,0:T(8,128)S(1)}, f32[224,256]{1,0:T(8,128)S(1)}, u32[]{:S(2)}, u32[]{:S(2)}) %collective-permute-start.34) | collective-permute-done | bytes 229408 | tf_op jit(solution)/shard_map/ppermute | solution.py:36
  157.4 1.3 pad_maximum_fusion
  (171 shorter events, 29.5 us)
Async XLA Ops:
  7.0 9.1 %collective-permute-start = (f32[256,512]{1,0:T(8,128)S(1)}, f32[256,512]{1,0:T(8,128)S(1)}, u32[]{:S(2)}, u32[]{:S(2)}) collective-permute-start(f32[256,512]{1,0:T(8,128)S(1)} %dynamic-slice_bitcast_fusion), channel_id=1, source_target_pairs={{0,1},{1,0},{2,3},{3,2},{4,5},{5,4},{6,7},{7,6},{8,9},{9,8},{10,11... | collective-permute-start | bytes 1572872 | tf_op jit(solution)/shard_map/ppermute | solution.py:45
  8.7 11.2 %collective-permute-start.4 = (f32[256,256]{1,0:T(8,128)}, f32[256,256]{1,0:T(8,128)S(1)}, u32[]{:S(2)}, u32[]{:S(2)}) collective-permute-start(f32[256,256]{1,0:T(8,128)} %slice.47), channel_id=1, source_target_pairs={{7,1},{15,9},{23,17},{31,25},{39,33},{47,41},{55,49},{63,57},{71,6... | collective-permute-start | bytes 786440 | tf_op jit(solution)/shard_map/ppermute | solution.py:114
  9.4 13.2 %collective-permute-start.5 = (f32[256,256]{1,0:T(8,128)}, f32[256,256]{1,0:T(8,128)S(1)}, u32[]{:S(2)}, u32[]{:S(2)}) collective-permute-start(f32[256,256]{1,0:T(8,128)} %slice.47), channel_id=1, source_target_pairs={{7,5},{15,13},{23,21},{31,29},{39,37},{47,45},{55,53},{63,61},{71,... | collective-permute-start | bytes 786440 | tf_op jit(solution)/shard_map/ppermute | solution.py:114
  10.1 12.5 %collective-permute-start.6 = (f32[256,256]{1,0:T(8,128)}, f32[256,256]{1,0:T(8,128)S(1)}, u32[]{:S(2)}, u32[]{:S(2)}) collective-permute-start(f32[256,256]{1,0:T(8,128)} %slice.47), channel_id=1, source_target_pairs={{7,3},{15,11},{23,19},{31,27},{39,35},{47,43},{55,51},{63,59},{71,... | collective-permute-start | bytes 786440 | tf_op jit(solution)/shard_map/ppermute | solution.py:114
  16.2 8.8 %collective-permute-start.1 = (f32[64,512]{1,0:T(8,128)S(1)}, f32[64,512]{1,0:T(8,128)S(1)}, u32[]{:S(2)}, u32[]{:S(2)}) collective-permute-start(f32[64,512]{1,0:T(8,128)S(1)} %get-tuple-element.24), channel_id=1, source_target_pairs={{0,4},{1,5},{2,6},{3,7},{4,0},{5,1},{6,2},{7,3},{8,12},{9,13},{10,... | collective-permute-start | bytes 393224 | tf_op jit(solution)/shard_map/ppermute | solution.py:41
  19.4 7.6 %collective-permute-start.2 = (f32[64,512]{1,0:T(8,128)S(1)}, f32[64,512]{1,0:T(8,128)S(1)}, u32[]{:S(2)}, u32[]{:S(2)}) collective-permute-start(f32[64,512]{1,0:T(8,128)S(1)} %get-tuple-element.26), channel_id=1, source_target_pairs={{0,2},{1,3},{2,4},{3,5},{4,6},{5,7},{6,0},{7,1},{8,10},{9,11},{10,... | collective-permute-start | bytes 393224 | tf_op jit(solution)/shard_map/ppermute | solution.py:41
  27.9 8.0 %collective-permute-start.8 = (f32[64,512]{1,0:T(8,128)S(1)}, f32[64,512]{1,0:T(8,128)}, u32[]{:S(2)}, u32[]{:S(2)}) collective-permute-start(f32[64,512]{1,0:T(8,128)S(1)} %pad_maximum_fusion.4), channel_id=1, source_target_pairs={{0,4},{1,5},{2,6},{3,7},{4,0},{5,1},{6,2},{7,3},{8,12},{9,13},{10,... | collective-permute-start | bytes 393224 | tf_op jit(solution)/shard_map/ppermute | solution.py:41
  29.5 8.6 %collective-permute-start.9 = (f32[64,512]{1,0:T(8,128)S(1)}, f32[64,512]{1,0:T(8,128)S(1)}, u32[]{:S(2)}, u32[]{:S(2)}) collective-permute-start(f32[64,512]{1,0:T(8,128)S(1)} %pad_maximum_fusion.4), channel_id=1, source_target_pairs={{0,2},{1,3},{2,4},{3,5},{4,6},{5,7},{6,0},{7,1},{8,10},{9,11},{10,... | collective-permute-start | bytes 393224 | tf_op jit(solution)/shard_map/ppermute | solution.py:41
  38.6 16.8 %collective-permute-start.11 = (f32[256,512]{1,0:T(8,128)S(1)}, f32[256,512]{1,0:T(8,128)}, u32[]{:S(2)}, u32[]{:S(2)}) collective-permute-start(f32[256,512]{1,0:T(8,128)S(1)} %bitcast.241), channel_id=1, source_target_pairs={{0,1},{1,0},{2,3},{3,2},{4,5},{5,4},{6,7},{7,6},{8,9},{9,8},{10,11... | collective-permute-start | bytes 1572872 | tf_op jit(solution)/shard_map/ppermute | solution.py:45
  39.6 22.4 %collective-permute-start.12 = (f32[224,256]{1,0:T(8,128)}, f32[224,256]{1,0:T(8,128)}, u32[]{:S(2)}, u32[]{:S(2)}) collective-permute-start(f32[224,256]{1,0:T(8,128)} %get-tuple-element.18), channel_id=1, source_target_pairs={{0,64},{8,72},{16,80},{24,88},{32,96},{40,104},{48,112},{56,120},{... | collective-permute-start | bytes 688136 | tf_op jit(solution)/shard_map/ppermute | solution.py:32
  42.9 20.0 %collective-permute-start.13 = (f32[224,256]{1,0:T(8,128)}, f32[224,256]{1,0:T(8,128)}, u32[]{:S(2)}, u32[]{:S(2)}) collective-permute-start(f32[224,256]{1,0:T(8,128)} %get-tuple-element.20), channel_id=1, source_target_pairs={{0,32},{8,40},{16,48},{24,56},{32,64},{40,72},{48,80},{56,88},{64,... | collective-permute-start | bytes 688136 | tf_op jit(solution)/shard_map/ppermute | solution.py:32
  43.5 21.8 %collective-permute-start.14 = (f32[224,256]{1,0:T(8,128)}, f32[224,256]{1,0:T(8,128)}, u32[]{:S(2)}, u32[]{:S(2)}) collective-permute-start(f32[224,256]{1,0:T(8,128)} %get-tuple-element.19), channel_id=1, source_target_pairs={{0,96},{8,104},{16,112},{24,120},{32,0},{40,8},{48,16},{56,24},{64... | collective-permute-start | bytes 688136 | tf_op jit(solution)/shard_map/ppermute | solution.py:32
  47.0 19.5 %collective-permute-start.18 = (f32[224,256]{1,0:T(8,128)}, f32[224,256]{1,0:T(8,128)}, u32[]{:S(2)}, u32[]{:S(2)}) collective-permute-start(f32[224,256]{1,0:T(8,128)} %get-tuple-element.21), channel_id=1, source_target_pairs={{0,16},{8,24},{16,0},{24,8},{32,48},{40,56},{48,32},{56,40},{64,80... | collective-permute-start | bytes 688136 | tf_op jit(solution)/shard_map/ppermute | solution.py:36
  62.0 10.3 %collective-permute-start.36 = (f32[224,256]{1,0:T(8,128)}, f32[224,256]{1,0:T(8,128)S(1)}, u32[]{:S(2)}, u32[]{:S(2)}) collective-permute-start(f32[224,256]{1,0:T(8,128)} %get-tuple-element.12), channel_id=1, source_target_pairs={{0,64},{8,72},{16,80},{24,88},{32,96},{40,104},{48,112},{56,120},{... | collective-permute-start | bytes 688136 | tf_op jit(solution)/shard_map/ppermute | solution.py:32
  62.0 13.3 %collective-permute-start.37 = (f32[224,256]{1,0:T(8,128)}, f32[224,256]{1,0:T(8,128)}, u32[]{:S(2)}, u32[]{:S(2)}) collective-permute-start(f32[224,256]{1,0:T(8,128)} %get-tuple-element.14), channel_id=1, source_target_pairs={{0,32},{8,40},{16,48},{24,56},{32,64},{40,72},{48,80},{56,88},{64,... | collective-permute-start | bytes 688136 | tf_op jit(solution)/shard_map/ppermute | solution.py:32
  62.9 13.5 %collective-permute-start.38 = (f32[224,256]{1,0:T(8,128)}, f32[224,256]{1,0:T(8,128)}, u32[]{:S(2)}, u32[]{:S(2)}) collective-permute-start(f32[224,256]{1,0:T(8,128)} %get-tuple-element.13), channel_id=1, source_target_pairs={{0,96},{8,104},{16,112},{24,120},{32,0},{40,8},{48,16},{56,24},{64... | collective-permute-start | bytes 688136 | tf_op jit(solution)/shard_map/ppermute | solution.py:32
  65.4 14.8 %collective-permute-start.19 = (f32[224,256]{1,0:T(8,128)}, f32[224,256]{1,0:T(8,128)S(1)}, u32[]{:S(2)}, u32[]{:S(2)}) collective-permute-start(f32[224,256]{1,0:T(8,128)} %get-tuple-element.23), channel_id=1, source_target_pairs={{0,8},{8,16},{16,24},{24,0},{32,40},{40,48},{48,56},{56,32},{64,72... | collective-permute-start | bytes 688136 | tf_op jit(solution)/shard_map/ppermute | solution.py:36
  66.4 13.8 %collective-permute-start.20 = (f32[224,256]{1,0:T(8,128)}, f32[224,256]{1,0:T(8,128)S(1)}, u32[]{:S(2)}, u32[]{:S(2)}) collective-permute-start(f32[224,256]{1,0:T(8,128)} %get-tuple-element.22), channel_id=1, source_target_pairs={{0,24},{8,0},{16,8},{24,16},{32,56},{40,32},{48,40},{56,48},{64,88... | collective-permute-start | bytes 688136 | tf_op jit(solution)/shard_map/ppermute | solution.py:36
  72.3 9.6 %collective-permute-start.42 = (f32[224,256]{1,0:T(8,128)S(1)}, f32[224,256]{1,0:T(8,128)S(1)}, u32[]{:S(2)}, u32[]{:S(2)}) collective-permute-start(f32[224,256]{1,0:T(8,128)S(1)} %get-tuple-element.15), channel_id=1, source_target_pairs={{0,16},{8,24},{16,0},{24,8},{32,48},{40,56},{48,32},{56,40},{64,80... | collective-permute-start | bytes 688136 | tf_op jit(solution)/shard_map/ppermute | solution.py:36
  75.4 11.8 %collective-permute-start.43 = (f32[224,256]{1,0:T(8,128)S(1)}, f32[224,256]{1,0:T(8,128)S(1)}, u32[]{:S(2)}, u32[]{:S(2)}) collective-permute-start(f32[224,256]{1,0:T(8,128)S(1)} %get-tuple-element.17), channel_id=1, source_target_pairs={{0,8},{8,16},{16,24},{24,0},{32,40},{40,48},{48,56},{56,32},{64,72... | collective-permute-start | bytes 688136 | tf_op jit(solution)/shard_map/ppermute | solution.py:36
  76.4 10.7 %collective-permute-start.44 = (f32[224,256]{1,0:T(8,128)S(1)}, f32[224,256]{1,0:T(8,128)S(1)}, u32[]{:S(2)}, u32[]{:S(2)}) collective-permute-start(f32[224,256]{1,0:T(8,128)S(1)} %get-tuple-element.16), channel_id=1, source_target_pairs={{0,24},{8,0},{16,8},{24,16},{32,56},{40,32},{48,40},{56,48},{64,88... | collective-permute-start | bytes 688136 | tf_op jit(solution)/shard_map/ppermute | solution.py:36
  80.2 9.0 %collective-permute-start.39 = (f32[56,256]{1,0:T(8,128)S(1)}, f32[56,256]{1,0:T(8,128)S(1)}, u32[]{:S(2)}, u32[]{:S(2)}) collective-permute-start(f32[56,256]{1,0:T(8,128)S(1)} %get-tuple-element.27), channel_id=1, source_target_pairs={{0,16},{8,24},{16,0},{24,8},{32,48},{40,56},{48,32},{56,40},{64,80... | collective-permute-start | bytes 172040 | tf_op jit(solution)/shard_map/ppermute | solution.py:36
  80.3 11.5 %collective-permute-start.40 = (f32[56,256]{1,0:T(8,128)S(1)}, f32[56,256]{1,0:T(8,128)S(1)}, u32[]{:S(2)}, u32[]{:S(2)}) collective-permute-start(f32[56,256]{1,0:T(8,128)S(1)} %get-tuple-element.29), channel_id=1, source_target_pairs={{0,8},{8,16},{16,24},{24,0},{32,40},{40,48},{48,56},{56,32},{64,72... | collective-permute-start | bytes 172040 | tf_op jit(solution)/shard_map/ppermute | solution.py:36
  81.9 10.1 %collective-permute-start.41 = (f32[56,256]{1,0:T(8,128)S(1)}, f32[56,256]{1,0:T(8,128)S(1)}, u32[]{:S(2)}, u32[]{:S(2)}) collective-permute-start(f32[56,256]{1,0:T(8,128)S(1)} %get-tuple-element.28), channel_id=1, source_target_pairs={{0,24},{8,0},{16,8},{24,16},{32,56},{40,32},{48,40},{56,48},{64,88... | collective-permute-start | bytes 172040 | tf_op jit(solution)/shard_map/ppermute | solution.py:36
  89.2 8.4 %collective-permute-start.47 = (f32[56,256]{1,0:T(8,128)S(1)}, f32[56,256]{1,0:T(8,128)S(1)}, u32[]{:S(2)}, u32[]{:S(2)}) collective-permute-start(f32[56,256]{1,0:T(8,128)S(1)} %get-tuple-element.31), channel_id=1, source_target_pairs={{0,96},{8,104},{16,112},{24,120},{32,0},{40,8},{48,16},{56,24},{64... | collective-permute-start | bytes 172040 | tf_op jit(solution)/shard_map/ppermute | solution.py:32
  92.0 9.2 %collective-permute-start.16 = (f32[56,256]{1,0:T(8,128)S(1)}, f32[56,256]{1,0:T(8,128)S(1)}, u32[]{:S(2)}, u32[]{:S(2)}) collective-permute-start(f32[56,256]{1,0:T(8,128)S(1)} %get-tuple-element.35), channel_id=1, source_target_pairs={{0,8},{8,16},{16,24},{24,0},{32,40},{40,48},{48,56},{56,32},{64,72... | collective-permute-start | bytes 172040 | tf_op jit(solution)/shard_map/ppermute | solution.py:36
  95.2 8.1 %collective-permute-start.17 = (f32[56,256]{1,0:T(8,128)S(1)}, f32[56,256]{1,0:T(8,128)S(1)}, u32[]{:S(2)}, u32[]{:S(2)}) collective-permute-start(f32[56,256]{1,0:T(8,128)S(1)} %get-tuple-element.34), channel_id=1, source_target_pairs={{0,24},{8,0},{16,8},{24,16},{32,56},{40,32},{48,40},{56,48},{64,88... | collective-permute-start | bytes 172040 | tf_op jit(solution)/shard_map/ppermute | solution.py:36
  95.4 8.0 %collective-permute-start.21 = (f32[56,256]{1,0:T(8,128)S(1)}, f32[56,256]{1,0:T(8,128)S(1)}, u32[]{:S(2)}, u32[]{:S(2)}) collective-permute-start(f32[56,256]{1,0:T(8,128)S(1)} %get-tuple-element.36), channel_id=1, source_target_pairs={{0,64},{8,72},{16,80},{24,88},{32,96},{40,104},{48,112},{56,120},{... | collective-permute-start | bytes 172040 | tf_op jit(solution)/shard_map/ppermute | solution.py:32
  97.6 9.1 %collective-permute-start.22 = (f32[56,256]{1,0:T(8,128)S(1)}, f32[56,256]{1,0:T(8,128)S(1)}, u32[]{:S(2)}, u32[]{:S(2)}) collective-permute-start(f32[56,256]{1,0:T(8,128)S(1)} %get-tuple-element.38), channel_id=1, source_target_pairs={{0,32},{8,40},{16,48},{24,56},{32,64},{40,72},{48,80},{56,88},{64,... | collective-permute-start | bytes 172040 | tf_op jit(solution)/shard_map/ppermute | solution.py:32
  97.9 8.8 %collective-permute-start.23 = (f32[56,256]{1,0:T(8,128)S(1)}, f32[56,256]{1,0:T(8,128)S(1)}, u32[]{:S(2)}, u32[]{:S(2)}) collective-permute-start(f32[56,256]{1,0:T(8,128)S(1)} %get-tuple-element.37), channel_id=1, source_target_pairs={{0,96},{8,104},{16,112},{24,120},{32,0},{40,8},{48,16},{56,24},{64... | collective-permute-start | bytes 172040 | tf_op jit(solution)/shard_map/ppermute | solution.py:32
  103.3 12.9 %collective-permute-start.49 = (f32[56,256]{1,0:T(8,128)S(1)}, f32[56,256]{1,0:T(8,128)S(1)}, u32[]{:S(2)}, u32[]{:S(2)}) collective-permute-start(f32[56,256]{1,0:T(8,128)S(1)} %get-tuple-element.39), channel_id=1, source_target_pairs={{0,8},{8,16},{16,24},{24,0},{32,40},{40,48},{48,56},{56,32},{64,72... | collective-permute-start | bytes 172040 | tf_op jit(solution)/shard_map/ppermute | solution.py:36
  103.4 18.4 %collective-permute-start.50 = (f32[56,256]{1,0:T(8,128)S(1)}, f32[56,256]{1,0:T(8,128)S(1)}, u32[]{:S(2)}, u32[]{:S(2)}) collective-permute-start(f32[56,256]{1,0:T(8,128)S(1)} %get-tuple-element.39), channel_id=1, source_target_pairs={{0,24},{8,0},{16,8},{24,16},{32,56},{40,32},{48,40},{56,48},{64,88... | collective-permute-start | bytes 172040 | tf_op jit(solution)/shard_map/ppermute | solution.py:36
  106.7 19.3 %collective-permute-start.54 = (f32[56,256]{1,0:T(8,128)S(1)}, f32[56,256]{1,0:T(8,128)S(1)}, u32[]{:S(2)}, u32[]{:S(2)}) collective-permute-start(f32[56,256]{1,0:T(8,128)S(1)} %get-tuple-element.40), channel_id=1, source_target_pairs={{0,64},{8,72},{16,80},{24,88},{32,96},{40,104},{48,112},{56,120},{... | collective-permute-start | bytes 172040 | tf_op jit(solution)/shard_map/ppermute | solution.py:32
  106.8 23.5 %collective-permute-start.55 = (f32[56,256]{1,0:T(8,128)S(1)}, f32[56,256]{1,0:T(8,128)S(1)}, u32[]{:S(2)}, u32[]{:S(2)}) collective-permute-start(f32[56,256]{1,0:T(8,128)S(1)} %get-tuple-element.40), channel_id=1, source_target_pairs={{0,32},{8,40},{16,48},{24,56},{32,64},{40,72},{48,80},{56,88},{64,... | collective-permute-start | bytes 172040 | tf_op jit(solution)/shard_map/ppermute | solution.py:32
  114.2 16.2 %collective-permute-start.56 = (f32[56,256]{1,0:T(8,128)S(1)}, f32[56,256]{1,0:T(8,128)S(1)}, u32[]{:S(2)}, u32[]{:S(2)}) collective-permute-start(f32[56,256]{1,0:T(8,128)S(1)} %get-tuple-element.40), channel_id=1, source_target_pairs={{0,96},{8,104},{16,112},{24,120},{32,0},{40,8},{48,16},{56,24},{64... | collective-permute-start | bytes 172040 | tf_op jit(solution)/shard_map/ppermute | solution.py:32
  125.8 8.0 %collective-permute-start.31 = (f32[56,256]{1,0:T(8,128)S(1)}, f32[56,256]{1,0:T(8,128)S(1)}, u32[]{:S(2)}, u32[]{:S(2)}) collective-permute-start(f32[56,256]{1,0:T(8,128)S(1)} %get-tuple-element.42), channel_id=1, source_target_pairs={{0,32},{8,40},{16,48},{24,56},{32,64},{40,72},{48,80},{56,88},{64,... | collective-permute-start | bytes 172040 | tf_op jit(solution)/shard_map/ppermute | solution.py:32
  126.0 8.9 %collective-permute-start.32 = (f32[56,256]{1,0:T(8,128)S(1)}, f32[56,256]{1,0:T(8,128)S(1)}, u32[]{:S(2)}, u32[]{:S(2)}) collective-permute-start(f32[56,256]{1,0:T(8,128)S(1)} %get-tuple-element.42), channel_id=1, source_target_pairs={{0,96},{8,104},{16,112},{24,120},{32,0},{40,8},{48,16},{56,24},{64... | collective-permute-start | bytes 172040 | tf_op jit(solution)/shard_map/ppermute | solution.py:32
  129.2 10.1 %collective-permute-start.51 = (f32[224,256]{1,0:T(8,128)S(1)}, f32[224,256]{1,0:T(8,128)S(1)}, u32[]{:S(2)}, u32[]{:S(2)}) collective-permute-start(f32[224,256]{1,0:T(8,128)S(1)} %bitcast.259), channel_id=1, source_target_pairs={{0,64},{8,72},{16,80},{24,88},{32,96},{40,104},{48,112},{56,120},{... | collective-permute-start | bytes 688136 | tf_op jit(solution)/shard_map/ppermute | solution.py:32
  130.3 13.0 %collective-permute-start.52 = (f32[224,256]{1,0:T(8,128)S(1)}, f32[224,256]{1,0:T(8,128)S(1)}, u32[]{:S(2)}, u32[]{:S(2)}) collective-permute-start(f32[224,256]{1,0:T(8,128)S(1)} %bitcast.260), channel_id=1, source_target_pairs={{0,32},{8,40},{16,48},{24,56},{32,64},{40,72},{48,80},{56,88},{64,... | collective-permute-start | bytes 688136 | tf_op jit(solution)/shard_map/ppermute | solution.py:32
  130.4 13.4 %collective-permute-start.53 = (f32[224,256]{1,0:T(8,128)S(1)}, f32[224,256]{1,0:T(8,128)S(1)}, u32[]{:S(2)}, u32[]{:S(2)}) collective-permute-start(f32[224,256]{1,0:T(8,128)S(1)} %bitcast.261), channel_id=1, source_target_pairs={{0,96},{8,104},{16,112},{24,120},{32,0},{40,8},{48,16},{56,24},{64... | collective-permute-start | bytes 688136 | tf_op jit(solution)/shard_map/ppermute | solution.py:32
  133.8 11.1 %collective-permute-start.57 = (f32[224,256]{1,0:T(8,128)S(1)}, f32[224,256]{1,0:T(8,128)S(1)}, u32[]{:S(2)}, u32[]{:S(2)}) collective-permute-start(f32[224,256]{1,0:T(8,128)S(1)} %bitcast.251), channel_id=1, source_target_pairs={{0,16},{8,24},{16,0},{24,8},{32,48},{40,56},{48,32},{56,40},{64,80... | collective-permute-start | bytes 688136 | tf_op jit(solution)/shard_map/ppermute | solution.py:36
  134.9 12.3 %collective-permute-start.58 = (f32[224,256]{1,0:T(8,128)S(1)}, f32[224,256]{1,0:T(8,128)S(1)}, u32[]{:S(2)}, u32[]{:S(2)}) collective-permute-start(f32[224,256]{1,0:T(8,128)S(1)} %bitcast.253), channel_id=1, source_target_pairs={{0,8},{8,16},{16,24},{24,0},{32,40},{40,48},{48,56},{56,32},{64,72... | collective-permute-start | bytes 688136 | tf_op jit(solution)/shard_map/ppermute | solution.py:36
  139.2 9.6 %collective-permute-start.59 = (f32[224,256]{1,0:T(8,128)S(1)}, f32[224,256]{1,0:T(8,128)S(1)}, u32[]{:S(2)}, u32[]{:S(2)}) collective-permute-start(f32[224,256]{1,0:T(8,128)S(1)} %bitcast.254), channel_id=1, source_target_pairs={{0,24},{8,0},{16,8},{24,16},{32,56},{40,32},{48,40},{56,48},{64,88... | collective-permute-start | bytes 688136 | tf_op jit(solution)/shard_map/ppermute | solution.py:36
  143.3 7.9 %collective-permute-start.27 = (f32[224,256]{1,0:T(8,128)S(1)}, f32[224,256]{1,0:T(8,128)S(1)}, u32[]{:S(2)}, u32[]{:S(2)}) collective-permute-start(f32[224,256]{1,0:T(8,128)S(1)} %bitcast.264), channel_id=1, source_target_pairs={{0,64},{8,72},{16,80},{24,88},{32,96},{40,104},{48,112},{56,120},{... | collective-permute-start | bytes 688136 | tf_op jit(solution)/shard_map/ppermute | solution.py:32
  143.8 9.8 %collective-permute-start.28 = (f32[224,256]{1,0:T(8,128)S(1)}, f32[224,256]{1,0:T(8,128)S(1)}, u32[]{:S(2)}, u32[]{:S(2)}) collective-permute-start(f32[224,256]{1,0:T(8,128)S(1)} %bitcast.265), channel_id=1, source_target_pairs={{0,32},{8,40},{16,48},{24,56},{32,64},{40,72},{48,80},{56,88},{64,... | collective-permute-start | bytes 688136 | tf_op jit(solution)/shard_map/ppermute | solution.py:32
  144.9 8.7 %collective-permute-start.29 = (f32[224,256]{1,0:T(8,128)S(1)}, f32[224,256]{1,0:T(8,128)S(1)}, u32[]{:S(2)}, u32[]{:S(2)}) collective-permute-start(f32[224,256]{1,0:T(8,128)S(1)} %bitcast.266), channel_id=1, source_target_pairs={{0,96},{8,104},{16,112},{24,120},{32,0},{40,8},{48,16},{56,24},{64... | collective-permute-start | bytes 688136 | tf_op jit(solution)/shard_map/ppermute | solution.py:32
  147.2 7.7 %collective-permute-start.33 = (f32[224,256]{1,0:T(8,128)S(1)}, f32[224,256]{1,0:T(8,128)S(1)}, u32[]{:S(2)}, u32[]{:S(2)}) collective-permute-start(f32[224,256]{1,0:T(8,128)S(1)} %bitcast.256), channel_id=1, source_target_pairs={{0,16},{8,24},{16,0},{24,8},{32,48},{40,56},{48,32},{56,40},{64,80... | collective-permute-start | bytes 688136 | tf_op jit(solution)/shard_map/ppermute | solution.py:36
  148.8 8.5 %collective-permute-start.34 = (f32[224,256]{1,0:T(8,128)S(1)}, f32[224,256]{1,0:T(8,128)S(1)}, u32[]{:S(2)}, u32[]{:S(2)}) collective-permute-start(f32[224,256]{1,0:T(8,128)S(1)} %bitcast.257), channel_id=1, source_target_pairs={{0,8},{8,16},{16,24},{24,0},{32,40},{40,48},{48,56},{56,32},{64,72... | collective-permute-start | bytes 688136 | tf_op jit(solution)/shard_map/ppermute | solution.py:36
  (20 other events, 160.9 us)

commit v2 on v0

v2 whole, which is shorter than its diff:
```python
import jax
import jax.numpy as jnp
from jax import lax
from jax.sharding import PartitionSpec as P

SIDE = 4


def matmul(left, right):
    return jnp.dot(left, right, precision=lax.Precision.HIGH, preferred_element_type=jnp.float32)


def tmatmul(left, right):
    return lax.dot_general(
        left,
        right,
        (((0,), (0,)), ((), ())),
        precision=lax.Precision.HIGH,
        preferred_element_type=jnp.float32,
    )


def row_pairs(dy, dz):
    return [
        (y * SIDE + z, ((y + dy) % SIDE) * SIDE + (z + dz) % SIDE)
        for y in range(SIDE)
        for z in range(SIDE)
    ]


def shift_y(value, step):
    return lax.ppermute(value, "row", row_pairs(step, 0))


def shift_z(value, step):
    return lax.ppermute(value, "row", row_pairs(0, step))


def block(value, index):
    return lax.dynamic_index_in_dim(value, index, 0, keepdims=False)


STEPS = (2, 1, 3)


def scatter_stage(parts):
    got = [[] for _ in parts]
    for step in STEPS:
        for i, (blocks, place, shift) in enumerate(parts):
            got[i].append(shift(block(blocks, (place + step) % SIDE), step))
    return [
        block(blocks, place) + got[i][0] + got[i][1] + got[i][2]
        for i, (blocks, place, _) in enumerate(parts)
    ]


def sum_stage(parts):
    got = [[] for _ in parts]
    for step in STEPS:
        for i, (own, shift) in enumerate(parts):
            got[i].append(shift(own, step))
    return [own + got[i][0] + got[i][1] + got[i][2] for i, (own, _) in enumerate(parts)]


def local(
    grad_window, rows_first, cols_first, rows_second, cols_second, inverse_first, inverse_second
):
    row = lax.axis_index("row")
    col = lax.axis_index("col")
    y, z = row // SIDE, row % SIDE
    core = col % 2
    last = 2 * SIDE - 1
    is_last = col == last
    tile_rows, tile_cols = grad_window.shape
    width = inverse_first.shape[0]

    left = matmul(grad_window, jnp.concatenate([cols_second, cols_first], 1))
    tail = jnp.where(is_last, cols_first[tile_cols - width :], 0.0)
    load = jnp.concatenate(
        [left, jnp.concatenate([tail[: width // 2], tail[width // 2 :]], 1)], 0
    )
    share = lax.psum_scatter(load, "col", scatter_dimension=0, tiled=True)
    full = lax.all_gather(share, "col", axis=0, tiled=True)
    tail = jnp.concatenate([full[tile_rows:, :width], full[tile_rows:, width:]], 0)
    panel_second = matmul(-full[:tile_rows, :width], inverse_second)
    panel_first = matmul(-(full[:tile_rows, width:] + matmul(panel_second, tail)), inverse_first)

    cross = tmatmul(matmul(-left[:, :width], inverse_second), rows_first)
    cross = cross + lax.ppermute(cross, "col", [(2 * i, 2 * i + 1) for i in range(SIDE)])
    others = [lax.ppermute(cross, "col", [(source, last)]) for source in (3, 1, 5)]
    cross = jnp.where(is_last, cross + others[0] + others[1] + others[2], 0.0)

    rows_both = jnp.concatenate([rows_second, rows_first], 1)
    half = tile_cols // 2
    quarter = half // SIDE
    first = tmatmul(grad_window[:, :half], rows_both)
    second = tmatmul(grad_window[:, half:], rows_both)
    second = second.at[half - width :, width:].add(cross)
    first, second = scatter_stage(
        [
            (first.reshape(SIDE, quarter, 2 * width), y, shift_y),
            (second.reshape(SIDE, quarter, 2 * width), z, shift_z),
        ]
    )
    first, second = sum_stage([(first, shift_z), (second, shift_y)])
    done = [
        jnp.concatenate(
            [matmul(-total[:, :width], inverse_second), matmul(-total[:, width:], inverse_first)], 1
        )
        for total in (first, second)
    ]
    pivots = [jnp.zeros((2 * SIDE, quarter, width), jnp.float32) for _ in range(2)]

    def place(value, index):
        for i in range(2):
            pivots[i] = lax.dynamic_update_index_in_dim(
                pivots[i], value[:, i * width : (i + 1) * width], index, 0
            )

    place(done[0], y)
    place(done[1], SIDE + z)
    for step in STEPS:
        place(shift_y(done[0], step), (y - step) % SIDE)
        place(shift_z(done[1], step), SIDE + (z - step) % SIDE)
    pivot_second, pivot_first = (value.reshape(tile_cols, width) for value in pivots)
    return (panel_second, pivot_second, panel_first, pivot_first)


def solution(mesh):
    in_specs = (
        P("row", "col"),
        P("row", None),
        P("col", None),
        P("row", None),
        P("col", None),
        P(),
        P(),
    )
    out_specs = (P("row", None), P("col", None), P("row", None), P("col", None))
    return jax.shard_map(local, mesh=mesh, in_specs=in_specs, out_specs=out_specs, check_vma=False)
```

time: 264 us -> 160 us (0.61)
  waiting for transfers between devices: 204 us -> 53.8 us
  starting transfers between devices: 0.52 us -> 39.4 us
  matrix products: 40.8 us -> 22.2 us
  local copies, waits for them, and re-layouts: 4 us -> 17.9 us
  other arithmetic: 0 us -> 10.4 us
    psum x3 -> x0, waiting for transfers between devices: 204 us -> none  [the longest x1 100 us: local(): pivot_sum = lax.psum(tmatmul(grad_window, rows_second), 'row')]
    ppermute x0 -> x22, waiting for transfers between devices: none -> 53.8 us  [the longest x9 36.3 us: shift_z(): return lax.ppermute(value, 'row', row_pairs(0, step))]
    ppermute x0 -> x22, starting transfers between devices: none -> 39.4 us  [the longest x9 19.9 us: shift_z(): return lax.ppermute(value, 'row', row_pairs(0, step))]
    dot_general x2 -> x3, matrix products: 18.3 us -> 8.54 us  [tmatmul(): lax.dot_general(left, right, (((0,), (0,)), ((), ())), precision=lax.Prec...]
    dot_general x6 -> x9, matrix products: 22.4 us -> 13.7 us  [matmul(): jnp.dot(left, right, precision=lax.Precision.HIGH, preferred_element_type...]
    add x0 -> x6, other arithmetic: none -> 6.85 us  [the longest x2 2.95 us: sum_stage(): own + got[i][0] + got[i][1] + got[i][2]]
    dynamic_update_slice x0 -> x6, local copies, waits for them, and re-layouts: none -> 6.41 us  [place(): lax.dynamic_update_index_in_dim(pivots[i], value[:, i * width:(i + 1) * w...]
  transfers between devices with their start and end apart: 3 -> 24, of which waited for: 3 -> 9; matrix products, arithmetic and copies ran while one was open for 8% -> 21% of each run, Pallas kernels for 0% -> 0%
where the time goes in v2:
time: 160 us; the launch traced here: 158 us
  waiting for transfers between devices  53.8 us (34%)
  starting transfers between devices  39.4 us (25%)
  matrix products  22.2 us (14%)
  local copies, waits for them, and re-layouts  17.9 us (11%)
  between operations  14.5 us (9%)
  other arithmetic  10.4 us (6%)
    ppermute x9, waiting for transfers between devices, shift_z(): return lax.ppermute(value, 'row', row_pairs(0, step))  36.3 us
    ppermute x9, starting transfers between devices, shift_z(): return lax.ppermute(value, 'row', row_pairs(0, step))  19.9 us
    ppermute x9, waiting for transfers between devices, shift_y(): return lax.ppermute(value, 'row', row_pairs(step, 0))  17.4 us
    ppermute x9, starting transfers between devices, shift_y(): return lax.ppermute(value, 'row', row_pairs(step, 0))  15.5 us
    dot_general x9, matrix products, matmul(): jnp.dot(left, right, precision=lax.Precision.HIGH, preferred_element_type...  13.7 us
    dot_general x3, matrix products, tmatmul(): lax.dot_general(left, right, (((0,), (0,)), ((), ())), precision=lax.Prec...  8.54 us
    dynamic_update_slice x6, local copies, waits for them, and re-layouts, place(): lax.dynamic_update_index_in_dim(pivots[i], value[:, i * width:(i + 1) * w...  6.41 us
  transfers between devices with their start and end apart: 24, of which 9 were waited for; matrix products, arithmetic and copies ran while one was open for 21% of the time, Pallas kernels for 0%

profile of v2, /device:TPU:0, one launch (start us, length us, event | category | flops | bytes accessed | tf_op | source)
XLA Modules:
  0.0 158.3 jit_solution(12060493307347191139)
XLA Ops:
  7.3 1.1 constant_dynamic-update-slice_fusion.1
  8.4 1.1 constant_dynamic-update-slice_fusion
  9.5 4.6 %fusion.8 = f32[896,512]{0,1:T(8,128)} fusion(f32[512,512]{1,0:T(8,128)S(1)} %constant_dynamic-update-slice_fusion, f32[512,1792]{1,0:T(8,128)} %param.9), kind=kOutput, calls=%fused_computation.8 | convolution fusion | flops 1409286144 | bytes 4718592 | tf_op jit(solution)/shard_map/dot_general | solution.py:14
  14.1 1.8 %copy.13 = f32[896,512]{1,0:T(8,128)S(1)} copy(f32[896,512]{0,1:T(8,128)} %fusion.8) | data formatting | bytes 3670016 | tf_op jit(solution)/shard_map/dot_general | solution.py:14
  16.0 1.2 dynamic-slice_bitcast_fusion.5
  17.1 3.3 %collective-permute-start = (f32[224,512]{1,0:T(8,128)}, f32[224,512]{1,0:T(8,128)}, u32[]{:S(2)}, u32[]{:S(2)}) collective-permute-start(f32[224,512]{1,0:T(8,128)} %get-tuple-element.19), channel_id=1, source_target_pairs={{0,64},{8,72},{16,80},{24,88},{32,96},{40,104},{48,112},{56,120},{... | collective-permute-start | bytes 1376264 | tf_op jit(solution)/shard_map/ppermute | solution.py:32
  21.1 2.6 %collective-permute-start.2 = (f32[224,512]{1,0:T(8,128)}, f32[224,512]{1,0:T(8,128)}, u32[]{:S(2)}, u32[]{:S(2)}) collective-permute-start(f32[224,512]{1,0:T(8,128)} %get-tuple-element.20), channel_id=1, source_target_pairs={{0,96},{8,104},{16,112},{24,120},{32,0},{40,8},{48,16},{56,24},{64... | collective-permute-start | bytes 1376264 | tf_op jit(solution)/shard_map/ppermute | solution.py:32
  23.6 7.2 %fusion.11 = f32[512,512]{1,0:T(8,128)} fusion(f32[512,1792]{1,0:T(8,128)} %param.9, f32[1792,256]{1,0:T(8,128)} %param.11, f32[1792,256]{1,0:T(8,128)} %param.13), kind=kOutput, calls=%fused_computation.9 | convolution fusion | flops 2819489792 | bytes 8388608 | tf_op jit(solution)/shard_map/dot_general | solution.py:10
  30.8 1.0 slice_select_fusion
  31.8 2.5 %maximum_maximum_fusion = f32[640,512]{1,0:T(8,128)} fusion(f32[128,256]{1,0:T(8,128)S(1)} %get-tuple-element.37, f32[128,256]{1,0:T(8,128)S(1)} %get-tuple-element.36, f32[512,512]{1,0:T(8,128)} %fusion.11), kind=kLoop, calls=%fused_computation.10 | loop fusion | flops 655360 | bytes 2621440 | tf_op jit(solution)/shard_map/concatenate | solution.py:79
  36.0 2.0 %collective-permute-start.6 = (f32[256,256]{1,0:T(8,128)S(1)}, f32[256,256]{1,0:T(8,128)}, u32[]{:S(2)}, u32[]{:S(2)}) collective-permute-start(f32[256,256]{1,0:T(8,128)S(1)} %fusion.44), channel_id=1, source_target_pairs={{0,1},{2,3},{4,5},{6,7},{8,9},{10,11},{12,13},{14,15},{16,17},{18,... | collective-permute-start | bytes 786440 | tf_op jit(solution)/shard_map/ppermute | solution.py:89
  38.0 3.3 %fusion.4 = f32[512,896]{1,0:T(8,128)S(1)} fusion(f32[512,512]{1,0:T(8,128)S(1)} %constant_dynamic-update-slice_fusion, f32[512,1792]{1,0:T(8,128)} %param.9), kind=kOutput, calls=%fused_computation.4 | convolution fusion | flops 1409286144 | bytes 4718592 | tf_op jit(solution)/shard_map/dot_general | solution.py:14
  41.6 1.0 add.218
  44.7 1.6 %fusion.20 = f32[224,512]{1,0:T(8,128)S(1)} fusion(f32[224,512]{1,0:T(8,128)} %collective-permute-done.2, f32[224,512]{1,0:T(8,128)} %collective-permute-done.1, f32[224,512]{1,0:T(8,128)} %collective-permute-done, f32[4,224,512]{2,1,0:T(8,128)} %bitcast.107, s32[]{:T(128)S(6)} %select_n.132), kind=kLoop, calls=%fused_computation.24 | loop fusion | flops 344064 | bytes 2293764 | tf_op jit(solution)/shard_map/add | solution.py:52
  46.3 4.0 %collective-permute-start.3 = (f32[224,512]{1,0:T(8,128)S(1)}, f32[224,512]{1,0:T(8,128)}, u32[]{:S(2)}, u32[]{:S(2)}) collective-permute-start(f32[224,512]{1,0:T(8,128)S(1)} %fusion.20), channel_id=1, source_target_pairs={{0,16},{8,24},{16,0},{24,8},{32,48},{40,56},{48,32},{56,40},{64,80... | collective-permute-start | bytes 1376264 | tf_op jit(solution)/shard_map/ppermute | solution.py:36
  50.3 1.0 collective-permute-start.4
  51.3 2.2 %collective-permute-start.5 = (f32[224,512]{1,0:T(8,128)S(1)}, f32[224,512]{1,0:T(8,128)}, u32[]{:S(2)}, u32[]{:S(2)}) collective-permute-start(f32[224,512]{1,0:T(8,128)S(1)} %fusion.20), channel_id=1, source_target_pairs={{0,24},{8,0},{16,8},{24,16},{32,56},{40,32},{48,40},{56,48},{64,88... | collective-permute-start | bytes 1376264 | tf_op jit(solution)/shard_map/ppermute | solution.py:36
  53.8 1.7 %copy.16 = f32[896,512]{1,0:T(8,128)} copy(f32[896,512]{0,1:T(8,128)S(1)} %constant_dynamic-update-slice_fusion.2) | data formatting | bytes 3670016 | tf_op jit(solution)/shard_map/scatter-add | solution.py:98
  55.5 1.4 dynamic-slice_bitcast_fusion.2
  57.0 0.9 collective-permute-start.11
  57.8 2.0 %collective-permute-done.3 = f32[224,512]{1,0:T(8,128)} collective-permute-done((f32[224,512]{1,0:T(8,128)S(1)}, f32[224,512]{1,0:T(8,128)}, u32[]{:S(2)}, u32[]{:S(2)}) %collective-permute-start.3) | collective-permute-done | bytes 458784 | tf_op jit(solution)/shard_map/ppermute | solution.py:36
  59.8 3.9 %collective-permute-start.12 = (f32[224,512]{1,0:T(8,128)S(1)}, f32[224,512]{1,0:T(8,128)S(1)}, u32[]{:S(2)}, u32[]{:S(2)}) collective-permute-start(f32[224,512]{1,0:T(8,128)S(1)} %get-tuple-element.17), channel_id=1, source_target_pairs={{0,24},{8,0},{16,8},{24,16},{32,56},{40,32},{48,40},{56,48},{64,88... | collective-permute-start | bytes 1376264 | tf_op jit(solution)/shard_map/ppermute | solution.py:36
  63.7 9.7 %collective-permute-done.4 = f32[224,512]{1,0:T(8,128)} collective-permute-done((f32[224,512]{1,0:T(8,128)S(1)}, f32[224,512]{1,0:T(8,128)}, u32[]{:S(2)}, u32[]{:S(2)}) %collective-permute-start.4) | collective-permute-done | bytes 458784 | tf_op jit(solution)/shard_map/ppermute | solution.py:36
  73.4 1.5 add_add_fusion.1
  74.9 4.5 %collective-permute-done.10 = f32[224,512]{1,0:T(8,128)S(1)} collective-permute-done((f32[224,512]{1,0:T(8,128)S(1)}, f32[224,512]{1,0:T(8,128)S(1)}, u32[]{:S(2)}, u32[]{:S(2)}) %collective-permute-start.10) | collective-permute-done | bytes 458784 | tf_op jit(solution)/shard_map/ppermute | solution.py:36
  79.4 11.6 %collective-permute-done.11 = f32[224,512]{1,0:T(8,128)S(1)} collective-permute-done((f32[224,512]{1,0:T(8,128)S(1)}, f32[224,512]{1,0:T(8,128)S(1)}, u32[]{:S(2)}, u32[]{:S(2)}) %collective-permute-start.11) | collective-permute-done | bytes 458784 | tf_op jit(solution)/shard_map/ppermute | solution.py:36
  91.1 1.2 fusion.18
  92.4 0.8 collective-permute-start.14
  93.2 2.5 %collective-permute-start.15 = (f32[224,512]{1,0:T(8,128)S(1)}, f32[224,512]{1,0:T(8,128)}, u32[]{:S(2)}, u32[]{:S(2)}) collective-permute-start(f32[224,512]{1,0:T(8,128)S(1)} %fusion.18), channel_id=1, source_target_pairs={{0,96},{8,104},{16,112},{24,120},{32,0},{40,8},{48,16},{56,24},{64... | collective-permute-start | bytes 1376264 | tf_op jit(solution)/shard_map/ppermute | solution.py:32
  97.4 2.3 %collective-permute-start.16 = (f32[224,512]{1,0:T(8,128)S(1)}, f32[224,512]{1,0:T(8,128)}, u32[]{:S(2)}, u32[]{:S(2)}) collective-permute-start(f32[224,512]{1,0:T(8,128)S(1)} %pad_maximum_fusion), channel_id=1, source_target_pairs={{0,64},{8,72},{16,80},{24,88},{32,96},{40,104},{48,112},{56,120},{... | collective-permute-start | bytes 1376264 | tf_op jit(solution)/shard_map/ppermute | solution.py:32
  99.7 7.7 %collective-permute-done.13 = f32[224,512]{1,0:T(8,128)} collective-permute-done((f32[224,512]{1,0:T(8,128)S(1)}, f32[224,512]{1,0:T(8,128)}, u32[]{:S(2)}, u32[]{:S(2)}) %collective-permute-start.13) | collective-permute-done | bytes 458784 | tf_op jit(solution)/shard_map/ppermute | solution.py:32
  107.4 9.5 %collective-permute-done.14 = f32[224,512]{1,0:T(8,128)} collective-permute-done((f32[224,512]{1,0:T(8,128)S(1)}, f32[224,512]{1,0:T(8,128)}, u32[]{:S(2)}, u32[]{:S(2)}) %collective-permute-start.14) | collective-permute-done | bytes 458784 | tf_op jit(solution)/shard_map/ppermute | solution.py:32
  116.9 1.5 add_add_fusion
  118.4 1.0 bitcast_dynamic-update-slice_fusion.2
  119.7 2.3 %collective-permute-start.17 = (f32[224,512]{1,0:T(8,128)S(1)}, f32[224,512]{1,0:T(8,128)}, u32[]{:S(2)}, u32[]{:S(2)}) collective-permute-start(f32[224,512]{1,0:T(8,128)S(1)} %pad_maximum_fusion.1), channel_id=1, source_target_pairs={{0,16},{8,24},{16,0},{24,8},{32,48},{40,56},{48,32},{56,40},{64,80... | collective-permute-start | bytes 1376264 | tf_op jit(solution)/shard_map/ppermute | solution.py:36
  122.0 3.2 %collective-permute-start.20 = (f32[224,512]{1,0:T(8,128)S(1)}, f32[224,512]{1,0:T(8,128)S(1)}, u32[]{:S(2)}, u32[]{:S(2)}) collective-permute-start(f32[224,512]{1,0:T(8,128)S(1)} %pad_maximum_fusion), channel_id=1, source_target_pairs={{0,96},{8,104},{16,112},{24,120},{32,0},{40,8},{48,16},{56,24},{64... | collective-permute-start | bytes 1376264 | tf_op jit(solution)/shard_map/ppermute | solution.py:32
  125.2 2.1 %collective-permute-start.19 = (f32[224,512]{1,0:T(8,128)S(1)}, f32[224,512]{1,0:T(8,128)S(1)}, u32[]{:S(2)}, u32[]{:S(2)}) collective-permute-start(f32[224,512]{1,0:T(8,128)S(1)} %pad_maximum_fusion.1), channel_id=1, source_target_pairs={{0,8},{8,16},{16,24},{24,0},{32,40},{40,48},{48,56},{56,32},{64,72... | collective-permute-start | bytes 1376264 | tf_op jit(solution)/shard_map/ppermute | solution.py:36
  127.3 3.4 %collective-permute-start.21 = (f32[224,512]{1,0:T(8,128)S(1)}, f32[224,512]{1,0:T(8,128)S(1)}, u32[]{:S(2)}, u32[]{:S(2)}) collective-permute-start(f32[224,512]{1,0:T(8,128)S(1)} %pad_maximum_fusion.1), channel_id=1, source_target_pairs={{0,24},{8,0},{16,8},{24,16},{32,56},{40,32},{48,40},{56,48},{64,88... | collective-permute-start | bytes 1376264 | tf_op jit(solution)/shard_map/ppermute | solution.py:36
  130.7 1.8 %fusion.29 = (f32[8,224,256]{2,1,0:T(8,128)S(1)}, f32[8,224,256]{2,1,0:T(8,128)}) fusion(f32[8,224,256]{2,1,0:T(8,128)S(1)} %get-tuple-element.40, s32[]{:T(128)S(6)} %select_n.151, f32[224,512]{1,0:T(8,128)} %collective-permute-done.16, f32[8,224,256]{2,1,0:T(8,128)} %get-tuple-element.44), kind=kLoop, calls=%fused_computation.49 | loop fusion | bytes 917508 | tf_op jit(solution)/shard_map/jit(dynamic_update_index_in_dim)/dynamic_update_slice | solution.py:116
  132.5 2.3 %collective-permute-done.17 = f32[224,512]{1,0:T(8,128)} collective-permute-done((f32[224,512]{1,0:T(8,128)S(1)}, f32[224,512]{1,0:T(8,128)}, u32[]{:S(2)}, u32[]{:S(2)}) %collective-permute-start.17) | collective-permute-done | bytes 458784 | tf_op jit(solution)/shard_map/ppermute | solution.py:36
  134.8 1.8 %fusion.28 = (f32[8,224,256]{2,1,0:T(8,128)S(1)}, f32[8,224,256]{2,1,0:T(8,128)}) fusion(f32[8,224,256]{2,1,0:T(8,128)S(1)} %get-tuple-element.34, s32[]{:T(128)S(6)} %select_n.153, f32[224,512]{1,0:T(8,128)} %collective-permute-done.17, f32[8,224,256]{2,1,0:T(8,128)} %get-tuple-element.35), kind=kLoop, calls=%fused_computation.47 | loop fusion | bytes 917508 | tf_op jit(solution)/shard_map/jit(dynamic_update_index_in_dim)/dynamic_update_slice | solution.py:116
  137.5 6.2 %collective-permute-done.19 = f32[224,512]{1,0:T(8,128)S(1)} collective-permute-done((f32[224,512]{1,0:T(8,128)S(1)}, f32[224,512]{1,0:T(8,128)S(1)}, u32[]{:S(2)}, u32[]{:S(2)}) %collective-permute-start.19) | collective-permute-done | bytes 458784 | tf_op jit(solution)/shard_map/ppermute | solution.py:36
  144.4 0.7 fusion.25
  145.1 0.7 fusion.24
  145.8 1.8 %fusion.16 = f32[512,256]{1,0:T(8,128)S(1)} fusion(f32[256,256]{1,0:T(8,128)S(1)} %copy-done, f32[640,512]{1,0:T(8,128)} %all-gather.2.cloned.1.call-done), kind=kOutput, calls=%fused_computation.16 | convolution fusion | flops 201457664 | bytes 1310720 | tf_op jit(solution)/shard_map/dot_general | solution.py:10
  147.6 1.2 fusion.42
  148.8 1.4 fusion.14
  150.3 1.2 fusion.45
  (60 shorter events, 8.6 us)
Async XLA Ops:
  7.2 27.3 %copy-start = (f32[256,256]{1,0:T(8,128)S(1)}, f32[256,256]{1,0:T(8,128)}, u32[]{:S(2)}) copy-start(f32[256,256]{1,0:T(8,128)} %param.15) | copy-start | bytes 786436
  7.2 92.5 %reduce-scatter.2.cloned.1.call-start = ((), (), s32[]{:S(2)}) async-start(), calls=%async_computation.1 | async-start | bytes 1474560 | tf_op jit(solution)/shard_map/reduce_scatter | solution.py:82
  15.9 14.9 %copy-start.1 = (f32[896,512]{1,0:T(8,128)}, f32[896,512]{1,0:T(8,128)S(1)}, u32[]{:S(2)}) copy-start(f32[896,512]{1,0:T(8,128)S(1)} %copy.13) | copy-start | bytes 5505028
  17.1 26.8 %collective-permute-start = (f32[224,512]{1,0:T(8,128)}, f32[224,512]{1,0:T(8,128)}, u32[]{:S(2)}, u32[]{:S(2)}) collective-permute-start(f32[224,512]{1,0:T(8,128)} %get-tuple-element.19), channel_id=1, source_target_pairs={{0,64},{8,72},{16,80},{24,88},{32,96},{40,104},{48,112},{56,120},{... | collective-permute-start | bytes 1376264 | tf_op jit(solution)/shard_map/ppermute | solution.py:32
  20.4 24.2 %collective-permute-start.1 = (f32[224,512]{1,0:T(8,128)}, f32[224,512]{1,0:T(8,128)}, u32[]{:S(2)}, u32[]{:S(2)}) collective-permute-start(f32[224,512]{1,0:T(8,128)} %get-tuple-element.21), channel_id=1, source_target_pairs={{0,32},{8,40},{16,48},{24,56},{32,64},{40,72},{48,80},{56,88},{64,... | collective-permute-start | bytes 1376264 | tf_op jit(solution)/shard_map/ppermute | solution.py:32
  21.1 23.6 %collective-permute-start.2 = (f32[224,512]{1,0:T(8,128)}, f32[224,512]{1,0:T(8,128)}, u32[]{:S(2)}, u32[]{:S(2)}) collective-permute-start(f32[224,512]{1,0:T(8,128)} %get-tuple-element.20), channel_id=1, source_target_pairs={{0,96},{8,104},{16,112},{24,120},{32,0},{40,8},{48,16},{56,24},{64... | collective-permute-start | bytes 1376264 | tf_op jit(solution)/shard_map/ppermute | solution.py:32
  31.8 2.6 %copy-start.2 = (f32[512,512]{1,0:T(8,128)S(1)}, f32[512,512]{1,0:T(8,128)}, u32[]{:S(2)}) copy-start(f32[512,512]{1,0:T(8,128)} %fusion.11) | copy-start | bytes 3145732
  34.4 1.0 copy-start.5
  34.4 111.4 %all-gather.2.cloned.1.call-start = ((), (), s32[]{:S(2)}) async-start(), calls=%async_computation.2 | async-start | bytes 1474560 | tf_op jit(solution)/shard_map/all_gather | solution.py:83
  36.0 5.6 %collective-permute-start.6 = (f32[256,256]{1,0:T(8,128)S(1)}, f32[256,256]{1,0:T(8,128)}, u32[]{:S(2)}, u32[]{:S(2)}) collective-permute-start(f32[256,256]{1,0:T(8,128)S(1)} %fusion.44), channel_id=1, source_target_pairs={{0,1},{2,3},{4,5},{6,7},{8,9},{10,11},{12,13},{14,15},{16,17},{18,... | collective-permute-start | bytes 786440 | tf_op jit(solution)/shard_map/ppermute | solution.py:89
  42.6 8.7 %collective-permute-start.7 = (f32[256,256]{1,0:T(8,128)S(1)}, f32[256,256]{1,0:T(8,128)S(1)}, u32[]{:S(2)}, u32[]{:S(2)}) collective-permute-start(f32[256,256]{1,0:T(8,128)S(1)} %add.218), channel_id=1, source_target_pairs={{3,7},{11,15},{19,23},{27,31},{35,39},{43,47},{51,55},{59,63},{67,... | collective-permute-start | bytes 786440 | tf_op jit(solution)/shard_map/ppermute | solution.py:90
  43.3 10.3 %collective-permute-start.8 = (f32[256,256]{1,0:T(8,128)S(1)}, f32[256,256]{1,0:T(8,128)S(1)}, u32[]{:S(2)}, u32[]{:S(2)}) collective-permute-start(f32[256,256]{1,0:T(8,128)S(1)} %add.218), channel_id=1, source_target_pairs={{1,7},{9,15},{17,23},{25,31},{33,39},{41,47},{49,55},{57,63},{65,7... | collective-permute-start | bytes 786440 | tf_op jit(solution)/shard_map/ppermute | solution.py:90
  44.0 9.6 %collective-permute-start.9 = (f32[256,256]{1,0:T(8,128)S(1)}, f32[256,256]{1,0:T(8,128)S(1)}, u32[]{:S(2)}, u32[]{:S(2)}) collective-permute-start(f32[256,256]{1,0:T(8,128)S(1)} %add.218), channel_id=1, source_target_pairs={{5,7},{13,15},{21,23},{29,31},{37,39},{45,47},{53,55},{61,63},{69,... | collective-permute-start | bytes 786440 | tf_op jit(solution)/shard_map/ppermute | solution.py:90
  46.3 13.5 %collective-permute-start.3 = (f32[224,512]{1,0:T(8,128)S(1)}, f32[224,512]{1,0:T(8,128)}, u32[]{:S(2)}, u32[]{:S(2)}) collective-permute-start(f32[224,512]{1,0:T(8,128)S(1)} %fusion.20), channel_id=1, source_target_pairs={{0,16},{8,24},{16,0},{24,8},{32,48},{40,56},{48,32},{56,40},{64,80... | collective-permute-start | bytes 1376264 | tf_op jit(solution)/shard_map/ppermute | solution.py:36
  50.3 23.1 %collective-permute-start.4 = (f32[224,512]{1,0:T(8,128)S(1)}, f32[224,512]{1,0:T(8,128)}, u32[]{:S(2)}, u32[]{:S(2)}) collective-permute-start(f32[224,512]{1,0:T(8,128)S(1)} %fusion.20), channel_id=1, source_target_pairs={{0,8},{8,16},{16,24},{24,0},{32,40},{40,48},{48,56},{56,32},{64,72... | collective-permute-start | bytes 1376264 | tf_op jit(solution)/shard_map/ppermute | solution.py:36
  51.3 22.1 %collective-permute-start.5 = (f32[224,512]{1,0:T(8,128)S(1)}, f32[224,512]{1,0:T(8,128)}, u32[]{:S(2)}, u32[]{:S(2)}) collective-permute-start(f32[224,512]{1,0:T(8,128)S(1)} %fusion.20), channel_id=1, source_target_pairs={{0,24},{8,0},{16,8},{24,16},{32,56},{40,32},{48,40},{56,48},{64,88... | collective-permute-start | bytes 1376264 | tf_op jit(solution)/shard_map/ppermute | solution.py:36
  56.9 22.5 %collective-permute-start.10 = (f32[224,512]{1,0:T(8,128)S(1)}, f32[224,512]{1,0:T(8,128)S(1)}, u32[]{:S(2)}, u32[]{:S(2)}) collective-permute-start(f32[224,512]{1,0:T(8,128)S(1)} %get-tuple-element.16), channel_id=1, source_target_pairs={{0,16},{8,24},{16,0},{24,8},{32,48},{40,56},{48,32},{56,40},{64,80... | collective-permute-start | bytes 1376264 | tf_op jit(solution)/shard_map/ppermute | solution.py:36
  57.0 34.1 %collective-permute-start.11 = (f32[224,512]{1,0:T(8,128)S(1)}, f32[224,512]{1,0:T(8,128)S(1)}, u32[]{:S(2)}, u32[]{:S(2)}) collective-permute-start(f32[224,512]{1,0:T(8,128)S(1)} %get-tuple-element.18), channel_id=1, source_target_pairs={{0,8},{8,16},{16,24},{24,0},{32,40},{40,48},{48,56},{56,32},{64,72... | collective-permute-start | bytes 1376264 | tf_op jit(solution)/shard_map/ppermute | solution.py:36
  59.8 31.2 %collective-permute-start.12 = (f32[224,512]{1,0:T(8,128)S(1)}, f32[224,512]{1,0:T(8,128)S(1)}, u32[]{:S(2)}, u32[]{:S(2)}) collective-permute-start(f32[224,512]{1,0:T(8,128)S(1)} %get-tuple-element.17), channel_id=1, source_target_pairs={{0,24},{8,0},{16,8},{24,16},{32,56},{40,32},{48,40},{56,48},{64,88... | collective-permute-start | bytes 1376264 | tf_op jit(solution)/shard_map/ppermute | solution.py:36
  92.3 15.2 %collective-permute-start.13 = (f32[224,512]{1,0:T(8,128)S(1)}, f32[224,512]{1,0:T(8,128)}, u32[]{:S(2)}, u32[]{:S(2)}) collective-permute-start(f32[224,512]{1,0:T(8,128)S(1)} %fusion.18), channel_id=1, source_target_pairs={{0,64},{8,72},{16,80},{24,88},{32,96},{40,104},{48,112},{56,120},{... | collective-permute-start | bytes 1376264 | tf_op jit(solution)/shard_map/ppermute | solution.py:32
  92.4 24.6 %collective-permute-start.14 = (f32[224,512]{1,0:T(8,128)S(1)}, f32[224,512]{1,0:T(8,128)}, u32[]{:S(2)}, u32[]{:S(2)}) collective-permute-start(f32[224,512]{1,0:T(8,128)S(1)} %fusion.18), channel_id=1, source_target_pairs={{0,32},{8,40},{16,48},{24,56},{32,64},{40,72},{48,80},{56,88},{64,... | collective-permute-start | bytes 1376264 | tf_op jit(solution)/shard_map/ppermute | solution.py:32
  93.2 23.8 %collective-permute-start.15 = (f32[224,512]{1,0:T(8,128)S(1)}, f32[224,512]{1,0:T(8,128)}, u32[]{:S(2)}, u32[]{:S(2)}) collective-permute-start(f32[224,512]{1,0:T(8,128)S(1)} %fusion.18), channel_id=1, source_target_pairs={{0,96},{8,104},{16,112},{24,120},{32,0},{40,8},{48,16},{56,24},{64... | collective-permute-start | bytes 1376264 | tf_op jit(solution)/shard_map/ppermute | solution.py:32
  95.8 1.0 copy-start.3
  96.1 1.2 copy-start.7
  97.4 29.9 %collective-permute-start.16 = (f32[224,512]{1,0:T(8,128)S(1)}, f32[224,512]{1,0:T(8,128)}, u32[]{:S(2)}, u32[]{:S(2)}) collective-permute-start(f32[224,512]{1,0:T(8,128)S(1)} %pad_maximum_fusion), channel_id=1, source_target_pairs={{0,64},{8,72},{16,80},{24,88},{32,96},{40,104},{48,112},{56,120},{... | collective-permute-start | bytes 1376264 | tf_op jit(solution)/shard_map/ppermute | solution.py:32
  119.7 15.1 %collective-permute-start.17 = (f32[224,512]{1,0:T(8,128)S(1)}, f32[224,512]{1,0:T(8,128)}, u32[]{:S(2)}, u32[]{:S(2)}) collective-permute-start(f32[224,512]{1,0:T(8,128)S(1)} %pad_maximum_fusion.1), channel_id=1, source_target_pairs={{0,16},{8,24},{16,0},{24,8},{32,48},{40,56},{48,32},{56,40},{64,80... | collective-permute-start | bytes 1376264 | tf_op jit(solution)/shard_map/ppermute | solution.py:36
  122.0 14.8 %collective-permute-start.18 = (f32[224,512]{1,0:T(8,128)S(1)}, f32[224,512]{1,0:T(8,128)S(1)}, u32[]{:S(2)}, u32[]{:S(2)}) collective-permute-start(f32[224,512]{1,0:T(8,128)S(1)} %pad_maximum_fusion), channel_id=1, source_target_pairs={{0,32},{8,40},{16,48},{24,56},{32,64},{40,72},{48,80},{56,88},{64,... | collective-permute-start | bytes 1376264 | tf_op jit(solution)/shard_map/ppermute | solution.py:32
  122.0 22.4 %collective-permute-start.20 = (f32[224,512]{1,0:T(8,128)S(1)}, f32[224,512]{1,0:T(8,128)S(1)}, u32[]{:S(2)}, u32[]{:S(2)}) collective-permute-start(f32[224,512]{1,0:T(8,128)S(1)} %pad_maximum_fusion), channel_id=1, source_target_pairs={{0,96},{8,104},{16,112},{24,120},{32,0},{40,8},{48,16},{56,24},{64... | collective-permute-start | bytes 1376264 | tf_op jit(solution)/shard_map/ppermute | solution.py:32
  125.2 18.4 %collective-permute-start.19 = (f32[224,512]{1,0:T(8,128)S(1)}, f32[224,512]{1,0:T(8,128)S(1)}, u32[]{:S(2)}, u32[]{:S(2)}) collective-permute-start(f32[224,512]{1,0:T(8,128)S(1)} %pad_maximum_fusion.1), channel_id=1, source_target_pairs={{0,8},{8,16},{16,24},{24,0},{32,40},{40,48},{48,56},{56,32},{64,72... | collective-permute-start | bytes 1376264 | tf_op jit(solution)/shard_map/ppermute | solution.py:36
  127.3 17.8 %collective-permute-start.21 = (f32[224,512]{1,0:T(8,128)S(1)}, f32[224,512]{1,0:T(8,128)S(1)}, u32[]{:S(2)}, u32[]{:S(2)}) collective-permute-start(f32[224,512]{1,0:T(8,128)S(1)} %pad_maximum_fusion.1), channel_id=1, source_target_pairs={{0,24},{8,0},{16,8},{24,16},{32,56},{40,32},{48,40},{56,48},{64,88... | collective-permute-start | bytes 1376264 | tf_op jit(solution)/shard_map/ppermute | solution.py:36
  145.8 4.4 %copy-start.6 = (f32[8,224,256]{2,1,0:T(8,128)}, f32[8,224,256]{2,1,0:T(8,128)S(1)}, u32[]{:S(2)}) copy-start(f32[8,224,256]{2,1,0:T(8,128)S(1)} %get-tuple-element.24) | copy-start | bytes 5505028
  147.6 3.8 %copy-start.4 = (f32[512,256]{1,0:T(8,128)}, f32[512,256]{1,0:T(8,128)S(1)}, u32[]{:S(2)}) copy-start(f32[512,256]{1,0:T(8,128)S(1)} %fusion.16) | copy-start | bytes 1572868
Sparse Core Ops, SparseCore 0:
  34.5 35.5 reduce-scatter.1
  99.8 23.9 all-gather.1

commit v3 on v0

v3 whole, which is shorter than its diff:
```python
import jax
import jax.numpy as jnp
from jax import lax
from jax.experimental import pallas as pl
from jax.experimental.pallas import tpu as pltpu
from jax.sharding import PartitionSpec as P

SIDE = 4
STEPS = (2, 1, 3)


def matmul(left, right):
    return jnp.dot(left, right, precision=lax.Precision.HIGH, preferred_element_type=jnp.float32)


def pairs(step, swap):
    out = []
    for y in range(SIDE):
        for z in range(SIDE):
            for x in range(SIDE):
                for core in range(2):
                    if core == swap:
                        to_y, to_z = (y + step) % SIDE, z
                    else:
                        to_y, to_z = y, (z + step) % SIDE
                    out.append(
                        (
                            (y * SIDE + z) * 2 * SIDE + 2 * x + core,
                            (to_y * SIDE + to_z) * 2 * SIDE + 2 * x + core,
                        )
                    )
    return out


def shift(value, step, swap):
    return lax.ppermute(value, ("row", "col"), pairs(step, swap))


def block(value, index):
    return lax.dynamic_index_in_dim(value, index, 0, keepdims=False)


def split(value):
    high = value.astype(jnp.bfloat16)
    return high, (value - high.astype(jnp.float32)).astype(jnp.bfloat16)


def dot3(left, right):
    total = jnp.dot(left[0], right[1], preferred_element_type=jnp.float32)
    total += jnp.dot(left[1], right[0], preferred_element_type=jnp.float32)
    return total + jnp.dot(left[0], right[0], preferred_element_type=jnp.float32)


def tdot3(left, right):
    def product(a, b):
        return lax.dot_general(a, b, (((0,), (0,)), ((), ())), preferred_element_type=jnp.float32)

    return product(left[0], right[1]) + product(left[1], right[0]) + product(left[0], right[0])


def whole(shape):
    return pl.BlockSpec(shape, lambda i: (0,) * len(shape))


def panel_kernel(full_ref, second_ref, first_ref, panel_second_ref, panel_first_ref):
    rows = panel_second_ref.shape[0]
    panel = dot3(split(-full_ref[:rows]), split(second_ref[...]))
    panel_second_ref[...] = panel
    left = full_ref[rows : 2 * rows] + dot3(split(panel), split(full_ref[2 * rows :]))
    panel_first_ref[...] = dot3(split(-left), split(first_ref[...]))


def panels(full, inverse_second, inverse_first):
    width = inverse_first.shape[0]
    rows = (full.shape[0] - width) // 2
    shape = jax.ShapeDtypeStruct((rows, width), jnp.float32)
    return pl.pallas_call(
        panel_kernel,
        grid=(1,),
        in_specs=[whole(full.shape), whole((width, width)), whole((width, width))],
        out_specs=[whole((rows, width))] * 2,
        out_shape=[shape, shape],
        cost_estimate=pl.CostEstimate(
            flops=18 * rows * width * width, bytes_accessed=16 * rows * width, transcendentals=0
        ),
        name="panels",
    )(full, inverse_second, inverse_first)


def place_of(row, col):
    return jnp.where(lax.rem(col, 2) == 0, lax.div(row, SIDE), lax.rem(row, SIDE))


def products_kernel(
    window_hbm, cols_second_hbm, cols_first_hbm, rows_second_hbm, rows_first_hbm, inverse_hbm,
    load_hbm, cross_hbm, *refs,
):
    outs, refs = refs[:SIDE], refs[SIDE:]
    (window, cols, rows, inverse, left, tail, pivot, cross, high, low, sem_in, sem_chunk, sem_out,
     sem_pivot) = refs
    chunks, tile_rows, width = window.shape
    piece = width // SIDE
    halves = (slice(0, width), slice(width, 2 * width))

    ready = [
        pltpu.make_async_copy(rows_second_hbm, rows.at[:, halves[0]], sem_in.at[0]),
        pltpu.make_async_copy(rows_first_hbm, rows.at[:, halves[1]], sem_in.at[1]),
        pltpu.make_async_copy(inverse_hbm, inverse, sem_in.at[2]),
    ]
    arriving = []
    for j in range(chunks):
        at = pl.ds(j * width, width)
        arriving.append(
            [
                pltpu.make_async_copy(window_hbm.at[:, at], window.at[j], sem_chunk.at[j, 0]),
                pltpu.make_async_copy(
                    cols_second_hbm.at[at], cols.at[j, :, halves[0]], sem_chunk.at[j, 1]
                ),
                pltpu.make_async_copy(
                    cols_first_hbm.at[at], cols.at[j, :, halves[1]], sem_chunk.at[j, 2]
                ),
            ]
        )
    for copy in ready[:2] + [copy for group in arriving for copy in group] + ready[2:]:
        copy.start()

    place = place_of(lax.axis_index("row"), lax.axis_index("col"))
    leaving = []
    for copy in ready[:2]:
        copy.wait()
    high[...], low[...] = split(rows[...])
    for j in range(chunks):
        for copy in arriving[j]:
            copy.wait()
        part = split(window[j])
        product = dot3(part, split(cols[j]))
        if j == 0:
            left[...] = product
        else:
            left[...] += product
        pivot[j] = tdot3(part, (high[...], low[...]))
        for step in range(SIDE):
            start = pl.multiple_of(lax.rem(place + step, SIDE) * piece, piece)
            for i in range(2):
                copy = pltpu.make_async_copy(
                    pivot.at[j, pl.ds(start, piece), halves[i]],
                    outs[step].at[pl.ds((i * chunks + j) * piece, piece)],
                    sem_pivot.at[j, i * SIDE + step],
                )
                copy.start()
                leaving.append(copy)

    is_last = lax.axis_index("col") == 2 * SIDE - 1
    tail[...] = jnp.where(is_last, cols[chunks - 1, :, halves[1]], 0.0)
    for i, source in enumerate((left.at[:, halves[0]], left.at[:, halves[1]], tail)):
        copy = pltpu.make_async_copy(
            source, load_hbm.at[pl.ds(i * tile_rows, source.shape[0])], sem_out.at[i]
        )
        copy.start()
        leaving.append(copy)
    ready[2].wait()
    panel = dot3(split(left[:, halves[0]]), split(inverse[...]))
    cross[...] = tdot3(split(-panel), (high[:, halves[1]], low[:, halves[1]]))
    copy = pltpu.make_async_copy(cross, cross_hbm, sem_out.at[3])
    copy.start()
    for copy in leaving + [copy]:
        copy.wait()


def products(window, cols_second, cols_first, rows_second, rows_first, inverse):
    tile_rows, tile_cols = window.shape
    width = inverse.shape[0]
    chunks = tile_cols // width
    hbm = pl.BlockSpec(memory_space=pl.ANY)
    f32 = lambda *shape: jax.ShapeDtypeStruct(shape, jnp.float32)
    buffer = lambda *shape: pltpu.VMEM(shape, jnp.float32)
    return pl.pallas_call(
        products_kernel,
        in_specs=[hbm] * 6,
        out_specs=[hbm] * (2 + SIDE),
        out_shape=[f32(2 * tile_rows + width, width), f32(width, width)]
        + [f32(2 * tile_cols // SIDE, width)] * SIDE,
        scratch_shapes=[
            buffer(chunks, tile_rows, width),
            buffer(chunks, width, 2 * width),
            buffer(tile_rows, 2 * width),
            buffer(width, width),
            buffer(tile_rows, 2 * width),
            buffer(width, width),
            buffer(chunks, width, 2 * width),
            buffer(width, width),
            pltpu.VMEM((tile_rows, 2 * width), jnp.bfloat16),
            pltpu.VMEM((tile_rows, 2 * width), jnp.bfloat16),
            pltpu.SemaphoreType.DMA((3,)),
            pltpu.SemaphoreType.DMA((chunks, 3)),
            pltpu.SemaphoreType.DMA((4,)),
            pltpu.SemaphoreType.DMA((chunks, 2 * SIDE)),
        ],
        cost_estimate=pl.CostEstimate(
            flops=24 * tile_rows * tile_cols * width,
            bytes_accessed=4 * (tile_rows * tile_cols + 4 * tile_cols * width),
            transcendentals=0,
        ),
        name="products",
    )(window, cols_second, cols_first, rows_second, rows_first, inverse)


def after(value, *others):
    return lax.optimization_barrier((value,) + others)[0]


def local(
    grad_window, rows_first, cols_first, rows_second, cols_second, inverse_first, inverse_second
):
    row = lax.axis_index("row")
    col = lax.axis_index("col")
    last = 2 * SIDE - 1
    is_last = col == last
    tile_cols = grad_window.shape[1]
    width = inverse_first.shape[0]
    chunks, piece = tile_cols // width, width // SIDE
    place = place_of(row, col)

    load, cross, *blocks = products(
        grad_window, cols_second, cols_first, rows_second, rows_first, inverse_second
    )

    share = lax.psum_scatter(load, "col", scatter_dimension=0, tiled=True)

    cross = cross + lax.ppermute(cross, "col", [(2 * i, 2 * i + 1) for i in range(SIDE)])
    others = [lax.ppermute(cross, "col", [(source, last)]) for source in (3, 1, 5)]
    cross = jnp.where(is_last, cross + others[0] + others[1] + others[2], 0.0)
    late = cross.reshape(SIDE, piece, width)
    late = [block(late, (place + step) % SIDE) for step in range(SIDE)]

    def arrivals(values, swap):
        return [shift(values[step], step, swap) for step in STEPS]

    got = arrivals(blocks, 0)
    got_late = arrivals(late, 0)
    value = blocks[0] + got[0] + got[1] + got[2]
    late = late[0] + got_late[0] + got_late[1] + got_late[2]
    value = value.at[value.shape[0] - piece :].add(late)

    got = arrivals([value] * SIDE, 1)
    full = lax.all_gather(after(share, got[0]), "col", axis=0, tiled=True)
    panel_second, panel_first = panels(full, inverse_second, inverse_first)
    value = value + got[0] + got[1] + got[2]

    half = value.shape[0] // 2
    value = jnp.concatenate(
        [matmul(-value[:half], inverse_second), matmul(-value[half:], inverse_first)], 0
    )
    got = arrivals([value] * SIDE, 0)
    pivots = [jnp.zeros((chunks, SIDE, piece, width), jnp.float32)] * 2
    parts = [(value, 0)] + list(zip(got, STEPS))
    for i, (part, step) in enumerate(parts):
        if i == len(parts) - 2:
            pivots = after(pivots, panel_second, panel_first)
        pivots = [
            lax.dynamic_update_index_in_dim(
                pivot, rows.reshape(chunks, piece, width), (place - step) % SIDE, 1
            )
            for pivot, rows in zip(pivots, (part[:half], part[half:]))
        ]
    pivot_second, pivot_first = (pivot.reshape(tile_cols, width) for pivot in pivots)
    return (panel_second, pivot_second, panel_first, pivot_first)


def solution(mesh):
    in_specs = (
        P("row", "col"),
        P("row", None),
        P("col", None),
        P("row", None),
        P("col", None),
        P(),
        P(),
    )
    out_specs = (P("row", None), P("col", None), P("row", None), P("col", None))
    return jax.shard_map(local, mesh=mesh, in_specs=in_specs, out_specs=out_specs, check_vma=False)
```

time: 264 us -> 121 us (0.46)
  waiting for transfers between devices: 204 us -> 55.6 us
  matrix products: 40.8 us -> 0.7 us
  starting transfers between devices: 0.52 us -> 23.3 us
  Pallas kernels: 0 us -> 16.3 us
  other arithmetic: 0 us -> 3.75 us
    psum x3 -> x0, waiting for transfers between devices: 204 us -> none  [the longest x1 100 us: local(): pivot_sum = lax.psum(tmatmul(grad_window, rows_second), 'row')]
    ppermute x0 -> x16, waiting for transfers between devices: none -> 55.5 us  [the longest x12 55.5 us: shift(): return lax.ppermute(value, ('row', 'col'), pairs(step, swap))]
    dot_general x8 -> x2, matrix products: 40.8 us -> 0.7 us  [matmul(): jnp.dot(left, right, precision=lax.Precision.HIGH, preferred_element_type...]
    ppermute x0 -> x16, starting transfers between devices: none -> 23.3 us  [the longest x12 19.2 us: shift(): return lax.ppermute(value, ('row', 'col'), pairs(step, swap))]
    pallas_call x0 -> x2, Pallas kernels: none -> 16.3 us  [the longest x1 12.9 us: products(): pl.pallas_call(products_kernel, in_specs=[hbm] * 6, out_specs=[hbm] * (2...]
    unnamed x17 -> x10, local copies, waits for them, and re-layouts: 4 us -> 0.03 us
    dynamic_update_slice x0 -> x7, local copies, waits for them, and re-layouts: none -> 3.38 us  [local(): lax.dynamic_update_index_in_dim(pivot, rows.reshape(chunks, piece, width)...]
    add x0 -> x3, other arithmetic: none -> 2.65 us  [the longest x1 1.42 us: local(): value = blocks[0] + got[0] + got[1] + got[2]]
  transfers between devices with their start and end apart: 3 -> 18, of which waited for: 3 -> 8; matrix products, arithmetic and copies ran while one was open for 8% -> 6% of each run, Pallas kernels for 0% -> 0%
where the time goes in v3:
time: 121 us; the launch traced here: 120 us
  waiting for transfers between devices  55.6 us (46%)
  starting transfers between devices  23.3 us (19%)
  Pallas kernels  16.3 us (13%)
  between operations  14.3 us (12%)
  local copies, waits for them, and re-layouts  6.31 us (5%)
  other arithmetic  3.75 us (3%)
    ppermute x12, waiting for transfers between devices, shift(): return lax.ppermute(value, ('row', 'col'), pairs(step, swap))  55.5 us
    ppermute x12, starting transfers between devices, shift(): return lax.ppermute(value, ('row', 'col'), pairs(step, swap))  19.2 us
    pallas_call x1, Pallas kernels, products(): pl.pallas_call(products_kernel, in_specs=[hbm] * 6, out_specs=[hbm] * (2...  12.9 us
    pallas_call x1, Pallas kernels, panels(): pl.pallas_call(panel_kernel, grid=(1,), in_specs=[whole(full.shape), whol...  3.4 us
    dynamic_update_slice x7, local copies, waits for them, and re-layouts, local(): lax.dynamic_update_index_in_dim(pivot, rows.reshape(chunks, piece, width)...  3.38 us
    ppermute x3, starting transfers between devices, local(): lax.ppermute(cross, 'col', [(source, last)])  2.71 us
    slice x3, local copies, waits for them, and re-layouts, local(): part[half:]  2.49 us
  transfers between devices with their start and end apart: 18, of which 8 were waited for; matrix products, arithmetic and copies ran while one was open for 6% of the time, Pallas kernels for 0%

profile of v3, /device:TPU:0, one launch (start us, length us, event | category | flops | bytes accessed | tf_op | source)
XLA Modules:
  0.0 120.3 jit_solution(16217253854838073763)
XLA Ops:
  7.2 0.0 reduce-scatter.2.cloned.1.call-start
  7.2 12.9 %products.1 = (f32[1280,256]{1,0:T(8,128)}, f32[256,256]{1,0:T(8,128)}, f32[896,256]{1,0:T(8,128)}, f32[896,256]{1,0:T(8,128)}, f32[896,256]{1,0:T(8,128)}, /*index=5*/f32[896,256]{1,0:T(8,128)}) custom-call(f32[512,1792]{1,0:T(8,128)} %window_hbm.1, f32[1792,256]{1,0:T(8,128)} %cols_second_hbm.1, f32[1792,256]{1,0:T(8,128)} %cols_first_hbm.1, ...), custom_call_target="tpu_custom_call" | custom-call | flops 5637144576 | bytes 11010048 | tf_op jit(solution)/shard_map/products/pallas_call | solution.py:177
  20.1 1.3 %collective-permute-start.3 = (f32[256,256]{1,0:T(8,128)}, f32[256,256]{1,0:T(8,128)S(1)}, u32[]{:S(2)}, u32[]{:S(2)}) collective-permute-start(f32[256,256]{1,0:T(8,128)} %get-tuple-element.32), channel_id=1, source_target_pairs={{0,1},{2,3},{4,5},{6,7},{8,9},{10,11},{12,13},{14,15},{16,17},{18,... | collective-permute-start | bytes 786440 | tf_op jit(solution)/shard_map/ppermute | solution.py:230
  21.4 3.6 %collective-permute-start.2 = (f32[896,256]{1,0:T(8,128)}, f32[896,256]{1,0:T(8,128)S(1)}, u32[]{:S(2)}, u32[]{:S(2)}) collective-permute-start(f32[896,256]{1,0:T(8,128)} %get-tuple-element.31), channel_id=1, source_target_pairs={{0,96},{1,25},{2,98},{3,27},{4,100},{5,29},{6,102},{7,31},{8,104},... | collective-permute-start | bytes 2752520 | tf_op jit(solution)/shard_map/ppermute | solution.py:36
  25.1 2.2 %collective-permute-start = (f32[896,256]{1,0:T(8,128)}, f32[896,256]{1,0:T(8,128)}, u32[]{:S(2)}, u32[]{:S(2)}) collective-permute-start(f32[896,256]{1,0:T(8,128)} %get-tuple-element.29), channel_id=1, source_target_pairs={{0,64},{1,17},{2,66},{3,19},{4,68},{5,21},{6,70},{7,23},{8,72},{9,... | collective-permute-start | bytes 2752520 | tf_op jit(solution)/shard_map/ppermute | solution.py:36
  27.3 1.0 add.118
  28.3 0.7 collective-permute-start.6
  28.9 0.0 reduce-scatter.2.cloned.1.call-update
  29.0 0.0 all-gather.2.cloned.1.call-start
  29.0 0.7 collective-permute-start.5
  29.7 1.4 %collective-permute-start.4 = (f32[256,256]{1,0:T(8,128)S(1)}, f32[256,256]{1,0:T(8,128)}, u32[]{:S(2)}, u32[]{:S(2)}) collective-permute-start(f32[256,256]{1,0:T(8,128)S(1)} %add.118), channel_id=1, source_target_pairs={{3,7},{11,15},{19,23},{27,31},{35,39},{43,47},{51,55},{59,63},{67,... | collective-permute-start | bytes 786440 | tf_op jit(solution)/shard_map/ppermute | solution.py:231
  31.1 1.0 add_select_fusion
  32.1 1.2 collective-permute-start.9
  33.3 0.9 collective-permute-start.8
  34.2 11.9 %collective-permute-done.2 = f32[896,256]{1,0:T(8,128)S(1)} collective-permute-done((f32[896,256]{1,0:T(8,128)}, f32[896,256]{1,0:T(8,128)S(1)}, u32[]{:S(2)}, u32[]{:S(2)}) %collective-permute-start.2) | collective-permute-done | bytes 917536 | tf_op jit(solution)/shard_map/ppermute | solution.py:36
  46.1 3.6 %collective-permute-done.1 = f32[896,256]{1,0:T(8,128)S(1)} collective-permute-done((f32[896,256]{1,0:T(8,128)}, f32[896,256]{1,0:T(8,128)S(1)}, u32[]{:S(2)}, u32[]{:S(2)}) %collective-permute-start.1) | collective-permute-done | bytes 917536 | tf_op jit(solution)/shard_map/ppermute | solution.py:36
  49.7 1.4 %add_add_fusion.1 = f32[896,256]{1,0:T(8,128)S(1)} fusion(f32[896,256]{1,0:T(8,128)S(1)} %collective-permute-done.2, f32[896,256]{1,0:T(8,128)S(1)} %collective-permute-done.1, f32[896,256]{1,0:T(8,128)S(1)} %copy-done.2, f32[896,256]{1,0:T(8,128)} %collective-permute-done), kind=kLoop, calls=%fused_computation.2 | loop fusion | flops 688128 | bytes 4587520 | tf_op jit(solution)/shard_map/add | solution.py:241
  51.2 0.7 collective-permute-done.7
  51.9 0.0 copy-start.4
  51.9 4.3 %collective-permute-start.10 = (f32[896,256]{1,0:T(8,128)S(1)}, f32[896,256]{1,0:T(8,128)S(1)}, u32[]{:S(2)}, u32[]{:S(2)}) collective-permute-start(f32[896,256]{1,0:T(8,128)S(1)} %fusion.2), channel_id=1, source_target_pairs={{0,16},{1,65},{2,18},{3,67},{4,20},{5,69},{6,22},{7,71},{8,24},{9,... | collective-permute-start | bytes 2752520 | tf_op jit(solution)/shard_map/ppermute | solution.py:36
  56.3 0.3 collective-permute-start.12
  56.6 1.7 %collective-permute-start.11 = (f32[896,256]{1,0:T(8,128)S(1)}, f32[896,256]{1,0:T(8,128)S(1)}, u32[]{:S(2)}, u32[]{:S(2)}) collective-permute-start(f32[896,256]{1,0:T(8,128)S(1)} %fusion.2), channel_id=1, source_target_pairs={{0,8},{1,33},{2,10},{3,35},{4,12},{5,37},{6,14},{7,39},{8,16},{9,4... | collective-permute-start | bytes 2752520 | tf_op jit(solution)/shard_map/ppermute | solution.py:36
  58.3 9.5 %collective-permute-done.10 = f32[896,256]{1,0:T(8,128)S(1)} collective-permute-done((f32[896,256]{1,0:T(8,128)S(1)}, f32[896,256]{1,0:T(8,128)S(1)}, u32[]{:S(2)}, u32[]{:S(2)}) %collective-permute-start.10) | collective-permute-done | bytes 917536 | tf_op jit(solution)/shard_map/ppermute | solution.py:36
  67.8 10.4 %collective-permute-done.12 = f32[896,256]{1,0:T(8,128)S(1)} collective-permute-done((f32[896,256]{1,0:T(8,128)S(1)}, f32[896,256]{1,0:T(8,128)S(1)}, u32[]{:S(2)}, u32[]{:S(2)}) %collective-permute-start.12) | collective-permute-done | bytes 917536 | tf_op jit(solution)/shard_map/ppermute | solution.py:36
  78.2 0.2 add_add_fusion
  78.4 0.0 reduce-scatter.2.cloned.1.call-done
  78.4 0.0 all-gather.2.cloned.1.call-update
  78.5 0.4 fusion.1
  78.8 0.3 fusion
  79.2 0.1 pad_maximum_fusion
  79.3 0.1 collective-permute-start.13
  79.4 4.9 %collective-permute-start.14 = (f32[896,256]{1,0:T(8,128)S(1)}, f32[896,256]{1,0:T(8,128)}, u32[]{:S(2)}, u32[]{:S(2)}) collective-permute-start(f32[896,256]{1,0:T(8,128)S(1)} %pad_maximum_fusion), channel_id=1, source_target_pairs={{0,32},{1,9},{2,34},{3,11},{4,36},{5,13},{6,38},{7,15},{8,40},{9,1... | collective-permute-start | bytes 2752520 | tf_op jit(solution)/shard_map/ppermute | solution.py:36
  84.2 0.2 broadcast_in_dim.33.clone
  84.5 0.2 broadcast_in_dim.33.clone.1
  84.7 9.6 %collective-permute-done.13 = f32[896,256]{1,0:T(8,128)S(1)} collective-permute-done((f32[896,256]{1,0:T(8,128)S(1)}, f32[896,256]{1,0:T(8,128)S(1)}, u32[]{:S(2)}, u32[]{:S(2)}) %collective-permute-start.13) | collective-permute-done | bytes 917536 | tf_op jit(solution)/shard_map/ppermute | solution.py:36
  94.3 0.1 fusion.7
  94.4 0.1 constant_dynamic-update-slice_fusion.3
  94.5 0.0 copy-start.1
  94.5 9.6 %collective-permute-done.14 = f32[896,256]{1,0:T(8,128)} collective-permute-done((f32[896,256]{1,0:T(8,128)S(1)}, f32[896,256]{1,0:T(8,128)}, u32[]{:S(2)}, u32[]{:S(2)}) %collective-permute-start.14) | collective-permute-done | bytes 917536 | tf_op jit(solution)/shard_map/ppermute | solution.py:36
  104.2 1.2 %fusion.6 = (f32[448,256]{1,0:T(8,128)S(1)}, f32[448,256]{1,0:T(8,128)S(1)}) fusion(f32[896,256]{1,0:T(8,128)} %collective-permute-done.14), kind=kLoop, calls=%fused_computation.25 | loop fusion | bytes 1835008 | tf_op jit(solution)/shard_map/slice | solution.py:264
  105.4 0.2 collective-permute-done.15
  105.6 1.2 %fusion.5 = (f32[448,256]{1,0:T(8,128)S(1)}, f32[448,256]{1,0:T(8,128)S(1)}) fusion(f32[896,256]{1,0:T(8,128)} %collective-permute-done.15), kind=kLoop, calls=%fused_computation.24 | loop fusion | bytes 1835008 | tf_op jit(solution)/shard_map/slice | solution.py:264
  106.8 0.0 all-gather.2.cloned.1.call-done.full_ref
  106.8 3.4 %panels.1 = (f32[512,256]{1,0:T(8,128)}, f32[512,256]{1,0:T(8,128)}) custom-call(f32[1280,256]{1,0:T(8,128)} %all-gather.2.cloned.1.call-done.full_ref, f32[256,256]{1,0:T(8,128)} %second_ref.1, f32[256,256]{1,0:T(8,128)} %first_ref.1), custom_call_target="tpu_custom_call" | custom-call | flops 603979776 | bytes 2097152 | tf_op jit(solution)/shard_map/panels/pallas_call | solution.py:77
  110.2 0.8 constant_dynamic-update-slice_fusion.2
  111.0 0.8 constant_dynamic-update-slice_fusion
  111.8 0.8 constant_dynamic-update-slice_fusion.1
  112.6 0.8 constant_dynamic-update-slice_fusion.7
  (23 shorter events, 0.2 us)
Async XLA Ops:
  7.2 71.3 %reduce-scatter.2.cloned.1.call-start = ((), (), s32[]{:S(2)}) async-start(), calls=%async_computation.1 | async-start | bytes 1474560 | tf_op jit(solution)/shard_map/reduce_scatter | solution.py:228
  20.1 7.1 %collective-permute-start.3 = (f32[256,256]{1,0:T(8,128)}, f32[256,256]{1,0:T(8,128)S(1)}, u32[]{:S(2)}, u32[]{:S(2)}) collective-permute-start(f32[256,256]{1,0:T(8,128)} %get-tuple-element.32), channel_id=1, source_target_pairs={{0,1},{2,3},{4,5},{6,7},{8,9},{10,11},{12,13},{14,15},{16,17},{18,... | collective-permute-start | bytes 786440 | tf_op jit(solution)/shard_map/ppermute | solution.py:230
  21.4 24.7 %collective-permute-start.2 = (f32[896,256]{1,0:T(8,128)}, f32[896,256]{1,0:T(8,128)S(1)}, u32[]{:S(2)}, u32[]{:S(2)}) collective-permute-start(f32[896,256]{1,0:T(8,128)} %get-tuple-element.31), channel_id=1, source_target_pairs={{0,96},{1,25},{2,98},{3,27},{4,100},{5,29},{6,102},{7,31},{8,104},... | collective-permute-start | bytes 2752520 | tf_op jit(solution)/shard_map/ppermute | solution.py:36
  25.1 24.6 %collective-permute-start.1 = (f32[896,256]{1,0:T(8,128)}, f32[896,256]{1,0:T(8,128)S(1)}, u32[]{:S(2)}, u32[]{:S(2)}) collective-permute-start(f32[896,256]{1,0:T(8,128)} %get-tuple-element.30), channel_id=1, source_target_pairs={{0,32},{1,9},{2,34},{3,11},{4,36},{5,13},{6,38},{7,15},{8,40},{9,1... | collective-permute-start | bytes 2752520 | tf_op jit(solution)/shard_map/ppermute | solution.py:36
  25.1 24.6 %copy-start.2 = (f32[896,256]{1,0:T(8,128)S(1)}, f32[896,256]{1,0:T(8,128)}, u32[]{:S(2)}) copy-start(f32[896,256]{1,0:T(8,128)} %get-tuple-element.28) | copy-start | bytes 2752516
  25.1 24.6 %collective-permute-start = (f32[896,256]{1,0:T(8,128)}, f32[896,256]{1,0:T(8,128)}, u32[]{:S(2)}, u32[]{:S(2)}) collective-permute-start(f32[896,256]{1,0:T(8,128)} %get-tuple-element.29), channel_id=1, source_target_pairs={{0,64},{1,17},{2,66},{3,19},{4,68},{5,21},{6,70},{7,23},{8,72},{9,... | collective-permute-start | bytes 2752520 | tf_op jit(solution)/shard_map/ppermute | solution.py:36
  28.3 1.4 %collective-permute-start.6 = (f32[256,256]{1,0:T(8,128)S(1)}, f32[256,256]{1,0:T(8,128)S(1)}, u32[]{:S(2)}, u32[]{:S(2)}) collective-permute-start(f32[256,256]{1,0:T(8,128)S(1)} %add.118), channel_id=1, source_target_pairs={{5,7},{13,15},{21,23},{29,31},{37,39},{45,47},{53,55},{61,63},{69,... | collective-permute-start | bytes 786440 | tf_op jit(solution)/shard_map/ppermute | solution.py:231
  29.0 77.9 %all-gather.2.cloned.1.call-start = ((), (), s32[]{:S(2)}) async-start(), calls=%async_computation.2 | async-start | bytes 1474560 | tf_op jit(solution)/shard_map/all_gather | solution.py:246
  29.0 2.1 %collective-permute-start.5 = (f32[256,256]{1,0:T(8,128)S(1)}, f32[256,256]{1,0:T(8,128)S(1)}, u32[]{:S(2)}, u32[]{:S(2)}) collective-permute-start(f32[256,256]{1,0:T(8,128)S(1)} %add.118), channel_id=1, source_target_pairs={{1,7},{9,15},{17,23},{25,31},{33,39},{41,47},{49,55},{57,63},{65,7... | collective-permute-start | bytes 786440 | tf_op jit(solution)/shard_map/ppermute | solution.py:231
  29.7 1.4 %collective-permute-start.4 = (f32[256,256]{1,0:T(8,128)S(1)}, f32[256,256]{1,0:T(8,128)}, u32[]{:S(2)}, u32[]{:S(2)}) collective-permute-start(f32[256,256]{1,0:T(8,128)S(1)} %add.118), channel_id=1, source_target_pairs={{3,7},{11,15},{19,23},{27,31},{35,39},{43,47},{51,55},{59,63},{67,... | collective-permute-start | bytes 786440 | tf_op jit(solution)/shard_map/ppermute | solution.py:231
  32.1 19.0 %collective-permute-start.9 = (f32[64,256]{1,0:T(8,128)S(1)}, f32[64,256]{1,0:T(8,128)S(1)}, u32[]{:S(2)}, u32[]{:S(2)}) collective-permute-start(f32[64,256]{1,0:T(8,128)S(1)} %get-tuple-element.45), channel_id=1, source_target_pairs={{0,96},{1,25},{2,98},{3,27},{4,100},{5,29},{6,102},{7,31},{8,104},... | collective-permute-start | bytes 196616 | tf_op jit(solution)/shard_map/ppermute | solution.py:36
  33.3 17.8 %collective-permute-start.8 = (f32[64,256]{1,0:T(8,128)S(1)}, f32[64,256]{1,0:T(8,128)S(1)}, u32[]{:S(2)}, u32[]{:S(2)}) collective-permute-start(f32[64,256]{1,0:T(8,128)S(1)} %get-tuple-element.46), channel_id=1, source_target_pairs={{0,32},{1,9},{2,34},{3,11},{4,36},{5,13},{6,38},{7,15},{8,40},{9,1... | collective-permute-start | bytes 196616 | tf_op jit(solution)/shard_map/ppermute | solution.py:36
  46.1 5.8 %collective-permute-start.7 = (f32[64,256]{1,0:T(8,128)S(1)}, f32[64,256]{1,0:T(8,128)S(1)}, u32[]{:S(2)}, u32[]{:S(2)}) collective-permute-start(f32[64,256]{1,0:T(8,128)S(1)} %get-tuple-element.44), channel_id=1, source_target_pairs={{0,64},{1,17},{2,66},{3,19},{4,68},{5,21},{6,70},{7,23},{8,72},{9,... | collective-permute-start | bytes 196616 | tf_op jit(solution)/shard_map/ppermute | solution.py:36
  51.9 26.5 %copy-start.3 = (f32[256,256]{1,0:T(8,128)S(1)}, f32[256,256]{1,0:T(8,128)}, u32[]{:S(2)}) copy-start(f32[256,256]{1,0:T(8,128)} %second_ref.1) | copy-start | bytes 786436
  51.9 26.9 %copy-start.4 = (f32[256,256]{1,0:T(8,128)S(1)}, f32[256,256]{1,0:T(8,128)}, u32[]{:S(2)}) copy-start(f32[256,256]{1,0:T(8,128)} %first_ref.1) | copy-start | bytes 786436
  51.9 15.8 %collective-permute-start.10 = (f32[896,256]{1,0:T(8,128)S(1)}, f32[896,256]{1,0:T(8,128)S(1)}, u32[]{:S(2)}, u32[]{:S(2)}) collective-permute-start(f32[896,256]{1,0:T(8,128)S(1)} %fusion.2), channel_id=1, source_target_pairs={{0,16},{1,65},{2,18},{3,67},{4,20},{5,69},{6,22},{7,71},{8,24},{9,... | collective-permute-start | bytes 2752520 | tf_op jit(solution)/shard_map/ppermute | solution.py:36
  56.3 21.9 %collective-permute-start.12 = (f32[896,256]{1,0:T(8,128)S(1)}, f32[896,256]{1,0:T(8,128)S(1)}, u32[]{:S(2)}, u32[]{:S(2)}) collective-permute-start(f32[896,256]{1,0:T(8,128)S(1)} %fusion.2), channel_id=1, source_target_pairs={{0,24},{1,97},{2,26},{3,99},{4,28},{5,101},{6,30},{7,103},{8,0},{9... | collective-permute-start | bytes 2752520 | tf_op jit(solution)/shard_map/ppermute | solution.py:36
  56.6 21.5 %collective-permute-start.11 = (f32[896,256]{1,0:T(8,128)S(1)}, f32[896,256]{1,0:T(8,128)S(1)}, u32[]{:S(2)}, u32[]{:S(2)}) collective-permute-start(f32[896,256]{1,0:T(8,128)S(1)} %fusion.2), channel_id=1, source_target_pairs={{0,8},{1,33},{2,10},{3,35},{4,12},{5,37},{6,14},{7,39},{8,16},{9,4... | collective-permute-start | bytes 2752520 | tf_op jit(solution)/shard_map/ppermute | solution.py:36
  79.3 15.1 %collective-permute-start.13 = (f32[896,256]{1,0:T(8,128)S(1)}, f32[896,256]{1,0:T(8,128)S(1)}, u32[]{:S(2)}, u32[]{:S(2)}) collective-permute-start(f32[896,256]{1,0:T(8,128)S(1)} %pad_maximum_fusion), channel_id=1, source_target_pairs={{0,64},{1,17},{2,66},{3,19},{4,68},{5,21},{6,70},{7,23},{8,72},{9,... | collective-permute-start | bytes 2752520 | tf_op jit(solution)/shard_map/ppermute | solution.py:36
  79.4 24.8 %collective-permute-start.14 = (f32[896,256]{1,0:T(8,128)S(1)}, f32[896,256]{1,0:T(8,128)}, u32[]{:S(2)}, u32[]{:S(2)}) collective-permute-start(f32[896,256]{1,0:T(8,128)S(1)} %pad_maximum_fusion), channel_id=1, source_target_pairs={{0,32},{1,9},{2,34},{3,11},{4,36},{5,13},{6,38},{7,15},{8,40},{9,1... | collective-permute-start | bytes 2752520 | tf_op jit(solution)/shard_map/ppermute | solution.py:36
  84.2 21.3 %collective-permute-start.15 = (f32[896,256]{1,0:T(8,128)S(1)}, f32[896,256]{1,0:T(8,128)}, u32[]{:S(2)}, u32[]{:S(2)}) collective-permute-start(f32[896,256]{1,0:T(8,128)S(1)} %pad_maximum_fusion), channel_id=1, source_target_pairs={{0,96},{1,25},{2,98},{3,27},{4,100},{5,29},{6,102},{7,31},{8,104},... | collective-permute-start | bytes 2752520 | tf_op jit(solution)/shard_map/ppermute | solution.py:36
  94.5 10.9 %copy-start = (f32[7,4,64,256]{3,2,1,0:T(8,128)}, f32[7,4,64,256]{3,2,1,0:T(8,128)S(1)}, u32[]{:S(2)}) copy-start(f32[7,4,64,256]{3,2,1,0:T(8,128)S(1)} %get-tuple-element.36) | copy-start | bytes 5505028
  94.5 11.1 %copy-start.1 = (f32[7,4,64,256]{3,2,1,0:T(8,128)}, f32[7,4,64,256]{3,2,1,0:T(8,128)S(1)}, u32[]{:S(2)}) copy-start(f32[7,4,64,256]{3,2,1,0:T(8,128)S(1)} %get-tuple-element.37) | copy-start | bytes 5505028
Sparse Core Ops, SparseCore 0:
  29.1 34.8 reduce-scatter.1
  78.6 26.9 all-gather.1

commit v4 on v3

v4 whole, which is shorter than its diff:
```python
import jax
import jax.numpy as jnp
from jax import lax
from jax.experimental import pallas as pl
from jax.experimental.pallas import tpu as pltpu
from jax.sharding import PartitionSpec as P

SIDE = 4
STEPS = (2, 1, 3)


def matmul(left, right):
    return jnp.dot(left, right, precision=lax.Precision.HIGH, preferred_element_type=jnp.float32)


def pairs(step, swap):
    out = []
    for y in range(SIDE):
        for z in range(SIDE):
            for x in range(SIDE):
                for core in range(2):
                    if core == swap:
                        to_y, to_z = (y + step) % SIDE, z
                    else:
                        to_y, to_z = y, (z + step) % SIDE
                    out.append(
                        (
                            (y * SIDE + z) * 2 * SIDE + 2 * x + core,
                            (to_y * SIDE + to_z) * 2 * SIDE + 2 * x + core,
                        )
                    )
    return out


def shift(value, step, swap):
    return lax.ppermute(value, ("row", "col"), pairs(step, swap))


def shift_x(value, step):
    pairs = [(2 * x + k, 2 * ((x + step) % SIDE) + k) for x in range(SIDE) for k in range(2)]
    return lax.ppermute(value, "col", pairs)


def swap_core(value):
    return lax.ppermute(value, "col", [(i, i ^ 1) for i in range(2 * SIDE)])


def block(value, index):
    return lax.dynamic_index_in_dim(value, index, 0, keepdims=False)


def split(value):
    high = value.astype(jnp.bfloat16)
    return high, (value - high.astype(jnp.float32)).astype(jnp.bfloat16)


def dot3(left, right):
    total = jnp.dot(left[0], right[1], preferred_element_type=jnp.float32)
    total += jnp.dot(left[1], right[0], preferred_element_type=jnp.float32)
    return total + jnp.dot(left[0], right[0], preferred_element_type=jnp.float32)


def tdot3(left, right):
    def product(a, b):
        return lax.dot_general(a, b, (((0,), (0,)), ((), ())), preferred_element_type=jnp.float32)

    return product(left[0], right[1]) + product(left[1], right[0]) + product(left[0], right[0])


def place_of(row, col):
    return jnp.where(lax.rem(col, 2) == 0, lax.div(row, SIDE), lax.rem(row, SIDE))


def pivot_kernel(window_hbm, rows_second_hbm, rows_first_hbm, *refs):
    outs, refs = refs[:SIDE], refs[SIDE:]
    window, rows, pivot, high, low, sem_rows, sem_window, sem_out = refs
    chunks, _, width = window.shape
    piece = width // SIDE
    halves = (slice(0, width), slice(width, 2 * width))

    ready = [
        pltpu.make_async_copy(source, rows.at[:, halves[i]], sem_rows.at[i])
        for i, source in enumerate((rows_second_hbm, rows_first_hbm))
    ]
    arriving = [
        pltpu.make_async_copy(
            window_hbm.at[:, pl.ds(j * width, width)], window.at[j], sem_window.at[j]
        )
        for j in range(chunks)
    ]
    for copy in ready + arriving:
        copy.start()
    place = place_of(lax.axis_index("row"), lax.axis_index("col"))
    leaving = []
    for copy in ready:
        copy.wait()
    high[...], low[...] = split(rows[...])
    for j in range(chunks):
        arriving[j].wait()
        pivot[j] = tdot3(split(window[j]), (high[...], low[...]))
        for step in range(SIDE):
            start = pl.multiple_of(lax.rem(place + step, SIDE) * piece, piece)
            for i in range(2):
                copy = pltpu.make_async_copy(
                    pivot.at[j, pl.ds(start, piece), halves[i]],
                    outs[step].at[pl.ds((i * chunks + j) * piece, piece)],
                    sem_out.at[j, i * SIDE + step],
                )
                copy.start()
                leaving.append(copy)
    for copy in leaving:
        copy.wait()


def pivot_products(window, rows_second, rows_first):
    tile_rows, tile_cols = window.shape
    width = rows_first.shape[1]
    chunks = tile_cols // width
    hbm = pl.BlockSpec(memory_space=pl.ANY)
    buffer = lambda *shape: pltpu.VMEM(shape, jnp.float32)
    return pl.pallas_call(
        pivot_kernel,
        in_specs=[hbm] * 3,
        out_specs=[hbm] * SIDE,
        out_shape=[jax.ShapeDtypeStruct((2 * tile_cols // SIDE, width), jnp.float32)] * SIDE,
        scratch_shapes=[
            buffer(chunks, tile_rows, width),
            buffer(tile_rows, 2 * width),
            buffer(chunks, width, 2 * width),
            pltpu.VMEM((tile_rows, 2 * width), jnp.bfloat16),
            pltpu.VMEM((tile_rows, 2 * width), jnp.bfloat16),
            pltpu.SemaphoreType.DMA((2,)),
            pltpu.SemaphoreType.DMA((chunks,)),
            pltpu.SemaphoreType.DMA((chunks, 2 * SIDE)),
        ],
        cost_estimate=pl.CostEstimate(
            flops=12 * tile_rows * tile_cols * width,
            bytes_accessed=4 * (tile_rows * tile_cols + 2 * tile_cols * width),
            transcendentals=0,
        ),
        name="pivot_products",
    )(window, rows_second, rows_first)


def left_kernel(
    window_hbm, cols_second_hbm, cols_first_hbm, rows_hbm, inverse_hbm, own_hbm, other_hbm,
    cross_hbm, window, cols, rows, inverse, left, cross, sem_in, sem_chunk, sem_out,
):
    chunks, tile_rows, width = window.shape
    halves = (slice(0, width), slice(width, 2 * width))
    arriving = []
    for j in range(chunks):
        at = pl.ds(j * width, width)
        arriving.append(
            [
                pltpu.make_async_copy(window_hbm.at[:, at], window.at[j], sem_chunk.at[j, 0]),
                pltpu.make_async_copy(
                    cols_second_hbm.at[at], cols.at[j, :, halves[0]], sem_chunk.at[j, 1]
                ),
                pltpu.make_async_copy(
                    cols_first_hbm.at[at], cols.at[j, :, halves[1]], sem_chunk.at[j, 2]
                ),
            ]
        )
    ready = [
        pltpu.make_async_copy(rows_hbm, rows, sem_in.at[0]),
        pltpu.make_async_copy(inverse_hbm, inverse, sem_in.at[1]),
    ]
    for copy in [copy for group in arriving for copy in group] + ready:
        copy.start()
    for j in range(chunks):
        for copy in arriving[j]:
            copy.wait()
        product = dot3(split(window[j]), split(cols[j]))
        if j == 0:
            left[...] = product
        else:
            left[...] += product
    half = tile_rows // 2
    core = lax.rem(lax.axis_index("col"), 2)
    leaving = [
        pltpu.make_async_copy(
            left.at[pl.ds(pl.multiple_of(place * half, half), half)], target, sem_out.at[i]
        )
        for i, (place, target) in enumerate(((core, own_hbm), (1 - core, other_hbm)))
    ]
    for copy in leaving:
        copy.start()
    for copy in ready:
        copy.wait()
    panel = dot3(split(left[:, halves[0]]), split(inverse[...]))
    cross[...] = tdot3(split(-panel), split(rows[...]))
    leaving.append(pltpu.make_async_copy(cross, cross_hbm, sem_out.at[2]))
    leaving[-1].start()
    for copy in leaving:
        copy.wait()


def left_products(window, cols_second, cols_first, rows, inverse):
    tile_rows, tile_cols = window.shape
    width = inverse.shape[0]
    chunks = tile_cols // width
    hbm = pl.BlockSpec(memory_space=pl.ANY)
    f32 = lambda *shape: jax.ShapeDtypeStruct(shape, jnp.float32)
    buffer = lambda *shape: pltpu.VMEM(shape, jnp.float32)
    return pl.pallas_call(
        left_kernel,
        in_specs=[hbm] * 5,
        out_specs=[hbm] * 3,
        out_shape=[f32(tile_rows // 2, 2 * width)] * 2 + [f32(width, width)],
        scratch_shapes=[
            buffer(chunks, tile_rows, width),
            buffer(chunks, width, 2 * width),
            buffer(tile_rows, width),
            buffer(width, width),
            buffer(tile_rows, 2 * width),
            buffer(width, width),
            pltpu.SemaphoreType.DMA((2,)),
            pltpu.SemaphoreType.DMA((chunks, 3)),
            pltpu.SemaphoreType.DMA((3,)),
        ],
        cost_estimate=pl.CostEstimate(
            flops=12 * tile_rows * tile_cols * width,
            bytes_accessed=4 * (tile_rows * tile_cols + 2 * tile_cols * width),
            transcendentals=0,
        ),
        name="left_products",
    )(window, cols_second, cols_first, rows, inverse)


def after(value, *others):
    return lax.optimization_barrier((value,) + others)[0]


def local(
    grad_window, rows_first, cols_first, rows_second, cols_second, inverse_first, inverse_second
):
    row = lax.axis_index("row")
    col = lax.axis_index("col")
    last = 2 * SIDE - 1
    is_last = col == last
    tile_cols = grad_window.shape[1]
    width = inverse_first.shape[0]
    chunks, piece = tile_cols // width, width // SIDE
    place = place_of(row, col)

    far_place = place_of(row, col + 1)
    x, core = col // 2, col % 2

    own_left, other_left, cross = left_products(
        grad_window, cols_second, cols_first, rows_first, inverse_second
    )
    blocks = pivot_products(after(grad_window, cross), rows_second, rows_first)
    left = own_left + swap_core(other_left)

    cross = cross + lax.ppermute(cross, "col", [(2 * i, 2 * i + 1) for i in range(SIDE)])
    others = [lax.ppermute(cross, "col", [(source, last)]) for source in (3, 1, 5)]
    cross = jnp.where(is_last, cross + others[0] + others[1] + others[2], 0.0)
    late = cross.reshape(SIDE, piece, width)
    late = [block(late, (place + step) % SIDE) for step in range(SIDE)]

    def arrivals(values, swap):
        return [shift(values[step], step, swap) for step in STEPS]

    tail = cols_first[tile_cols - width :]
    held = jnp.where(is_last, tail, 0.0)
    for target in (1, 5, 3):
        held = held + lax.ppermute(after(tail, late[1]), "col", [(last, target)])

    tail = lax.ppermute(held, "col", [(2 * i + 1, 2 * i) for i in range(SIDE)])
    tail = jnp.where(core == 1, held, tail)
    left = after(left, late[1]).reshape(SIDE, -1, 2 * width)
    got_left = [shift_x(block(left, (x + step) % SIDE), step) for step in STEPS]
    left = block(left, x) + got_left[0] + got_left[1] + got_left[2]
    panel_second = matmul(-left[:, :width], inverse_second)
    panel_first = matmul(-(left[:, width:] + matmul(panel_second, tail)), inverse_first)
    panel = jnp.concatenate([panel_second, panel_first], 1)

    got = arrivals(blocks, 0)
    got_late = arrivals(late, 0)
    value = blocks[0] + got[0] + got[1] + got[2]
    late = late[0] + got_late[0] + got_late[1] + got_late[2]
    value = value.at[value.shape[0] - piece :].add(late)

    half = value.shape[0] // 2
    quarters = value.reshape(SIDE, half // 2, width)
    got = arrivals([block(quarters, (far_place + step) % SIDE) for step in range(SIDE)], 1)
    quarter = block(quarters, far_place) + got[0] + got[1] + got[2]
    inverse = jnp.where(far_place < SIDE // 2, inverse_second, inverse_first)
    quarter = matmul(-quarter, inverse)

    got = arrivals([quarter] * SIDE, 1)
    value = jnp.zeros((SIDE,) + quarter.shape, jnp.float32)
    for part, step in [(quarter, 0)] + list(zip(got, STEPS)):
        value = lax.dynamic_update_index_in_dim(value, part, (far_place - step) % SIDE, 0)
    value = value.reshape(2 * half, width)

    got = arrivals([value] * SIDE, 0)
    panel = after(panel, got[0])
    panels = jnp.zeros((SIDE,) + panel.shape, jnp.float32)
    for part, step in [(panel, 0)] + [(shift_x(panel, step), step) for step in STEPS]:
        panels = lax.dynamic_update_index_in_dim(panels, part, (x - step) % SIDE, 0)
    panels = panels.reshape(-1, 2 * width)
    both = jnp.zeros((2,) + panels.shape, jnp.float32)
    both = lax.dynamic_update_index_in_dim(both, panels, core, 0)
    both = lax.dynamic_update_index_in_dim(both, swap_core(panels), 1 - core, 0)
    both = both.reshape(-1, 2 * width)
    panel_second, panel_first = both[:, :width], both[:, width:]
    pivots = [jnp.zeros((chunks, SIDE, piece, width), jnp.float32)] * 2
    parts = [(value, 0)] + list(zip(got, STEPS))
    for i, (part, step) in enumerate(parts):
        if i == 1:
            pivots = after(pivots, panel_second, panel_first)
        pivots = [
            lax.dynamic_update_index_in_dim(
                pivot, rows.reshape(chunks, piece, width), (place - step) % SIDE, 1
            )
            for pivot, rows in zip(pivots, (part[:half], part[half:]))
        ]
    pivot_second, pivot_first = (pivot.reshape(tile_cols, width) for pivot in pivots)
    return (panel_second, pivot_second, panel_first, pivot_first)


def solution(mesh):
    in_specs = (
        P("row", "col"),
        P("row", None),
        P("col", None),
        P("row", None),
        P("col", None),
        P(),
        P(),
    )
    out_specs = (P("row", None), P("col", None), P("row", None), P("col", None))
    return jax.shard_map(local, mesh=mesh, in_specs=in_specs, out_specs=out_specs, check_vma=False)
```

time: 121 us -> 110 us (0.909)
  starting transfers between devices: 23.3 us -> 51.4 us
  waiting for transfers between devices: 55.6 us -> 29.8 us
  between operations: 14.3 us -> 1.33 us
  Pallas kernels: 16.3 us -> 14.5 us
    ppermute x12 -> x15, waiting for transfers between devices: 55.5 us -> 18.7 us  [shift(): return lax.ppermute(value, ('row', 'col'), pairs(step, swap))]
    ppermute x0 -> x12, starting transfers between devices: none -> 17.1 us  [the longest x6 13.7 us: shift_x(): return lax.ppermute(value, 'col', pairs)]
    ppermute x12 -> x15, starting transfers between devices: 19.2 us -> 30.1 us  [shift(): return lax.ppermute(value, ('row', 'col'), pairs(step, swap))]
    ppermute x0 -> x12, waiting for transfers between devices: none -> 9.81 us  [the longest x6 8.32 us: shift_x(): return lax.ppermute(value, 'col', pairs)]
    dynamic_update_slice x7, local copies, waits for them, and re-layouts: 3.38 us -> 0.33 us  [local(): lax.dynamic_update_index_in_dim(pivot, rows.reshape(chunks, piece, width)...]
    slice x3 -> x4, local copies, waits for them, and re-layouts: 2.49 us -> 0.24 us  [local(): part[half:]]
    slice x0 -> x2, local copies, waits for them, and re-layouts: none -> 2.01 us  [the longest x1 1.05 us: local(): panel_second, panel_first = (both[:, :width], both[:, width:])]
    pallas_call x2, Pallas kernels: 16.3 us -> 14.5 us  [the longest x1 7.95 us: pivot_products(): pl.pallas_call(pivot_kernel, in_specs=[hbm] * 3, out_specs=[hbm] * SIDE,...]
  transfers between devices with their start and end apart: 18 -> 31, of which waited for: 8 -> 15; matrix products, arithmetic and copies ran while one was open for 6% -> 8% of each run, Pallas kernels for 0% -> 7%
where the time goes in v4:
time: 110 us; the launch traced here: 109 us
  starting transfers between devices  51.4 us (47%)
  waiting for transfers between devices  29.8 us (27%)
  Pallas kernels  14.5 us (13%)
  local copies, waits for them, and re-layouts  5.96 us (5%)
  other arithmetic  4.88 us (4%)
  between operations  1.33 us (1%)
    ppermute x15, starting transfers between devices, shift(): return lax.ppermute(value, ('row', 'col'), pairs(step, swap))  30.1 us
    ppermute x15, waiting for transfers between devices, shift(): return lax.ppermute(value, ('row', 'col'), pairs(step, swap))  18.7 us
    ppermute x6, starting transfers between devices, shift_x(): return lax.ppermute(value, 'col', pairs)  13.7 us
    ppermute x6, waiting for transfers between devices, shift_x(): return lax.ppermute(value, 'col', pairs)  8.32 us
    pallas_call x1, Pallas kernels, pivot_products(): pl.pallas_call(pivot_kernel, in_specs=[hbm] * 3, out_specs=[hbm] * SIDE,...  7.95 us
    pallas_call x1, Pallas kernels, left_products(): pl.pallas_call(left_kernel, in_specs=[hbm] * 5, out_specs=[hbm] * 3, out_...  6.57 us
    ppermute x3, starting transfers between devices, local(): lax.ppermute(cross, 'col', [(source, last)])  2.86 us
  transfers between devices with their start and end apart: 31, of which 15 were waited for; matrix products, arithmetic and copies ran while one was open for 8% of the time, Pallas kernels for 7%

profile of v4, /device:TPU:0, one launch (start us, length us, event | category | flops | bytes accessed | tf_op | source)
XLA Modules:
  0.0 108.8 jit_solution(11614122817870018107)
XLA Ops:
  0.6 6.6 %left_products.1 = (f32[256,512]{1,0:T(8,128)}, f32[256,512]{1,0:T(8,128)}, f32[256,256]{1,0:T(8,128)}) custom-call(f32[512,1792]{1,0:T(8,128)} %window_hbm.2, f32[1792,256]{1,0:T(8,128)} %cols_second_hbm.1, f32[1792,256]{1,0:T(8,128)} %cols_first_hbm.1, f32[512,256]{1,0:T(8,128)} %rows_first_hbm.1, f32[256,256]{1,0:T(8,128)} %inverse_hbm.1), custom_call_target="tpu_custom_call" | custom-call | flops 2818572288 | bytes 7340032 | tf_op jit(solution)/shard_map/left_products/pallas_call | solution.py:206
  7.2 1.3 %collective-permute-start.1 = (f32[256,256]{1,0:T(8,128)}, f32[256,256]{1,0:T(8,128)S(1)}, u32[]{:S(2)}, u32[]{:S(2)}) collective-permute-start(f32[256,256]{1,0:T(8,128)} %get-tuple-element.31), channel_id=1, source_target_pairs={{0,1},{2,3},{4,5},{6,7},{8,9},{10,11},{12,13},{14,15},{16,17},{18,... | collective-permute-start | bytes 786440 | tf_op jit(solution)/shard_map/ppermute | solution.py:256
  8.6 1.2 %collective-permute-done.1 = f32[256,256]{1,0:T(8,128)S(1)} collective-permute-done((f32[256,256]{1,0:T(8,128)}, f32[256,256]{1,0:T(8,128)S(1)}, u32[]{:S(2)}, u32[]{:S(2)}) %collective-permute-start.1) | collective-permute-done | bytes 262176 | tf_op jit(solution)/shard_map/ppermute | solution.py:256
  9.9 1.0 add.271
  10.9 0.8 collective-permute-start.2
  11.7 0.7 collective-permute-start.3
  12.4 1.4 %collective-permute-start.4 = (f32[256,256]{1,0:T(8,128)S(1)}, f32[256,256]{1,0:T(8,128)}, u32[]{:S(2)}, u32[]{:S(2)}) collective-permute-start(f32[256,256]{1,0:T(8,128)S(1)} %add.271), channel_id=1, source_target_pairs={{5,7},{13,15},{21,23},{29,31},{37,39},{45,47},{53,55},{61,63},{69,... | collective-permute-start | bytes 786440 | tf_op jit(solution)/shard_map/ppermute | solution.py:257
  13.7 8.0 %pivot_products.1 = (f32[896,256]{1,0:T(8,128)}, f32[896,256]{1,0:T(8,128)}, f32[896,256]{1,0:T(8,128)}, f32[896,256]{1,0:T(8,128)}) custom-call(f32[512,1792]{1,0:T(8,128)} %window_hbm.2, f32[512,256]{1,0:T(8,128)} %rows_second_hbm.1, f32[512,256]{1,0:T(8,128)} %rows_first_hbm.1), custom_call_target="tpu_custom_call" | custom-call | flops 2818572288 | bytes 7340032 | tf_op jit(solution)/shard_map/pivot_products/pallas_call | solution.py:121
  21.7 3.8 %collective-permute-start.12 = (f32[896,256]{1,0:T(8,128)}, f32[896,256]{1,0:T(8,128)S(1)}, u32[]{:S(2)}, u32[]{:S(2)}) collective-permute-start(f32[896,256]{1,0:T(8,128)} %get-tuple-element.36), channel_id=1, source_target_pairs={{0,64},{1,17},{2,66},{3,19},{4,68},{5,21},{6,70},{7,23},{8,72},{9,... | collective-permute-start | bytes 2752520 | tf_op jit(solution)/shard_map/ppermute | solution.py:36
  25.5 0.7 collective-permute-start.13
  26.3 2.6 %collective-permute-start.14 = (f32[896,256]{1,0:T(8,128)}, f32[896,256]{1,0:T(8,128)}, u32[]{:S(2)}, u32[]{:S(2)}) collective-permute-start(f32[896,256]{1,0:T(8,128)} %get-tuple-element.38), channel_id=1, source_target_pairs={{0,96},{1,25},{2,98},{3,27},{4,100},{5,29},{6,102},{7,31},{8,104},... | collective-permute-start | bytes 2752520 | tf_op jit(solution)/shard_map/ppermute | solution.py:36
  28.9 1.0 add_select_fusion
  29.9 0.7 dynamic-slice_bitcast_fusion.7
  30.7 3.1 %collective-permute-start.5 = (f32[64,512]{1,0:T(8,128)S(1)}, f32[64,512]{1,0:T(8,128)S(1)}, u32[]{:S(2)}, u32[]{:S(2)}) collective-permute-start(f32[64,512]{1,0:T(8,128)S(1)} %get-tuple-element.55), channel_id=1, source_target_pairs={{0,4},{1,5},{2,6},{3,7},{4,0},{5,1},{6,2},{7,3},{8,12},{9,13},{10,... | collective-permute-start | bytes 393224 | tf_op jit(solution)/shard_map/ppermute | solution.py:41
  34.4 2.9 %collective-permute-done.5 = f32[64,512]{1,0:T(8,128)S(1)} collective-permute-done((f32[64,512]{1,0:T(8,128)S(1)}, f32[64,512]{1,0:T(8,128)S(1)}, u32[]{:S(2)}, u32[]{:S(2)}) %collective-permute-start.5) | collective-permute-done | bytes 131104 | tf_op jit(solution)/shard_map/ppermute | solution.py:41
  37.2 3.7 %collective-permute-start.7 = (f32[64,512]{1,0:T(8,128)S(1)}, f32[64,512]{1,0:T(8,128)S(1)}, u32[]{:S(2)}, u32[]{:S(2)}) collective-permute-start(f32[64,512]{1,0:T(8,128)S(1)} %get-tuple-element.56), channel_id=1, source_target_pairs={{0,6},{1,7},{2,0},{3,1},{4,2},{5,3},{6,4},{7,5},{8,14},{9,15},{10,... | collective-permute-start | bytes 393224 | tf_op jit(solution)/shard_map/ppermute | solution.py:41
  40.9 1.0 slice.62
  42.2 1.9 %collective-permute-done.7 = f32[64,512]{1,0:T(8,128)S(1)} collective-permute-done((f32[64,512]{1,0:T(8,128)S(1)}, f32[64,512]{1,0:T(8,128)S(1)}, u32[]{:S(2)}, u32[]{:S(2)}) %collective-permute-start.7) | collective-permute-done | bytes 131104 | tf_op jit(solution)/shard_map/ppermute | solution.py:41
  44.1 0.7 collective-permute-start.10
  44.8 0.7 collective-permute-start.8
  45.5 1.5 %collective-permute-done.13 = f32[896,256]{1,0:T(8,128)} collective-permute-done((f32[896,256]{1,0:T(8,128)}, f32[896,256]{1,0:T(8,128)}, u32[]{:S(2)}, u32[]{:S(2)}) %collective-permute-start.13) | collective-permute-done | bytes 917536 | tf_op jit(solution)/shard_map/ppermute | solution.py:36
  47.0 2.7 %collective-permute-start.15 = (f32[64,256]{1,0:T(8,128)}, f32[64,256]{1,0:T(8,128)S(1)}, u32[]{:S(2)}, u32[]{:S(2)}) collective-permute-start(f32[64,256]{1,0:T(8,128)} %get-tuple-element.58), channel_id=1, source_target_pairs={{0,64},{1,17},{2,66},{3,19},{4,68},{5,21},{6,70},{7,23},{8,72},{9,... | collective-permute-start | bytes 196616 | tf_op jit(solution)/shard_map/ppermute | solution.py:36
  49.8 2.0 %collective-permute-start.17 = (f32[64,256]{1,0:T(8,128)}, f32[64,256]{1,0:T(8,128)S(1)}, u32[]{:S(2)}, u32[]{:S(2)}) collective-permute-start(f32[64,256]{1,0:T(8,128)} %get-tuple-element.59), channel_id=1, source_target_pairs={{0,96},{1,25},{2,98},{3,27},{4,100},{5,29},{6,102},{7,31},{8,104},... | collective-permute-start | bytes 196616 | tf_op jit(solution)/shard_map/ppermute | solution.py:36
  51.8 1.7 %add_add_fusion = f32[896,256]{1,0:T(8,128)S(1)} fusion(f32[896,256]{1,0:T(8,128)} %collective-permute-done.14, f32[896,256]{1,0:T(8,128)} %collective-permute-done.13, f32[896,256]{1,0:T(8,128)S(1)} %copy-done.4, f32[896,256]{1,0:T(8,128)S(1)} %collective-permute-done.12), kind=kLoop, calls=%fused_computation | loop fusion | flops 688128 | bytes 4587520 | tf_op jit(solution)/shard_map/add | solution.py:281
  53.5 0.7 collective-permute-done.17
  54.3 4.0 %collective-permute-start.18 = (f32[224,256]{1,0:T(8,128)S(1)}, f32[224,256]{1,0:T(8,128)S(1)}, u32[]{:S(2)}, u32[]{:S(2)}) collective-permute-start(f32[224,256]{1,0:T(8,128)S(1)} %get-tuple-element.52), channel_id=1, source_target_pairs={{0,16},{1,65},{2,18},{3,67},{4,20},{5,69},{6,22},{7,71},{8,24},{9,... | collective-permute-start | bytes 688136 | tf_op jit(solution)/shard_map/ppermute | solution.py:36
  58.3 1.0 collective-permute-start.19
  59.3 2.2 %collective-permute-start.20 = (f32[224,256]{1,0:T(8,128)S(1)}, f32[224,256]{1,0:T(8,128)S(1)}, u32[]{:S(2)}, u32[]{:S(2)}) collective-permute-start(f32[224,256]{1,0:T(8,128)S(1)} %get-tuple-element.53), channel_id=1, source_target_pairs={{0,24},{1,97},{2,26},{3,99},{4,28},{5,101},{6,30},{7,103},{8,0},{9... | collective-permute-start | bytes 688136 | tf_op jit(solution)/shard_map/ppermute | solution.py:36
  62.3 0.7 collective-permute-start.9
  63.0 2.6 %collective-permute-done.19 = f32[224,256]{1,0:T(8,128)S(1)} collective-permute-done((f32[224,256]{1,0:T(8,128)S(1)}, f32[224,256]{1,0:T(8,128)S(1)}, u32[]{:S(2)}, u32[]{:S(2)}) %collective-permute-start.19) | collective-permute-done | bytes 229408 | tf_op jit(solution)/shard_map/ppermute | solution.py:36
  66.1 2.2 %collective-permute-start.21 = (f32[224,256]{1,0:T(8,128)S(1)}, f32[224,256]{1,0:T(8,128)S(1)}, u32[]{:S(2)}, u32[]{:S(2)}) collective-permute-start(f32[224,256]{1,0:T(8,128)S(1)} %get-tuple-element.62), channel_id=1, source_target_pairs={{0,16},{1,65},{2,18},{3,67},{4,20},{5,69},{6,22},{7,71},{8,24},{9,... | collective-permute-start | bytes 688136 | tf_op jit(solution)/shard_map/ppermute | solution.py:36
  68.3 1.0 add_add_fusion.1
  69.3 1.3 %collective-permute-start.11 = (f32[256,256]{1,0:T(8,128)S(1)}, f32[256,256]{1,0:T(8,128)S(1)}, u32[]{:S(2)}, u32[]{:S(2)}) collective-permute-start(f32[256,256]{1,0:T(8,128)S(1)} %add_add_fusion.1), channel_id=1, source_target_pairs={{1,0},{3,2},{5,4},{7,6},{9,8},{11,10},{13,12},{15,14},{17,16},{19,... | collective-permute-start | bytes 786440 | tf_op jit(solution)/shard_map/ppermute | solution.py:270
  70.6 1.9 %collective-permute-start.22 = (f32[224,256]{1,0:T(8,128)S(1)}, f32[224,256]{1,0:T(8,128)S(1)}, u32[]{:S(2)}, u32[]{:S(2)}) collective-permute-start(f32[224,256]{1,0:T(8,128)S(1)} %get-tuple-element.62), channel_id=1, source_target_pairs={{0,8},{1,33},{2,10},{3,35},{4,12},{5,37},{6,14},{7,39},{8,16},{9,4... | collective-permute-start | bytes 688136 | tf_op jit(solution)/shard_map/ppermute | solution.py:36
  72.5 1.5 %collective-permute-start.23 = (f32[224,256]{1,0:T(8,128)S(1)}, f32[224,256]{1,0:T(8,128)S(1)}, u32[]{:S(2)}, u32[]{:S(2)}) collective-permute-start(f32[224,256]{1,0:T(8,128)S(1)} %get-tuple-element.62), channel_id=1, source_target_pairs={{0,24},{1,97},{2,26},{3,99},{4,28},{5,101},{6,30},{7,103},{8,0},{9... | collective-permute-start | bytes 688136 | tf_op jit(solution)/shard_map/ppermute | solution.py:36
  74.0 4.0 %collective-permute-done.22 = f32[224,256]{1,0:T(8,128)S(1)} collective-permute-done((f32[224,256]{1,0:T(8,128)S(1)}, f32[224,256]{1,0:T(8,128)S(1)}, u32[]{:S(2)}, u32[]{:S(2)}) %collective-permute-start.22) | collective-permute-done | bytes 229408 | tf_op jit(solution)/shard_map/ppermute | solution.py:36
  78.5 2.2 %collective-permute-start.24 = (f32[896,256]{1,0:T(8,128)S(1)}, f32[896,256]{1,0:T(8,128)S(1)}, u32[]{:S(2)}, u32[]{:S(2)}) collective-permute-start(f32[896,256]{1,0:T(8,128)S(1)} %bitcast.86), channel_id=1, source_target_pairs={{0,64},{1,17},{2,66},{3,19},{4,68},{5,21},{6,70},{7,23},{8,72},{9,... | collective-permute-start | bytes 2752520 | tf_op jit(solution)/shard_map/ppermute | solution.py:36
  81.2 2.0 %collective-permute-start.29 = (f32[896,256]{1,0:T(8,128)S(1)}, f32[896,256]{1,0:T(8,128)S(1)}, u32[]{:S(2)}, u32[]{:S(2)}) collective-permute-start(f32[896,256]{1,0:T(8,128)S(1)} %bitcast.87), channel_id=1, source_target_pairs={{0,32},{1,9},{2,34},{3,11},{4,36},{5,13},{6,38},{7,15},{8,40},{9,1... | collective-permute-start | bytes 2752520 | tf_op jit(solution)/shard_map/ppermute | solution.py:36
  83.2 1.3 %collective-permute-start.30 = (f32[896,256]{1,0:T(8,128)S(1)}, f32[896,256]{1,0:T(8,128)S(1)}, u32[]{:S(2)}, u32[]{:S(2)}) collective-permute-start(f32[896,256]{1,0:T(8,128)S(1)} %bitcast.88), channel_id=1, source_target_pairs={{0,96},{1,25},{2,98},{3,27},{4,100},{5,29},{6,102},{7,31},{8,104},... | collective-permute-start | bytes 2752520 | tf_op jit(solution)/shard_map/ppermute | solution.py:36
  85.1 8.5 %collective-permute-done.24 = f32[896,256]{1,0:T(8,128)S(1)} collective-permute-done((f32[896,256]{1,0:T(8,128)S(1)}, f32[896,256]{1,0:T(8,128)S(1)}, u32[]{:S(2)}, u32[]{:S(2)}) %collective-permute-start.24) | collective-permute-done | bytes 917536 | tf_op jit(solution)/shard_map/ppermute | solution.py:36
  93.6 3.0 %collective-permute-start.25 = (f32[64,512]{1,0:T(8,128)S(1)}, f32[64,512]{1,0:T(8,128)S(1)}, u32[]{:S(2)}, u32[]{:S(2)}) collective-permute-start(f32[64,512]{1,0:T(8,128)S(1)} %pad_maximum_fusion), channel_id=1, source_target_pairs={{0,4},{1,5},{2,6},{3,7},{4,0},{5,1},{6,2},{7,3},{8,12},{9,13},{10,... | collective-permute-start | bytes 393224 | tf_op jit(solution)/shard_map/ppermute | solution.py:41
  97.2 2.6 %collective-permute-start.27 = (f32[64,512]{1,0:T(8,128)S(1)}, f32[64,512]{1,0:T(8,128)S(1)}, u32[]{:S(2)}, u32[]{:S(2)}) collective-permute-start(f32[64,512]{1,0:T(8,128)S(1)} %pad_maximum_fusion), channel_id=1, source_target_pairs={{0,6},{1,7},{2,0},{3,1},{4,2},{5,3},{6,4},{7,5},{8,14},{9,15},{10,... | collective-permute-start | bytes 393224 | tf_op jit(solution)/shard_map/ppermute | solution.py:41
  100.0 1.5 %collective-permute-done.25 = f32[64,512]{1,0:T(8,128)S(1)} collective-permute-done((f32[64,512]{1,0:T(8,128)S(1)}, f32[64,512]{1,0:T(8,128)S(1)}, u32[]{:S(2)}, u32[]{:S(2)}) %collective-permute-start.25) | collective-permute-done | bytes 131104 | tf_op jit(solution)/shard_map/ppermute | solution.py:41
  101.6 2.0 %collective-permute-done.26 = f32[64,512]{1,0:T(8,128)S(1)} collective-permute-done((f32[64,512]{1,0:T(8,128)S(1)}, f32[64,512]{1,0:T(8,128)S(1)}, u32[]{:S(2)}, u32[]{:S(2)}) %collective-permute-start.26) | collective-permute-done | bytes 131104 | tf_op jit(solution)/shard_map/ppermute | solution.py:41
  104.2 1.5 %collective-permute-done.28 = f32[256,512]{1,0:T(8,128)S(1)} collective-permute-done((f32[256,512]{1,0:T(8,128)S(1)}, f32[256,512]{1,0:T(8,128)S(1)}, u32[]{:S(2)}, u32[]{:S(2)}) %collective-permute-start.28) | collective-permute-done | bytes 524320 | tf_op jit(solution)/shard_map/ppermute | solution.py:45
  105.7 1.0 fusion.21
  107.0 1.2 %copy-done.1 = f32[7,4,64,256]{3,2,1,0:T(8,128)} copy-done((f32[7,4,64,256]{3,2,1,0:T(8,128)}, f32[7,4,64,256]{3,2,1,0:T(8,128)S(1)}, u32[]{:S(2)}) %copy-start.1) | copy-done | bytes 1835032
  108.2 0.6 copy-done
  (70 shorter events, 5.5 us)
Async XLA Ops:
  7.2 2.7 %collective-permute-start.1 = (f32[256,256]{1,0:T(8,128)}, f32[256,256]{1,0:T(8,128)S(1)}, u32[]{:S(2)}, u32[]{:S(2)}) collective-permute-start(f32[256,256]{1,0:T(8,128)} %get-tuple-element.31), channel_id=1, source_target_pairs={{0,1},{2,3},{4,5},{6,7},{8,9},{10,11},{12,13},{14,15},{16,17},{18,... | collective-permute-start | bytes 786440 | tf_op jit(solution)/shard_map/ppermute | solution.py:256
  8.5 17.0 %collective-permute-start = (f32[256,512]{1,0:T(8,128)}, f32[256,512]{1,0:T(8,128)S(1)}, u32[]{:S(2)}, u32[]{:S(2)}) collective-permute-start(f32[256,512]{1,0:T(8,128)} %get-tuple-element.30), channel_id=1, source_target_pairs={{0,1},{1,0},{2,3},{3,2},{4,5},{5,4},{6,7},{7,6},{8,9},{9,8},{10,11... | collective-permute-start | bytes 1572872 | tf_op jit(solution)/shard_map/ppermute | solution.py:45
  10.8 15.3 %copy-start.5 = (f32[256,512]{1,0:T(8,128)S(1)}, f32[256,512]{1,0:T(8,128)}, u32[]{:S(2)}) copy-start(f32[256,512]{1,0:T(8,128)} %get-tuple-element.29) | copy-start | bytes 1572868
  10.9 15.4 %collective-permute-start.2 = (f32[256,256]{1,0:T(8,128)S(1)}, f32[256,256]{1,0:T(8,128)S(1)}, u32[]{:S(2)}, u32[]{:S(2)}) collective-permute-start(f32[256,256]{1,0:T(8,128)S(1)} %add.271), channel_id=1, source_target_pairs={{3,7},{11,15},{19,23},{27,31},{35,39},{43,47},{51,55},{59,63},{67,... | collective-permute-start | bytes 786440 | tf_op jit(solution)/shard_map/ppermute | solution.py:257
  11.7 17.2 %collective-permute-start.3 = (f32[256,256]{1,0:T(8,128)S(1)}, f32[256,256]{1,0:T(8,128)S(1)}, u32[]{:S(2)}, u32[]{:S(2)}) collective-permute-start(f32[256,256]{1,0:T(8,128)S(1)} %add.271), channel_id=1, source_target_pairs={{1,7},{9,15},{17,23},{25,31},{33,39},{41,47},{49,55},{57,63},{65,7... | collective-permute-start | bytes 786440 | tf_op jit(solution)/shard_map/ppermute | solution.py:257
  12.4 16.6 %collective-permute-start.4 = (f32[256,256]{1,0:T(8,128)S(1)}, f32[256,256]{1,0:T(8,128)}, u32[]{:S(2)}, u32[]{:S(2)}) collective-permute-start(f32[256,256]{1,0:T(8,128)S(1)} %add.271), channel_id=1, source_target_pairs={{5,7},{13,15},{21,23},{29,31},{37,39},{45,47},{53,55},{61,63},{69,... | collective-permute-start | bytes 786440 | tf_op jit(solution)/shard_map/ppermute | solution.py:257
  21.7 23.1 %collective-permute-start.12 = (f32[896,256]{1,0:T(8,128)}, f32[896,256]{1,0:T(8,128)S(1)}, u32[]{:S(2)}, u32[]{:S(2)}) collective-permute-start(f32[896,256]{1,0:T(8,128)} %get-tuple-element.36), channel_id=1, source_target_pairs={{0,64},{1,17},{2,66},{3,19},{4,68},{5,21},{6,70},{7,23},{8,72},{9,... | collective-permute-start | bytes 2752520 | tf_op jit(solution)/shard_map/ppermute | solution.py:36
  25.5 21.5 %collective-permute-start.13 = (f32[896,256]{1,0:T(8,128)}, f32[896,256]{1,0:T(8,128)}, u32[]{:S(2)}, u32[]{:S(2)}) collective-permute-start(f32[896,256]{1,0:T(8,128)} %get-tuple-element.37), channel_id=1, source_target_pairs={{0,32},{1,9},{2,34},{3,11},{4,36},{5,13},{6,38},{7,15},{8,40},{9,1... | collective-permute-start | bytes 2752520 | tf_op jit(solution)/shard_map/ppermute | solution.py:36
  26.3 25.5 %copy-start.4 = (f32[896,256]{1,0:T(8,128)S(1)}, f32[896,256]{1,0:T(8,128)}, u32[]{:S(2)}) copy-start(f32[896,256]{1,0:T(8,128)} %get-tuple-element.35) | copy-start | bytes 2752516
  26.3 23.5 %collective-permute-start.14 = (f32[896,256]{1,0:T(8,128)}, f32[896,256]{1,0:T(8,128)}, u32[]{:S(2)}, u32[]{:S(2)}) collective-permute-start(f32[896,256]{1,0:T(8,128)} %get-tuple-element.38), channel_id=1, source_target_pairs={{0,96},{1,25},{2,98},{3,27},{4,100},{5,29},{6,102},{7,31},{8,104},... | collective-permute-start | bytes 2752520 | tf_op jit(solution)/shard_map/ppermute | solution.py:36
  30.7 6.6 %collective-permute-start.5 = (f32[64,512]{1,0:T(8,128)S(1)}, f32[64,512]{1,0:T(8,128)S(1)}, u32[]{:S(2)}, u32[]{:S(2)}) collective-permute-start(f32[64,512]{1,0:T(8,128)S(1)} %get-tuple-element.55), channel_id=1, source_target_pairs={{0,4},{1,5},{2,6},{3,7},{4,0},{5,1},{6,2},{7,3},{8,12},{9,13},{10,... | collective-permute-start | bytes 393224 | tf_op jit(solution)/shard_map/ppermute | solution.py:41
  33.8 8.4 %collective-permute-start.6 = (f32[64,512]{1,0:T(8,128)S(1)}, f32[64,512]{1,0:T(8,128)S(1)}, u32[]{:S(2)}, u32[]{:S(2)}) collective-permute-start(f32[64,512]{1,0:T(8,128)S(1)} %get-tuple-element.57), channel_id=1, source_target_pairs={{0,2},{1,3},{2,4},{3,5},{4,6},{5,7},{6,0},{7,1},{8,10},{9,11},{10,... | collective-permute-start | bytes 393224 | tf_op jit(solution)/shard_map/ppermute | solution.py:41
  37.2 6.9 %collective-permute-start.7 = (f32[64,512]{1,0:T(8,128)S(1)}, f32[64,512]{1,0:T(8,128)S(1)}, u32[]{:S(2)}, u32[]{:S(2)}) collective-permute-start(f32[64,512]{1,0:T(8,128)S(1)} %get-tuple-element.56), channel_id=1, source_target_pairs={{0,6},{1,7},{2,0},{3,1},{4,2},{5,3},{6,4},{7,5},{8,14},{9,15},{10,... | collective-permute-start | bytes 393224 | tf_op jit(solution)/shard_map/ppermute | solution.py:41
  42.1 11.4 %collective-permute-start.16 = (f32[64,256]{1,0:T(8,128)}, f32[64,256]{1,0:T(8,128)S(1)}, u32[]{:S(2)}, u32[]{:S(2)}) collective-permute-start(f32[64,256]{1,0:T(8,128)} %get-tuple-element.60), channel_id=1, source_target_pairs={{0,32},{1,9},{2,34},{3,11},{4,36},{5,13},{6,38},{7,15},{8,40},{9,1... | collective-permute-start | bytes 196616 | tf_op jit(solution)/shard_map/ppermute | solution.py:36
  44.1 24.2 %collective-permute-start.10 = (f32[256,256]{1,0:T(8,128)S(1)}, f32[256,256]{1,0:T(8,128)S(1)}, u32[]{:S(2)}, u32[]{:S(2)}) collective-permute-start(f32[256,256]{1,0:T(8,128)S(1)} %slice.62), channel_id=1, source_target_pairs={{7,3},{15,11},{23,19},{31,27},{39,35},{47,43},{55,51},{63,59},{71,... | collective-permute-start | bytes 786440 | tf_op jit(solution)/shard_map/ppermute | solution.py:268
  44.8 23.5 %collective-permute-start.8 = (f32[256,256]{1,0:T(8,128)S(1)}, f32[256,256]{1,0:T(8,128)S(1)}, u32[]{:S(2)}, u32[]{:S(2)}) collective-permute-start(f32[256,256]{1,0:T(8,128)S(1)} %slice.62), channel_id=1, source_target_pairs={{7,1},{15,9},{23,17},{31,25},{39,33},{47,41},{55,49},{63,57},{71,6... | collective-permute-start | bytes 786440 | tf_op jit(solution)/shard_map/ppermute | solution.py:268
  47.0 6.5 %collective-permute-start.15 = (f32[64,256]{1,0:T(8,128)}, f32[64,256]{1,0:T(8,128)S(1)}, u32[]{:S(2)}, u32[]{:S(2)}) collective-permute-start(f32[64,256]{1,0:T(8,128)} %get-tuple-element.58), channel_id=1, source_target_pairs={{0,64},{1,17},{2,66},{3,19},{4,68},{5,21},{6,70},{7,23},{8,72},{9,... | collective-permute-start | bytes 196616 | tf_op jit(solution)/shard_map/ppermute | solution.py:36
  49.8 4.5 %collective-permute-start.17 = (f32[64,256]{1,0:T(8,128)}, f32[64,256]{1,0:T(8,128)S(1)}, u32[]{:S(2)}, u32[]{:S(2)}) collective-permute-start(f32[64,256]{1,0:T(8,128)} %get-tuple-element.59), channel_id=1, source_target_pairs={{0,96},{1,25},{2,98},{3,27},{4,100},{5,29},{6,102},{7,31},{8,104},... | collective-permute-start | bytes 196616 | tf_op jit(solution)/shard_map/ppermute | solution.py:36
  53.5 8.1 %copy-start.3 = (f32[256,256]{1,0:T(8,128)S(1)}, f32[256,256]{1,0:T(8,128)}, u32[]{:S(2)}) copy-start(f32[256,256]{1,0:T(8,128)} %inverse_hbm.1) | copy-start | bytes 786436
  53.5 12.4 %copy-start.2 = (f32[256,256]{1,0:T(8,128)S(1)}, f32[256,256]{1,0:T(8,128)}, u32[]{:S(2)}) copy-start(f32[256,256]{1,0:T(8,128)} %param.14) | copy-start | bytes 786436
  54.3 8.0 %collective-permute-start.18 = (f32[224,256]{1,0:T(8,128)S(1)}, f32[224,256]{1,0:T(8,128)S(1)}, u32[]{:S(2)}, u32[]{:S(2)}) collective-permute-start(f32[224,256]{1,0:T(8,128)S(1)} %get-tuple-element.52), channel_id=1, source_target_pairs={{0,16},{1,65},{2,18},{3,67},{4,20},{5,69},{6,22},{7,71},{8,24},{9,... | collective-permute-start | bytes 688136 | tf_op jit(solution)/shard_map/ppermute | solution.py:36
  58.3 7.2 %collective-permute-start.19 = (f32[224,256]{1,0:T(8,128)S(1)}, f32[224,256]{1,0:T(8,128)S(1)}, u32[]{:S(2)}, u32[]{:S(2)}) collective-permute-start(f32[224,256]{1,0:T(8,128)S(1)} %get-tuple-element.54), channel_id=1, source_target_pairs={{0,8},{1,33},{2,10},{3,35},{4,12},{5,37},{6,14},{7,39},{8,16},{9,4... | collective-permute-start | bytes 688136 | tf_op jit(solution)/shard_map/ppermute | solution.py:36
  59.3 6.5 %collective-permute-start.20 = (f32[224,256]{1,0:T(8,128)S(1)}, f32[224,256]{1,0:T(8,128)S(1)}, u32[]{:S(2)}, u32[]{:S(2)}) collective-permute-start(f32[224,256]{1,0:T(8,128)S(1)} %get-tuple-element.53), channel_id=1, source_target_pairs={{0,24},{1,97},{2,26},{3,99},{4,28},{5,101},{6,30},{7,103},{8,0},{9... | collective-permute-start | bytes 688136 | tf_op jit(solution)/shard_map/ppermute | solution.py:36
  62.3 6.0 %collective-permute-start.9 = (f32[256,256]{1,0:T(8,128)S(1)}, f32[256,256]{1,0:T(8,128)S(1)}, u32[]{:S(2)}, u32[]{:S(2)}) collective-permute-start(f32[256,256]{1,0:T(8,128)S(1)} %slice.62), channel_id=1, source_target_pairs={{7,5},{15,13},{23,21},{31,29},{39,37},{47,45},{55,53},{63,61},{71,... | collective-permute-start | bytes 786440 | tf_op jit(solution)/shard_map/ppermute | solution.py:268
  66.1 7.8 %collective-permute-start.21 = (f32[224,256]{1,0:T(8,128)S(1)}, f32[224,256]{1,0:T(8,128)S(1)}, u32[]{:S(2)}, u32[]{:S(2)}) collective-permute-start(f32[224,256]{1,0:T(8,128)S(1)} %get-tuple-element.62), channel_id=1, source_target_pairs={{0,16},{1,65},{2,18},{3,67},{4,20},{5,69},{6,22},{7,71},{8,24},{9,... | collective-permute-start | bytes 688136 | tf_op jit(solution)/shard_map/ppermute | solution.py:36
  69.3 11.4 %collective-permute-start.11 = (f32[256,256]{1,0:T(8,128)S(1)}, f32[256,256]{1,0:T(8,128)S(1)}, u32[]{:S(2)}, u32[]{:S(2)}) collective-permute-start(f32[256,256]{1,0:T(8,128)S(1)} %add_add_fusion.1), channel_id=1, source_target_pairs={{1,0},{3,2},{5,4},{7,6},{9,8},{11,10},{13,12},{15,14},{17,16},{19,... | collective-permute-start | bytes 786440 | tf_op jit(solution)/shard_map/ppermute | solution.py:270
  70.6 7.3 %collective-permute-start.22 = (f32[224,256]{1,0:T(8,128)S(1)}, f32[224,256]{1,0:T(8,128)S(1)}, u32[]{:S(2)}, u32[]{:S(2)}) collective-permute-start(f32[224,256]{1,0:T(8,128)S(1)} %get-tuple-element.62), channel_id=1, source_target_pairs={{0,8},{1,33},{2,10},{3,35},{4,12},{5,37},{6,14},{7,39},{8,16},{9,4... | collective-permute-start | bytes 688136 | tf_op jit(solution)/shard_map/ppermute | solution.py:36
  72.5 6.0 %collective-permute-start.23 = (f32[224,256]{1,0:T(8,128)S(1)}, f32[224,256]{1,0:T(8,128)S(1)}, u32[]{:S(2)}, u32[]{:S(2)}) collective-permute-start(f32[224,256]{1,0:T(8,128)S(1)} %get-tuple-element.62), channel_id=1, source_target_pairs={{0,24},{1,97},{2,26},{3,99},{4,28},{5,101},{6,30},{7,103},{8,0},{9... | collective-permute-start | bytes 688136 | tf_op jit(solution)/shard_map/ppermute | solution.py:36
  78.5 15.1 %collective-permute-start.24 = (f32[896,256]{1,0:T(8,128)S(1)}, f32[896,256]{1,0:T(8,128)S(1)}, u32[]{:S(2)}, u32[]{:S(2)}) collective-permute-start(f32[896,256]{1,0:T(8,128)S(1)} %bitcast.86), channel_id=1, source_target_pairs={{0,64},{1,17},{2,66},{3,19},{4,68},{5,21},{6,70},{7,23},{8,72},{9,... | collective-permute-start | bytes 2752520 | tf_op jit(solution)/shard_map/ppermute | solution.py:36
  81.2 22.5 %collective-permute-start.29 = (f32[896,256]{1,0:T(8,128)S(1)}, f32[896,256]{1,0:T(8,128)S(1)}, u32[]{:S(2)}, u32[]{:S(2)}) collective-permute-start(f32[896,256]{1,0:T(8,128)S(1)} %bitcast.87), channel_id=1, source_target_pairs={{0,32},{1,9},{2,34},{3,11},{4,36},{5,13},{6,38},{7,15},{8,40},{9,1... | collective-permute-start | bytes 2752520 | tf_op jit(solution)/shard_map/ppermute | solution.py:36
  83.2 20.7 %collective-permute-start.30 = (f32[896,256]{1,0:T(8,128)S(1)}, f32[896,256]{1,0:T(8,128)S(1)}, u32[]{:S(2)}, u32[]{:S(2)}) collective-permute-start(f32[896,256]{1,0:T(8,128)S(1)} %bitcast.88), channel_id=1, source_target_pairs={{0,96},{1,25},{2,98},{3,27},{4,100},{5,29},{6,102},{7,31},{8,104},... | collective-permute-start | bytes 2752520 | tf_op jit(solution)/shard_map/ppermute | solution.py:36
  93.6 7.9 %collective-permute-start.25 = (f32[64,512]{1,0:T(8,128)S(1)}, f32[64,512]{1,0:T(8,128)S(1)}, u32[]{:S(2)}, u32[]{:S(2)}) collective-permute-start(f32[64,512]{1,0:T(8,128)S(1)} %pad_maximum_fusion), channel_id=1, source_target_pairs={{0,4},{1,5},{2,6},{3,7},{4,0},{5,1},{6,2},{7,3},{8,12},{9,13},{10,... | collective-permute-start | bytes 393224 | tf_op jit(solution)/shard_map/ppermute | solution.py:41
  96.6 7.0 %collective-permute-start.26 = (f32[64,512]{1,0:T(8,128)S(1)}, f32[64,512]{1,0:T(8,128)S(1)}, u32[]{:S(2)}, u32[]{:S(2)}) collective-permute-start(f32[64,512]{1,0:T(8,128)S(1)} %pad_maximum_fusion), channel_id=1, source_target_pairs={{0,2},{1,3},{2,4},{3,5},{4,6},{5,7},{6,0},{7,1},{8,10},{9,11},{10,... | collective-permute-start | bytes 393224 | tf_op jit(solution)/shard_map/ppermute | solution.py:41
  97.2 6.4 %collective-permute-start.27 = (f32[64,512]{1,0:T(8,128)S(1)}, f32[64,512]{1,0:T(8,128)S(1)}, u32[]{:S(2)}, u32[]{:S(2)}) collective-permute-start(f32[64,512]{1,0:T(8,128)S(1)} %pad_maximum_fusion), channel_id=1, source_target_pairs={{0,6},{1,7},{2,0},{3,1},{4,2},{5,3},{6,4},{7,5},{8,14},{9,15},{10,... | collective-permute-start | bytes 393224 | tf_op jit(solution)/shard_map/ppermute | solution.py:41
  103.7 2.0 %collective-permute-start.28 = (f32[256,512]{1,0:T(8,128)S(1)}, f32[256,512]{1,0:T(8,128)S(1)}, u32[]{:S(2)}, u32[]{:S(2)}) collective-permute-start(f32[256,512]{1,0:T(8,128)S(1)} %bitcast.91), channel_id=1, source_target_pairs={{0,1},{1,0},{2,3},{3,2},{4,5},{5,4},{6,7},{7,6},{8,9},{9,8},{10,11... | collective-permute-start | bytes 1572872 | tf_op jit(solution)/shard_map/ppermute | solution.py:45
  107.0 1.2 %copy-start.1 = (f32[7,4,64,256]{3,2,1,0:T(8,128)}, f32[7,4,64,256]{3,2,1,0:T(8,128)S(1)}, u32[]{:S(2)}) copy-start(f32[7,4,64,256]{3,2,1,0:T(8,128)S(1)} %constant_dynamic-update-slice_fusion.7) | copy-start | bytes 5505028
  107.0 1.8 %copy-start = (f32[7,4,64,256]{3,2,1,0:T(8,128)}, f32[7,4,64,256]{3,2,1,0:T(8,128)S(1)}, u32[]{:S(2)}) copy-start(f32[7,4,64,256]{3,2,1,0:T(8,128)S(1)} %constant_dynamic-update-slice_fusion.2) | copy-start | bytes 5505028

commit v5 on v4

--- a/solution.py
+++ b/solution.py
@@ -296,7 +296,7 @@
     value = value.reshape(2 * half, width)
 
     got = arrivals([value] * SIDE, 0)
-    panel = after(panel, got[0])
+    panel = after(panel, got[1])
     panels = jnp.zeros((SIDE,) + panel.shape, jnp.float32)
     for part, step in [(panel, 0)] + [(shift_x(panel, step), step) for step in STEPS]:
         panels = lax.dynamic_update_index_in_dim(panels, part, (x - step) % SIDE, 0)
@@ -305,18 +305,17 @@
     both = lax.dynamic_update_index_in_dim(both, panels, core, 0)
     both = lax.dynamic_update_index_in_dim(both, swap_core(panels), 1 - core, 0)
     both = both.reshape(-1, 2 * width)
-    panel_second, panel_first = both[:, :width], both[:, width:]
     pivots = [jnp.zeros((chunks, SIDE, piece, width), jnp.float32)] * 2
     parts = [(value, 0)] + list(zip(got, STEPS))
-    for i, (part, step) in enumerate(parts):
-        if i == 1:
-            pivots = after(pivots, panel_second, panel_first)
+    for part, step in parts:
         pivots = [
             lax.dynamic_update_index_in_dim(
                 pivot, rows.reshape(chunks, piece, width), (place - step) % SIDE, 1
             )
             for pivot, rows in zip(pivots, (part[:half], part[half:]))
         ]
+    both = after(both, *pivots)
+    panel_second, panel_first = both[:, :width], both[:, width:]
     pivot_second, pivot_first = (pivot.reshape(tile_cols, width) for pivot in pivots)
     return (panel_second, pivot_second, panel_first, pivot_first)
 

time: 110 us -> 109 us (level)
  local copies, waits for them, and re-layouts: 5.96 us -> 4.21 us
  waiting for transfers between devices: 29.8 us -> 31.3 us
    ppermute x15, waiting for transfers between devices: 18.7 us -> 23.7 us  [shift(): return lax.ppermute(value, ('row', 'col'), pairs(step, swap))]
    ppermute x6, waiting for transfers between devices: 8.32 us -> 4.8 us  [shift_x(): return lax.ppermute(value, 'col', pairs)]
    unnamed x12, local copies, waits for them, and re-layouts: 1.79 us -> 0.04 us
  transfers between devices with their start and end apart: 31 -> 31, of which waited for: 15 -> 13; matrix products, arithmetic and copies ran while one was open for 8% -> 8% of each run, Pallas kernels for 7% -> 7%
where the time goes in v5:
time: 109 us; the launch traced here: 108 us
  starting transfers between devices  50.8 us (47%)
  waiting for transfers between devices  31.3 us (29%)
  Pallas kernels  14.5 us (13%)
  other arithmetic  4.88 us (4%)
  local copies, waits for them, and re-layouts  4.21 us (4%)
  between operations  1.32 us (1%)
    ppermute x15, starting transfers between devices, shift(): return lax.ppermute(value, ('row', 'col'), pairs(step, swap))  29.5 us
    ppermute x15, waiting for transfers between devices, shift(): return lax.ppermute(value, ('row', 'col'), pairs(step, swap))  23.7 us
    ppermute x6, starting transfers between devices, shift_x(): return lax.ppermute(value, 'col', pairs)  13.7 us
    pallas_call x1, Pallas kernels, pivot_products(): pl.pallas_call(pivot_kernel, in_specs=[hbm] * 3, out_specs=[hbm] * SIDE,...  7.95 us
    pallas_call x1, Pallas kernels, left_products(): pl.pallas_call(left_kernel, in_specs=[hbm] * 5, out_specs=[hbm] * 3, out_...  6.57 us
    ppermute x6, waiting for transfers between devices, shift_x(): return lax.ppermute(value, 'col', pairs)  4.8 us
    ppermute x3, starting transfers between devices, local(): lax.ppermute(cross, 'col', [(source, last)])  2.86 us
  transfers between devices with their start and end apart: 31, of which 13 were waited for; matrix products, arithmetic and copies ran while one was open for 8% of the time, Pallas kernels for 7%

profile of v5, /device:TPU:0, one launch (start us, length us, event | category | flops | bytes accessed | tf_op | source)
XLA Modules:
  0.0 107.9 jit_solution(1819837099733407260)
XLA Ops:
  0.6 6.6 %left_products.1 = (f32[256,512]{1,0:T(8,128)}, f32[256,512]{1,0:T(8,128)}, f32[256,256]{1,0:T(8,128)}) custom-call(f32[512,1792]{1,0:T(8,128)} %window_hbm.2, f32[1792,256]{1,0:T(8,128)} %cols_second_hbm.1, f32[1792,256]{1,0:T(8,128)} %cols_first_hbm.1, f32[512,256]{1,0:T(8,128)} %rows_first_hbm.1, f32[256,256]{1,0:T(8,128)} %inverse_hbm.1), custom_call_target="tpu_custom_call" | custom-call | flops 2818572288 | bytes 7340032 | tf_op jit(solution)/shard_map/left_products/pallas_call | solution.py:206
  7.2 1.3 %collective-permute-start.1 = (f32[256,256]{1,0:T(8,128)}, f32[256,256]{1,0:T(8,128)S(1)}, u32[]{:S(2)}, u32[]{:S(2)}) collective-permute-start(f32[256,256]{1,0:T(8,128)} %get-tuple-element.30), channel_id=1, source_target_pairs={{0,1},{2,3},{4,5},{6,7},{8,9},{10,11},{12,13},{14,15},{16,17},{18,... | collective-permute-start | bytes 786440 | tf_op jit(solution)/shard_map/ppermute | solution.py:256
  8.6 1.2 %collective-permute-done.1 = f32[256,256]{1,0:T(8,128)S(1)} collective-permute-done((f32[256,256]{1,0:T(8,128)}, f32[256,256]{1,0:T(8,128)S(1)}, u32[]{:S(2)}, u32[]{:S(2)}) %collective-permute-start.1) | collective-permute-done | bytes 262176 | tf_op jit(solution)/shard_map/ppermute | solution.py:256
  9.9 1.0 add.271
  10.9 0.8 collective-permute-start.2
  11.7 0.7 collective-permute-start.3
  12.4 1.4 %collective-permute-start.4 = (f32[256,256]{1,0:T(8,128)S(1)}, f32[256,256]{1,0:T(8,128)}, u32[]{:S(2)}, u32[]{:S(2)}) collective-permute-start(f32[256,256]{1,0:T(8,128)S(1)} %add.271), channel_id=1, source_target_pairs={{5,7},{13,15},{21,23},{29,31},{37,39},{45,47},{53,55},{61,63},{69,... | collective-permute-start | bytes 786440 | tf_op jit(solution)/shard_map/ppermute | solution.py:257
  13.7 8.0 %pivot_products.1 = (f32[896,256]{1,0:T(8,128)}, f32[896,256]{1,0:T(8,128)}, f32[896,256]{1,0:T(8,128)}, f32[896,256]{1,0:T(8,128)}) custom-call(f32[512,1792]{1,0:T(8,128)} %window_hbm.2, f32[512,256]{1,0:T(8,128)} %rows_second_hbm.1, f32[512,256]{1,0:T(8,128)} %rows_first_hbm.1), custom_call_target="tpu_custom_call" | custom-call | flops 2818572288 | bytes 7340032 | tf_op jit(solution)/shard_map/pivot_products/pallas_call | solution.py:121
  21.7 3.8 %collective-permute-start.12 = (f32[896,256]{1,0:T(8,128)}, f32[896,256]{1,0:T(8,128)S(1)}, u32[]{:S(2)}, u32[]{:S(2)}) collective-permute-start(f32[896,256]{1,0:T(8,128)} %get-tuple-element.35), channel_id=1, source_target_pairs={{0,64},{1,17},{2,66},{3,19},{4,68},{5,21},{6,70},{7,23},{8,72},{9,... | collective-permute-start | bytes 2752520 | tf_op jit(solution)/shard_map/ppermute | solution.py:36
  25.5 0.7 collective-permute-start.13
  26.3 2.6 %collective-permute-start.14 = (f32[896,256]{1,0:T(8,128)}, f32[896,256]{1,0:T(8,128)}, u32[]{:S(2)}, u32[]{:S(2)}) collective-permute-start(f32[896,256]{1,0:T(8,128)} %get-tuple-element.37), channel_id=1, source_target_pairs={{0,96},{1,25},{2,98},{3,27},{4,100},{5,29},{6,102},{7,31},{8,104},... | collective-permute-start | bytes 2752520 | tf_op jit(solution)/shard_map/ppermute | solution.py:36
  28.9 1.0 add_select_fusion
  29.9 0.7 dynamic-slice_bitcast_fusion.7
  30.7 3.1 %collective-permute-start.5 = (f32[64,512]{1,0:T(8,128)S(1)}, f32[64,512]{1,0:T(8,128)S(1)}, u32[]{:S(2)}, u32[]{:S(2)}) collective-permute-start(f32[64,512]{1,0:T(8,128)S(1)} %get-tuple-element.53), channel_id=1, source_target_pairs={{0,4},{1,5},{2,6},{3,7},{4,0},{5,1},{6,2},{7,3},{8,12},{9,13},{10,... | collective-permute-start | bytes 393224 | tf_op jit(solution)/shard_map/ppermute | solution.py:41
  33.8 0.6 collective-permute-start.6
  34.4 2.9 %collective-permute-done.5 = f32[64,512]{1,0:T(8,128)S(1)} collective-permute-done((f32[64,512]{1,0:T(8,128)S(1)}, f32[64,512]{1,0:T(8,128)S(1)}, u32[]{:S(2)}, u32[]{:S(2)}) %collective-permute-start.5) | collective-permute-done | bytes 131104 | tf_op jit(solution)/shard_map/ppermute | solution.py:41
  37.2 3.7 %collective-permute-start.7 = (f32[64,512]{1,0:T(8,128)S(1)}, f32[64,512]{1,0:T(8,128)S(1)}, u32[]{:S(2)}, u32[]{:S(2)}) collective-permute-start(f32[64,512]{1,0:T(8,128)S(1)} %get-tuple-element.54), channel_id=1, source_target_pairs={{0,6},{1,7},{2,0},{3,1},{4,2},{5,3},{6,4},{7,5},{8,14},{9,15},{10,... | collective-permute-start | bytes 393224 | tf_op jit(solution)/shard_map/ppermute | solution.py:41
  40.9 1.0 slice.62
  42.2 1.9 %collective-permute-done.7 = f32[64,512]{1,0:T(8,128)S(1)} collective-permute-done((f32[64,512]{1,0:T(8,128)S(1)}, f32[64,512]{1,0:T(8,128)S(1)}, u32[]{:S(2)}, u32[]{:S(2)}) %collective-permute-start.7) | collective-permute-done | bytes 131104 | tf_op jit(solution)/shard_map/ppermute | solution.py:41
  44.1 0.7 collective-permute-start.10
  44.8 0.7 collective-permute-start.8
  45.5 1.5 %collective-permute-done.13 = f32[896,256]{1,0:T(8,128)} collective-permute-done((f32[896,256]{1,0:T(8,128)}, f32[896,256]{1,0:T(8,128)}, u32[]{:S(2)}, u32[]{:S(2)}) %collective-permute-start.13) | collective-permute-done | bytes 917536 | tf_op jit(solution)/shard_map/ppermute | solution.py:36
  47.0 2.7 %collective-permute-start.15 = (f32[64,256]{1,0:T(8,128)}, f32[64,256]{1,0:T(8,128)S(1)}, u32[]{:S(2)}, u32[]{:S(2)}) collective-permute-start(f32[64,256]{1,0:T(8,128)} %get-tuple-element.56), channel_id=1, source_target_pairs={{0,64},{1,17},{2,66},{3,19},{4,68},{5,21},{6,70},{7,23},{8,72},{9,... | collective-permute-start | bytes 196616 | tf_op jit(solution)/shard_map/ppermute | solution.py:36
  49.8 2.0 %collective-permute-start.17 = (f32[64,256]{1,0:T(8,128)}, f32[64,256]{1,0:T(8,128)S(1)}, u32[]{:S(2)}, u32[]{:S(2)}) collective-permute-start(f32[64,256]{1,0:T(8,128)} %get-tuple-element.57), channel_id=1, source_target_pairs={{0,96},{1,25},{2,98},{3,27},{4,100},{5,29},{6,102},{7,31},{8,104},... | collective-permute-start | bytes 196616 | tf_op jit(solution)/shard_map/ppermute | solution.py:36
  51.8 1.7 %add_add_fusion = f32[896,256]{1,0:T(8,128)S(1)} fusion(f32[896,256]{1,0:T(8,128)} %collective-permute-done.14, f32[896,256]{1,0:T(8,128)} %collective-permute-done.13, f32[896,256]{1,0:T(8,128)S(1)} %copy-done.4, f32[896,256]{1,0:T(8,128)S(1)} %collective-permute-done.12), kind=kLoop, calls=%fused_computation | loop fusion | flops 688128 | bytes 4587520 | tf_op jit(solution)/shard_map/add | solution.py:281
  53.5 0.7 collective-permute-done.17
  54.3 4.0 %collective-permute-start.18 = (f32[224,256]{1,0:T(8,128)S(1)}, f32[224,256]{1,0:T(8,128)S(1)}, u32[]{:S(2)}, u32[]{:S(2)}) collective-permute-start(f32[224,256]{1,0:T(8,128)S(1)} %get-tuple-element.50), channel_id=1, source_target_pairs={{0,16},{1,65},{2,18},{3,67},{4,20},{5,69},{6,22},{7,71},{8,24},{9,... | collective-permute-start | bytes 688136 | tf_op jit(solution)/shard_map/ppermute | solution.py:36
  58.3 1.0 collective-permute-start.19
  59.3 2.2 %collective-permute-start.20 = (f32[224,256]{1,0:T(8,128)S(1)}, f32[224,256]{1,0:T(8,128)S(1)}, u32[]{:S(2)}, u32[]{:S(2)}) collective-permute-start(f32[224,256]{1,0:T(8,128)S(1)} %get-tuple-element.51), channel_id=1, source_target_pairs={{0,24},{1,97},{2,26},{3,99},{4,28},{5,101},{6,30},{7,103},{8,0},{9... | collective-permute-start | bytes 688136 | tf_op jit(solution)/shard_map/ppermute | solution.py:36
  61.8 0.5 collective-permute-done.18
  62.3 0.7 collective-permute-start.9
  63.0 2.6 %collective-permute-done.19 = f32[224,256]{1,0:T(8,128)S(1)} collective-permute-done((f32[224,256]{1,0:T(8,128)S(1)}, f32[224,256]{1,0:T(8,128)S(1)}, u32[]{:S(2)}, u32[]{:S(2)}) %collective-permute-start.19) | collective-permute-done | bytes 229408 | tf_op jit(solution)/shard_map/ppermute | solution.py:36
  66.1 2.2 %collective-permute-start.21 = (f32[224,256]{1,0:T(8,128)S(1)}, f32[224,256]{1,0:T(8,128)S(1)}, u32[]{:S(2)}, u32[]{:S(2)}) collective-permute-start(f32[224,256]{1,0:T(8,128)S(1)} %get-tuple-element.60), channel_id=1, source_target_pairs={{0,16},{1,65},{2,18},{3,67},{4,20},{5,69},{6,22},{7,71},{8,24},{9,... | collective-permute-start | bytes 688136 | tf_op jit(solution)/shard_map/ppermute | solution.py:36
  68.3 1.0 add_add_fusion.1
  69.3 1.3 %collective-permute-start.11 = (f32[256,256]{1,0:T(8,128)S(1)}, f32[256,256]{1,0:T(8,128)S(1)}, u32[]{:S(2)}, u32[]{:S(2)}) collective-permute-start(f32[256,256]{1,0:T(8,128)S(1)} %add_add_fusion.1), channel_id=1, source_target_pairs={{1,0},{3,2},{5,4},{7,6},{9,8},{11,10},{13,12},{15,14},{17,16},{19,... | collective-permute-start | bytes 786440 | tf_op jit(solution)/shard_map/ppermute | solution.py:270
  70.6 1.9 %collective-permute-start.22 = (f32[224,256]{1,0:T(8,128)S(1)}, f32[224,256]{1,0:T(8,128)S(1)}, u32[]{:S(2)}, u32[]{:S(2)}) collective-permute-start(f32[224,256]{1,0:T(8,128)S(1)} %get-tuple-element.60), channel_id=1, source_target_pairs={{0,8},{1,33},{2,10},{3,35},{4,12},{5,37},{6,14},{7,39},{8,16},{9,4... | collective-permute-start | bytes 688136 | tf_op jit(solution)/shard_map/ppermute | solution.py:36
  72.5 1.5 %collective-permute-start.23 = (f32[224,256]{1,0:T(8,128)S(1)}, f32[224,256]{1,0:T(8,128)S(1)}, u32[]{:S(2)}, u32[]{:S(2)}) collective-permute-start(f32[224,256]{1,0:T(8,128)S(1)} %get-tuple-element.60), channel_id=1, source_target_pairs={{0,24},{1,97},{2,26},{3,99},{4,28},{5,101},{6,30},{7,103},{8,0},{9... | collective-permute-start | bytes 688136 | tf_op jit(solution)/shard_map/ppermute | solution.py:36
  74.0 4.0 %collective-permute-done.22 = f32[224,256]{1,0:T(8,128)S(1)} collective-permute-done((f32[224,256]{1,0:T(8,128)S(1)}, f32[224,256]{1,0:T(8,128)S(1)}, u32[]{:S(2)}, u32[]{:S(2)}) %collective-permute-start.22) | collective-permute-done | bytes 229408 | tf_op jit(solution)/shard_map/ppermute | solution.py:36
  78.0 0.6 collective-permute-done.23
  78.5 0.9 collective-permute-start.24
  79.9 3.9 %collective-permute-start.29 = (f32[896,256]{1,0:T(8,128)S(1)}, f32[896,256]{1,0:T(8,128)S(1)}, u32[]{:S(2)}, u32[]{:S(2)}) collective-permute-start(f32[896,256]{1,0:T(8,128)S(1)} %bitcast.87), channel_id=1, source_target_pairs={{0,64},{1,17},{2,66},{3,19},{4,68},{5,21},{6,70},{7,23},{8,72},{9,... | collective-permute-start | bytes 2752520 | tf_op jit(solution)/shard_map/ppermute | solution.py:36
  84.5 8.7 %collective-permute-done.24 = f32[896,256]{1,0:T(8,128)S(1)} collective-permute-done((f32[896,256]{1,0:T(8,128)S(1)}, f32[896,256]{1,0:T(8,128)S(1)}, u32[]{:S(2)}, u32[]{:S(2)}) %collective-permute-start.24) | collective-permute-done | bytes 917536 | tf_op jit(solution)/shard_map/ppermute | solution.py:36
  93.2 3.0 %collective-permute-start.25 = (f32[64,512]{1,0:T(8,128)S(1)}, f32[64,512]{1,0:T(8,128)S(1)}, u32[]{:S(2)}, u32[]{:S(2)}) collective-permute-start(f32[64,512]{1,0:T(8,128)S(1)} %pad_maximum_fusion), channel_id=1, source_target_pairs={{0,4},{1,5},{2,6},{3,7},{4,0},{5,1},{6,2},{7,3},{8,12},{9,13},{10,... | collective-permute-start | bytes 393224 | tf_op jit(solution)/shard_map/ppermute | solution.py:41
  96.2 0.6 collective-permute-start.26
  96.8 2.6 %collective-permute-start.27 = (f32[64,512]{1,0:T(8,128)S(1)}, f32[64,512]{1,0:T(8,128)S(1)}, u32[]{:S(2)}, u32[]{:S(2)}) collective-permute-start(f32[64,512]{1,0:T(8,128)S(1)} %pad_maximum_fusion), channel_id=1, source_target_pairs={{0,6},{1,7},{2,0},{3,1},{4,2},{5,3},{6,4},{7,5},{8,14},{9,15},{10,... | collective-permute-start | bytes 393224 | tf_op jit(solution)/shard_map/ppermute | solution.py:41
  99.6 4.9 %collective-permute-done.29 = f32[896,256]{1,0:T(8,128)S(1)} collective-permute-done((f32[896,256]{1,0:T(8,128)S(1)}, f32[896,256]{1,0:T(8,128)S(1)}, u32[]{:S(2)}, u32[]{:S(2)}) %collective-permute-start.29) | collective-permute-done | bytes 917536 | tf_op jit(solution)/shard_map/ppermute | solution.py:36
  105.3 1.5 %collective-permute-done.28 = f32[256,512]{1,0:T(8,128)S(1)} collective-permute-done((f32[256,512]{1,0:T(8,128)S(1)}, f32[256,512]{1,0:T(8,128)S(1)}, u32[]{:S(2)}, u32[]{:S(2)}) %collective-permute-start.28) | collective-permute-done | bytes 524320 | tf_op jit(solution)/shard_map/ppermute | solution.py:45
  106.8 1.0 fusion.21
  (70 shorter events, 3.2 us)
Async XLA Ops:
  7.2 2.7 %collective-permute-start.1 = (f32[256,256]{1,0:T(8,128)}, f32[256,256]{1,0:T(8,128)S(1)}, u32[]{:S(2)}, u32[]{:S(2)}) collective-permute-start(f32[256,256]{1,0:T(8,128)} %get-tuple-element.30), channel_id=1, source_target_pairs={{0,1},{2,3},{4,5},{6,7},{8,9},{10,11},{12,13},{14,15},{16,17},{18,... | collective-permute-start | bytes 786440 | tf_op jit(solution)/shard_map/ppermute | solution.py:256
  8.5 17.0 %collective-permute-start = (f32[256,512]{1,0:T(8,128)}, f32[256,512]{1,0:T(8,128)S(1)}, u32[]{:S(2)}, u32[]{:S(2)}) collective-permute-start(f32[256,512]{1,0:T(8,128)} %get-tuple-element.29), channel_id=1, source_target_pairs={{0,1},{1,0},{2,3},{3,2},{4,5},{5,4},{6,7},{7,6},{8,9},{9,8},{10,11... | collective-permute-start | bytes 1572872 | tf_op jit(solution)/shard_map/ppermute | solution.py:45
  10.8 15.3 %copy-start.5 = (f32[256,512]{1,0:T(8,128)S(1)}, f32[256,512]{1,0:T(8,128)}, u32[]{:S(2)}) copy-start(f32[256,512]{1,0:T(8,128)} %get-tuple-element.28) | copy-start | bytes 1572868
  10.9 15.4 %collective-permute-start.2 = (f32[256,256]{1,0:T(8,128)S(1)}, f32[256,256]{1,0:T(8,128)S(1)}, u32[]{:S(2)}, u32[]{:S(2)}) collective-permute-start(f32[256,256]{1,0:T(8,128)S(1)} %add.271), channel_id=1, source_target_pairs={{3,7},{11,15},{19,23},{27,31},{35,39},{43,47},{51,55},{59,63},{67,... | collective-permute-start | bytes 786440 | tf_op jit(solution)/shard_map/ppermute | solution.py:257
  11.7 17.2 %collective-permute-start.3 = (f32[256,256]{1,0:T(8,128)S(1)}, f32[256,256]{1,0:T(8,128)S(1)}, u32[]{:S(2)}, u32[]{:S(2)}) collective-permute-start(f32[256,256]{1,0:T(8,128)S(1)} %add.271), channel_id=1, source_target_pairs={{1,7},{9,15},{17,23},{25,31},{33,39},{41,47},{49,55},{57,63},{65,7... | collective-permute-start | bytes 786440 | tf_op jit(solution)/shard_map/ppermute | solution.py:257
  12.4 16.6 %collective-permute-start.4 = (f32[256,256]{1,0:T(8,128)S(1)}, f32[256,256]{1,0:T(8,128)}, u32[]{:S(2)}, u32[]{:S(2)}) collective-permute-start(f32[256,256]{1,0:T(8,128)S(1)} %add.271), channel_id=1, source_target_pairs={{5,7},{13,15},{21,23},{29,31},{37,39},{45,47},{53,55},{61,63},{69,... | collective-permute-start | bytes 786440 | tf_op jit(solution)/shard_map/ppermute | solution.py:257
  21.7 23.1 %collective-permute-start.12 = (f32[896,256]{1,0:T(8,128)}, f32[896,256]{1,0:T(8,128)S(1)}, u32[]{:S(2)}, u32[]{:S(2)}) collective-permute-start(f32[896,256]{1,0:T(8,128)} %get-tuple-element.35), channel_id=1, source_target_pairs={{0,64},{1,17},{2,66},{3,19},{4,68},{5,21},{6,70},{7,23},{8,72},{9,... | collective-permute-start | bytes 2752520 | tf_op jit(solution)/shard_map/ppermute | solution.py:36
  25.5 21.5 %collective-permute-start.13 = (f32[896,256]{1,0:T(8,128)}, f32[896,256]{1,0:T(8,128)}, u32[]{:S(2)}, u32[]{:S(2)}) collective-permute-start(f32[896,256]{1,0:T(8,128)} %get-tuple-element.36), channel_id=1, source_target_pairs={{0,32},{1,9},{2,34},{3,11},{4,36},{5,13},{6,38},{7,15},{8,40},{9,1... | collective-permute-start | bytes 2752520 | tf_op jit(solution)/shard_map/ppermute | solution.py:36
  26.3 25.5 %copy-start.4 = (f32[896,256]{1,0:T(8,128)S(1)}, f32[896,256]{1,0:T(8,128)}, u32[]{:S(2)}) copy-start(f32[896,256]{1,0:T(8,128)} %get-tuple-element.34) | copy-start | bytes 2752516
  26.3 23.5 %collective-permute-start.14 = (f32[896,256]{1,0:T(8,128)}, f32[896,256]{1,0:T(8,128)}, u32[]{:S(2)}, u32[]{:S(2)}) collective-permute-start(f32[896,256]{1,0:T(8,128)} %get-tuple-element.37), channel_id=1, source_target_pairs={{0,96},{1,25},{2,98},{3,27},{4,100},{5,29},{6,102},{7,31},{8,104},... | collective-permute-start | bytes 2752520 | tf_op jit(solution)/shard_map/ppermute | solution.py:36
  30.7 6.6 %collective-permute-start.5 = (f32[64,512]{1,0:T(8,128)S(1)}, f32[64,512]{1,0:T(8,128)S(1)}, u32[]{:S(2)}, u32[]{:S(2)}) collective-permute-start(f32[64,512]{1,0:T(8,128)S(1)} %get-tuple-element.53), channel_id=1, source_target_pairs={{0,4},{1,5},{2,6},{3,7},{4,0},{5,1},{6,2},{7,3},{8,12},{9,13},{10,... | collective-permute-start | bytes 393224 | tf_op jit(solution)/shard_map/ppermute | solution.py:41
  33.8 8.3 %collective-permute-start.6 = (f32[64,512]{1,0:T(8,128)S(1)}, f32[64,512]{1,0:T(8,128)S(1)}, u32[]{:S(2)}, u32[]{:S(2)}) collective-permute-start(f32[64,512]{1,0:T(8,128)S(1)} %get-tuple-element.55), channel_id=1, source_target_pairs={{0,2},{1,3},{2,4},{3,5},{4,6},{5,7},{6,0},{7,1},{8,10},{9,11},{10,... | collective-permute-start | bytes 393224 | tf_op jit(solution)/shard_map/ppermute | solution.py:41
  37.2 6.9 %collective-permute-start.7 = (f32[64,512]{1,0:T(8,128)S(1)}, f32[64,512]{1,0:T(8,128)S(1)}, u32[]{:S(2)}, u32[]{:S(2)}) collective-permute-start(f32[64,512]{1,0:T(8,128)S(1)} %get-tuple-element.54), channel_id=1, source_target_pairs={{0,6},{1,7},{2,0},{3,1},{4,2},{5,3},{6,4},{7,5},{8,14},{9,15},{10,... | collective-permute-start | bytes 393224 | tf_op jit(solution)/shard_map/ppermute | solution.py:41
  42.1 11.4 %collective-permute-start.16 = (f32[64,256]{1,0:T(8,128)}, f32[64,256]{1,0:T(8,128)S(1)}, u32[]{:S(2)}, u32[]{:S(2)}) collective-permute-start(f32[64,256]{1,0:T(8,128)} %get-tuple-element.58), channel_id=1, source_target_pairs={{0,32},{1,9},{2,34},{3,11},{4,36},{5,13},{6,38},{7,15},{8,40},{9,1... | collective-permute-start | bytes 196616 | tf_op jit(solution)/shard_map/ppermute | solution.py:36
  44.1 24.2 %collective-permute-start.10 = (f32[256,256]{1,0:T(8,128)S(1)}, f32[256,256]{1,0:T(8,128)S(1)}, u32[]{:S(2)}, u32[]{:S(2)}) collective-permute-start(f32[256,256]{1,0:T(8,128)S(1)} %slice.62), channel_id=1, source_target_pairs={{7,3},{15,11},{23,19},{31,27},{39,35},{47,43},{55,51},{63,59},{71,... | collective-permute-start | bytes 786440 | tf_op jit(solution)/shard_map/ppermute | solution.py:268
  44.8 23.5 %collective-permute-start.8 = (f32[256,256]{1,0:T(8,128)S(1)}, f32[256,256]{1,0:T(8,128)S(1)}, u32[]{:S(2)}, u32[]{:S(2)}) collective-permute-start(f32[256,256]{1,0:T(8,128)S(1)} %slice.62), channel_id=1, source_target_pairs={{7,1},{15,9},{23,17},{31,25},{39,33},{47,41},{55,49},{63,57},{71,6... | collective-permute-start | bytes 786440 | tf_op jit(solution)/shard_map/ppermute | solution.py:268
  47.0 6.5 %collective-permute-start.15 = (f32[64,256]{1,0:T(8,128)}, f32[64,256]{1,0:T(8,128)S(1)}, u32[]{:S(2)}, u32[]{:S(2)}) collective-permute-start(f32[64,256]{1,0:T(8,128)} %get-tuple-element.56), channel_id=1, source_target_pairs={{0,64},{1,17},{2,66},{3,19},{4,68},{5,21},{6,70},{7,23},{8,72},{9,... | collective-permute-start | bytes 196616 | tf_op jit(solution)/shard_map/ppermute | solution.py:36
  49.8 4.5 %collective-permute-start.17 = (f32[64,256]{1,0:T(8,128)}, f32[64,256]{1,0:T(8,128)S(1)}, u32[]{:S(2)}, u32[]{:S(2)}) collective-permute-start(f32[64,256]{1,0:T(8,128)} %get-tuple-element.57), channel_id=1, source_target_pairs={{0,96},{1,25},{2,98},{3,27},{4,100},{5,29},{6,102},{7,31},{8,104},... | collective-permute-start | bytes 196616 | tf_op jit(solution)/shard_map/ppermute | solution.py:36
  53.5 8.1 %copy-start.3 = (f32[256,256]{1,0:T(8,128)S(1)}, f32[256,256]{1,0:T(8,128)}, u32[]{:S(2)}) copy-start(f32[256,256]{1,0:T(8,128)} %inverse_hbm.1) | copy-start | bytes 786436
  53.5 12.4 %copy-start.2 = (f32[256,256]{1,0:T(8,128)S(1)}, f32[256,256]{1,0:T(8,128)}, u32[]{:S(2)}) copy-start(f32[256,256]{1,0:T(8,128)} %param.14) | copy-start | bytes 786436
  54.3 8.0 %collective-permute-start.18 = (f32[224,256]{1,0:T(8,128)S(1)}, f32[224,256]{1,0:T(8,128)S(1)}, u32[]{:S(2)}, u32[]{:S(2)}) collective-permute-start(f32[224,256]{1,0:T(8,128)S(1)} %get-tuple-element.50), channel_id=1, source_target_pairs={{0,16},{1,65},{2,18},{3,67},{4,20},{5,69},{6,22},{7,71},{8,24},{9,... | collective-permute-start | bytes 688136 | tf_op jit(solution)/shard_map/ppermute | solution.py:36
  58.3 7.2 %collective-permute-start.19 = (f32[224,256]{1,0:T(8,128)S(1)}, f32[224,256]{1,0:T(8,128)S(1)}, u32[]{:S(2)}, u32[]{:S(2)}) collective-permute-start(f32[224,256]{1,0:T(8,128)S(1)} %get-tuple-element.52), channel_id=1, source_target_pairs={{0,8},{1,33},{2,10},{3,35},{4,12},{5,37},{6,14},{7,39},{8,16},{9,4... | collective-permute-start | bytes 688136 | tf_op jit(solution)/shard_map/ppermute | solution.py:36
  59.3 6.5 %collective-permute-start.20 = (f32[224,256]{1,0:T(8,128)S(1)}, f32[224,256]{1,0:T(8,128)S(1)}, u32[]{:S(2)}, u32[]{:S(2)}) collective-permute-start(f32[224,256]{1,0:T(8,128)S(1)} %get-tuple-element.51), channel_id=1, source_target_pairs={{0,24},{1,97},{2,26},{3,99},{4,28},{5,101},{6,30},{7,103},{8,0},{9... | collective-permute-start | bytes 688136 | tf_op jit(solution)/shard_map/ppermute | solution.py:36
  62.3 6.0 %collective-permute-start.9 = (f32[256,256]{1,0:T(8,128)S(1)}, f32[256,256]{1,0:T(8,128)S(1)}, u32[]{:S(2)}, u32[]{:S(2)}) collective-permute-start(f32[256,256]{1,0:T(8,128)S(1)} %slice.62), channel_id=1, source_target_pairs={{7,5},{15,13},{23,21},{31,29},{39,37},{47,45},{55,53},{63,61},{71,... | collective-permute-start | bytes 786440 | tf_op jit(solution)/shard_map/ppermute | solution.py:268
  66.1 7.8 %collective-permute-start.21 = (f32[224,256]{1,0:T(8,128)S(1)}, f32[224,256]{1,0:T(8,128)S(1)}, u32[]{:S(2)}, u32[]{:S(2)}) collective-permute-start(f32[224,256]{1,0:T(8,128)S(1)} %get-tuple-element.60), channel_id=1, source_target_pairs={{0,16},{1,65},{2,18},{3,67},{4,20},{5,69},{6,22},{7,71},{8,24},{9,... | collective-permute-start | bytes 688136 | tf_op jit(solution)/shard_map/ppermute | solution.py:36
  69.3 10.1 %collective-permute-start.11 = (f32[256,256]{1,0:T(8,128)S(1)}, f32[256,256]{1,0:T(8,128)S(1)}, u32[]{:S(2)}, u32[]{:S(2)}) collective-permute-start(f32[256,256]{1,0:T(8,128)S(1)} %add_add_fusion.1), channel_id=1, source_target_pairs={{1,0},{3,2},{5,4},{7,6},{9,8},{11,10},{13,12},{15,14},{17,16},{19,... | collective-permute-start | bytes 786440 | tf_op jit(solution)/shard_map/ppermute | solution.py:270
  70.6 7.3 %collective-permute-start.22 = (f32[224,256]{1,0:T(8,128)S(1)}, f32[224,256]{1,0:T(8,128)S(1)}, u32[]{:S(2)}, u32[]{:S(2)}) collective-permute-start(f32[224,256]{1,0:T(8,128)S(1)} %get-tuple-element.60), channel_id=1, source_target_pairs={{0,8},{1,33},{2,10},{3,35},{4,12},{5,37},{6,14},{7,39},{8,16},{9,4... | collective-permute-start | bytes 688136 | tf_op jit(solution)/shard_map/ppermute | solution.py:36
  72.5 6.0 %collective-permute-start.23 = (f32[224,256]{1,0:T(8,128)S(1)}, f32[224,256]{1,0:T(8,128)S(1)}, u32[]{:S(2)}, u32[]{:S(2)}) collective-permute-start(f32[224,256]{1,0:T(8,128)S(1)} %get-tuple-element.60), channel_id=1, source_target_pairs={{0,24},{1,97},{2,26},{3,99},{4,28},{5,101},{6,30},{7,103},{8,0},{9... | collective-permute-start | bytes 688136 | tf_op jit(solution)/shard_map/ppermute | solution.py:36
  78.5 14.7 %collective-permute-start.24 = (f32[896,256]{1,0:T(8,128)S(1)}, f32[896,256]{1,0:T(8,128)S(1)}, u32[]{:S(2)}, u32[]{:S(2)}) collective-permute-start(f32[896,256]{1,0:T(8,128)S(1)} %bitcast.86), channel_id=1, source_target_pairs={{0,32},{1,9},{2,34},{3,11},{4,36},{5,13},{6,38},{7,15},{8,40},{9,1... | collective-permute-start | bytes 2752520 | tf_op jit(solution)/shard_map/ppermute | solution.py:36
  79.9 24.6 %collective-permute-start.29 = (f32[896,256]{1,0:T(8,128)S(1)}, f32[896,256]{1,0:T(8,128)S(1)}, u32[]{:S(2)}, u32[]{:S(2)}) collective-permute-start(f32[896,256]{1,0:T(8,128)S(1)} %bitcast.87), channel_id=1, source_target_pairs={{0,64},{1,17},{2,66},{3,19},{4,68},{5,21},{6,70},{7,23},{8,72},{9,... | collective-permute-start | bytes 2752520 | tf_op jit(solution)/shard_map/ppermute | solution.py:36
  83.8 20.7 %collective-permute-start.30 = (f32[896,256]{1,0:T(8,128)S(1)}, f32[896,256]{1,0:T(8,128)S(1)}, u32[]{:S(2)}, u32[]{:S(2)}) collective-permute-start(f32[896,256]{1,0:T(8,128)S(1)} %bitcast.88), channel_id=1, source_target_pairs={{0,96},{1,25},{2,98},{3,27},{4,100},{5,29},{6,102},{7,31},{8,104},... | collective-permute-start | bytes 2752520 | tf_op jit(solution)/shard_map/ppermute | solution.py:36
  93.2 11.5 %collective-permute-start.25 = (f32[64,512]{1,0:T(8,128)S(1)}, f32[64,512]{1,0:T(8,128)S(1)}, u32[]{:S(2)}, u32[]{:S(2)}) collective-permute-start(f32[64,512]{1,0:T(8,128)S(1)} %pad_maximum_fusion), channel_id=1, source_target_pairs={{0,4},{1,5},{2,6},{3,7},{4,0},{5,1},{6,2},{7,3},{8,12},{9,13},{10,... | collective-permute-start | bytes 393224 | tf_op jit(solution)/shard_map/ppermute | solution.py:41
  96.2 8.5 %collective-permute-start.26 = (f32[64,512]{1,0:T(8,128)S(1)}, f32[64,512]{1,0:T(8,128)S(1)}, u32[]{:S(2)}, u32[]{:S(2)}) collective-permute-start(f32[64,512]{1,0:T(8,128)S(1)} %pad_maximum_fusion), channel_id=1, source_target_pairs={{0,2},{1,3},{2,4},{3,5},{4,6},{5,7},{6,0},{7,1},{8,10},{9,11},{10,... | collective-permute-start | bytes 393224 | tf_op jit(solution)/shard_map/ppermute | solution.py:41
  96.8 7.9 %collective-permute-start.27 = (f32[64,512]{1,0:T(8,128)S(1)}, f32[64,512]{1,0:T(8,128)S(1)}, u32[]{:S(2)}, u32[]{:S(2)}) collective-permute-start(f32[64,512]{1,0:T(8,128)S(1)} %pad_maximum_fusion), channel_id=1, source_target_pairs={{0,6},{1,7},{2,0},{3,1},{4,2},{5,3},{6,4},{7,5},{8,14},{9,15},{10,... | collective-permute-start | bytes 393224 | tf_op jit(solution)/shard_map/ppermute | solution.py:41
  104.8 2.0 %collective-permute-start.28 = (f32[256,512]{1,0:T(8,128)S(1)}, f32[256,512]{1,0:T(8,128)S(1)}, u32[]{:S(2)}, u32[]{:S(2)}) collective-permute-start(f32[256,512]{1,0:T(8,128)S(1)} %bitcast.91), channel_id=1, source_target_pairs={{0,1},{1,0},{2,3},{3,2},{4,5},{5,4},{6,7},{7,6},{8,9},{9,8},{10,11... | collective-permute-start | bytes 1572872 | tf_op jit(solution)/shard_map/ppermute | solution.py:45
  105.0 1.8 %copy-start.1 = (f32[7,4,64,256]{3,2,1,0:T(8,128)}, f32[7,4,64,256]{3,2,1,0:T(8,128)S(1)}, u32[]{:S(2)}) copy-start(f32[7,4,64,256]{3,2,1,0:T(8,128)S(1)} %constant_dynamic-update-slice_fusion.7) | copy-start | bytes 5505028
  105.1 2.8 %copy-start = (f32[7,4,64,256]{3,2,1,0:T(8,128)}, f32[7,4,64,256]{3,2,1,0:T(8,128)S(1)}, u32[]{:S(2)}) copy-start(f32[7,4,64,256]{3,2,1,0:T(8,128)S(1)} %constant_dynamic-update-slice_fusion.3) | copy-start | bytes 5505028

commit v6 on v5

--- a/solution.py
+++ b/solution.py
@@ -253,7 +253,7 @@
     blocks = pivot_products(after(grad_window, cross), rows_second, rows_first)
     left = own_left + swap_core(other_left)
 
-    cross = cross + lax.ppermute(cross, "col", [(2 * i, 2 * i + 1) for i in range(SIDE)])
+    cross = cross + swap_core(cross)
     others = [lax.ppermute(cross, "col", [(source, last)]) for source in (3, 1, 5)]
     cross = jnp.where(is_last, cross + others[0] + others[1] + others[2], 0.0)
     late = cross.reshape(SIDE, piece, width)

time: 109 us -> 108 us (level)
  starting transfers between devices: 50.8 us -> 49.5 us
    ppermute x1 -> x0, starting transfers between devices: 1.31 us -> none  [local(): lax.ppermute(cross, 'col', [(2 * i, 2 * i + 1) for i in range(SIDE)])]
    ppermute x1 -> x0, waiting for transfers between devices: 1.25 us -> none  [local(): lax.ppermute(cross, 'col', [(2 * i, 2 * i + 1) for i in range(SIDE)])]
    ppermute x2 -> x3, waiting for transfers between devices: 1.5 us -> 2.74 us  [swap_core(): return lax.ppermute(value, 'col', [(i, i ^ 1) for i in range(2 * SIDE)])]
where the time goes in v6:
time: 108 us; the launch traced here: 107 us
  starting transfers between devices  49.5 us (46%)
  waiting for transfers between devices  31.3 us (29%)
  Pallas kernels  14.5 us (13%)
  other arithmetic  4.88 us (5%)
  local copies, waits for them, and re-layouts  4.21 us (4%)
  between operations  1.31 us (1%)
    ppermute x15, starting transfers between devices, shift(): return lax.ppermute(value, ('row', 'col'), pairs(step, swap))  28.8 us
    ppermute x15, waiting for transfers between devices, shift(): return lax.ppermute(value, ('row', 'col'), pairs(step, swap))  23.9 us
    ppermute x6, starting transfers between devices, shift_x(): return lax.ppermute(value, 'col', pairs)  13.9 us
    pallas_call x1, Pallas kernels, pivot_products(): pl.pallas_call(pivot_kernel, in_specs=[hbm] * 3, out_specs=[hbm] * SIDE,...  7.94 us
    pallas_call x1, Pallas kernels, left_products(): pl.pallas_call(left_kernel, in_specs=[hbm] * 5, out_specs=[hbm] * 3, out_...  6.57 us
    ppermute x6, waiting for transfers between devices, shift_x(): return lax.ppermute(value, 'col', pairs)  4.66 us
    ppermute x3, starting transfers between devices, local(): lax.ppermute(cross, 'col', [(source, last)])  2.86 us
    ppermute x3, waiting for transfers between devices, swap_core(): return lax.ppermute(value, 'col', [(i, i ^ 1) for i in range(2 * SIDE)])  2.74 us
  transfers between devices with their start and end apart: 31, of which 13 were waited for; matrix products, arithmetic and copies ran while one was open for 8% of the time, Pallas kernels for 7%

profile of v6, /device:TPU:0, one launch (start us, length us, event | category | flops | bytes accessed | tf_op | source)
XLA Modules:
  0.0 106.6 jit_solution(8736305014816733397)
XLA Ops:
  0.6 6.6 %left_products.1 = (f32[256,512]{1,0:T(8,128)}, f32[256,512]{1,0:T(8,128)}, f32[256,256]{1,0:T(8,128)}) custom-call(f32[512,1792]{1,0:T(8,128)} %window_hbm.2, f32[1792,256]{1,0:T(8,128)} %cols_second_hbm.1, f32[1792,256]{1,0:T(8,128)} %cols_first_hbm.1, f32[512,256]{1,0:T(8,128)} %rows_first_hbm.1, f32[256,256]{1,0:T(8,128)} %inverse_hbm.1), custom_call_target="tpu_custom_call" | custom-call | flops 2818572288 | bytes 7340032 | tf_op jit(solution)/shard_map/left_products/pallas_call | solution.py:206
  7.3 0.5 collective-permute-start
  7.8 1.2 %collective-permute-done.1 = f32[256,256]{1,0:T(8,128)S(1)} collective-permute-done((f32[256,256]{1,0:T(8,128)}, f32[256,256]{1,0:T(8,128)S(1)}, u32[]{:S(2)}, u32[]{:S(2)}) %collective-permute-start.1) | collective-permute-done | bytes 262176 | tf_op jit(solution)/shard_map/ppermute | solution.py:45
  9.0 1.0 add.271
  10.0 0.8 collective-permute-start.2
  10.8 0.7 collective-permute-start.3
  11.5 1.4 %collective-permute-start.4 = (f32[256,256]{1,0:T(8,128)S(1)}, f32[256,256]{1,0:T(8,128)}, u32[]{:S(2)}, u32[]{:S(2)}) collective-permute-start(f32[256,256]{1,0:T(8,128)S(1)} %add.271), channel_id=1, source_target_pairs={{5,7},{13,15},{21,23},{29,31},{37,39},{45,47},{53,55},{61,63},{69,... | collective-permute-start | bytes 786440 | tf_op jit(solution)/shard_map/ppermute | solution.py:257
  12.9 7.9 %pivot_products.1 = (f32[896,256]{1,0:T(8,128)}, f32[896,256]{1,0:T(8,128)}, f32[896,256]{1,0:T(8,128)}, f32[896,256]{1,0:T(8,128)}) custom-call(f32[512,1792]{1,0:T(8,128)} %window_hbm.2, f32[512,256]{1,0:T(8,128)} %rows_second_hbm.1, f32[512,256]{1,0:T(8,128)} %rows_first_hbm.1), custom_call_target="tpu_custom_call" | custom-call | flops 2818572288 | bytes 7340032 | tf_op jit(solution)/shard_map/pivot_products/pallas_call | solution.py:121
  20.9 3.4 %collective-permute-start.12 = (f32[896,256]{1,0:T(8,128)}, f32[896,256]{1,0:T(8,128)S(1)}, u32[]{:S(2)}, u32[]{:S(2)}) collective-permute-start(f32[896,256]{1,0:T(8,128)} %get-tuple-element.35), channel_id=1, source_target_pairs={{0,64},{1,17},{2,66},{3,19},{4,68},{5,21},{6,70},{7,23},{8,72},{9,... | collective-permute-start | bytes 2752520 | tf_op jit(solution)/shard_map/ppermute | solution.py:36
  24.2 0.7 collective-permute-start.13
  25.0 2.6 %collective-permute-start.14 = (f32[896,256]{1,0:T(8,128)}, f32[896,256]{1,0:T(8,128)}, u32[]{:S(2)}, u32[]{:S(2)}) collective-permute-start(f32[896,256]{1,0:T(8,128)} %get-tuple-element.37), channel_id=1, source_target_pairs={{0,96},{1,25},{2,98},{3,27},{4,100},{5,29},{6,102},{7,31},{8,104},... | collective-permute-start | bytes 2752520 | tf_op jit(solution)/shard_map/ppermute | solution.py:36
  27.6 1.0 add_select_fusion
  28.7 0.7 dynamic-slice_bitcast_fusion.7
  29.4 3.1 %collective-permute-start.5 = (f32[64,512]{1,0:T(8,128)S(1)}, f32[64,512]{1,0:T(8,128)S(1)}, u32[]{:S(2)}, u32[]{:S(2)}) collective-permute-start(f32[64,512]{1,0:T(8,128)S(1)} %get-tuple-element.53), channel_id=1, source_target_pairs={{0,4},{1,5},{2,6},{3,7},{4,0},{5,1},{6,2},{7,3},{8,12},{9,13},{10,... | collective-permute-start | bytes 393224 | tf_op jit(solution)/shard_map/ppermute | solution.py:41
  32.5 0.6 collective-permute-start.6
  33.1 2.9 %collective-permute-done.5 = f32[64,512]{1,0:T(8,128)S(1)} collective-permute-done((f32[64,512]{1,0:T(8,128)S(1)}, f32[64,512]{1,0:T(8,128)S(1)}, u32[]{:S(2)}, u32[]{:S(2)}) %collective-permute-start.5) | collective-permute-done | bytes 131104 | tf_op jit(solution)/shard_map/ppermute | solution.py:41
  35.9 3.9 %collective-permute-start.7 = (f32[64,512]{1,0:T(8,128)S(1)}, f32[64,512]{1,0:T(8,128)S(1)}, u32[]{:S(2)}, u32[]{:S(2)}) collective-permute-start(f32[64,512]{1,0:T(8,128)S(1)} %get-tuple-element.54), channel_id=1, source_target_pairs={{0,6},{1,7},{2,0},{3,1},{4,2},{5,3},{6,4},{7,5},{8,14},{9,15},{10,... | collective-permute-start | bytes 393224 | tf_op jit(solution)/shard_map/ppermute | solution.py:41
  39.8 1.0 slice.62
  41.1 1.8 %collective-permute-done.7 = f32[64,512]{1,0:T(8,128)S(1)} collective-permute-done((f32[64,512]{1,0:T(8,128)S(1)}, f32[64,512]{1,0:T(8,128)S(1)}, u32[]{:S(2)}, u32[]{:S(2)}) %collective-permute-start.7) | collective-permute-done | bytes 131104 | tf_op jit(solution)/shard_map/ppermute | solution.py:41
  42.9 0.7 collective-permute-start.10
  43.6 0.7 collective-permute-start.8
  44.3 1.7 %collective-permute-done.13 = f32[896,256]{1,0:T(8,128)} collective-permute-done((f32[896,256]{1,0:T(8,128)}, f32[896,256]{1,0:T(8,128)}, u32[]{:S(2)}, u32[]{:S(2)}) %collective-permute-start.13) | collective-permute-done | bytes 917536 | tf_op jit(solution)/shard_map/ppermute | solution.py:36
  46.0 2.5 %collective-permute-start.15 = (f32[64,256]{1,0:T(8,128)}, f32[64,256]{1,0:T(8,128)S(1)}, u32[]{:S(2)}, u32[]{:S(2)}) collective-permute-start(f32[64,256]{1,0:T(8,128)} %get-tuple-element.56), channel_id=1, source_target_pairs={{0,64},{1,17},{2,66},{3,19},{4,68},{5,21},{6,70},{7,23},{8,72},{9,... | collective-permute-start | bytes 196616 | tf_op jit(solution)/shard_map/ppermute | solution.py:36
  48.5 2.0 %collective-permute-start.17 = (f32[64,256]{1,0:T(8,128)}, f32[64,256]{1,0:T(8,128)S(1)}, u32[]{:S(2)}, u32[]{:S(2)}) collective-permute-start(f32[64,256]{1,0:T(8,128)} %get-tuple-element.57), channel_id=1, source_target_pairs={{0,96},{1,25},{2,98},{3,27},{4,100},{5,29},{6,102},{7,31},{8,104},... | collective-permute-start | bytes 196616 | tf_op jit(solution)/shard_map/ppermute | solution.py:36
  50.5 1.7 %add_add_fusion = f32[896,256]{1,0:T(8,128)S(1)} fusion(f32[896,256]{1,0:T(8,128)} %collective-permute-done.14, f32[896,256]{1,0:T(8,128)} %collective-permute-done.13, f32[896,256]{1,0:T(8,128)S(1)} %copy-done.4, f32[896,256]{1,0:T(8,128)S(1)} %collective-permute-done.12), kind=kLoop, calls=%fused_computation | loop fusion | flops 688128 | bytes 4587520 | tf_op jit(solution)/shard_map/add | solution.py:281
  52.2 0.7 collective-permute-done.17
  53.1 4.0 %collective-permute-start.18 = (f32[224,256]{1,0:T(8,128)S(1)}, f32[224,256]{1,0:T(8,128)S(1)}, u32[]{:S(2)}, u32[]{:S(2)}) collective-permute-start(f32[224,256]{1,0:T(8,128)S(1)} %get-tuple-element.50), channel_id=1, source_target_pairs={{0,16},{1,65},{2,18},{3,67},{4,20},{5,69},{6,22},{7,71},{8,24},{9,... | collective-permute-start | bytes 688136 | tf_op jit(solution)/shard_map/ppermute | solution.py:36
  57.0 1.0 collective-permute-start.19
  58.0 2.2 %collective-permute-start.20 = (f32[224,256]{1,0:T(8,128)S(1)}, f32[224,256]{1,0:T(8,128)S(1)}, u32[]{:S(2)}, u32[]{:S(2)}) collective-permute-start(f32[224,256]{1,0:T(8,128)S(1)} %get-tuple-element.51), channel_id=1, source_target_pairs={{0,24},{1,97},{2,26},{3,99},{4,28},{5,101},{6,30},{7,103},{8,0},{9... | collective-permute-start | bytes 688136 | tf_op jit(solution)/shard_map/ppermute | solution.py:36
  60.5 0.5 collective-permute-done.18
  61.0 0.7 collective-permute-start.9
  61.7 2.6 %collective-permute-done.19 = f32[224,256]{1,0:T(8,128)S(1)} collective-permute-done((f32[224,256]{1,0:T(8,128)S(1)}, f32[224,256]{1,0:T(8,128)S(1)}, u32[]{:S(2)}, u32[]{:S(2)}) %collective-permute-start.19) | collective-permute-done | bytes 229408 | tf_op jit(solution)/shard_map/ppermute | solution.py:36
  64.9 2.2 %collective-permute-start.21 = (f32[224,256]{1,0:T(8,128)S(1)}, f32[224,256]{1,0:T(8,128)S(1)}, u32[]{:S(2)}, u32[]{:S(2)}) collective-permute-start(f32[224,256]{1,0:T(8,128)S(1)} %get-tuple-element.60), channel_id=1, source_target_pairs={{0,16},{1,65},{2,18},{3,67},{4,20},{5,69},{6,22},{7,71},{8,24},{9,... | collective-permute-start | bytes 688136 | tf_op jit(solution)/shard_map/ppermute | solution.py:36
  67.0 1.0 add_add_fusion.1
  68.1 1.3 %collective-permute-start.11 = (f32[256,256]{1,0:T(8,128)S(1)}, f32[256,256]{1,0:T(8,128)S(1)}, u32[]{:S(2)}, u32[]{:S(2)}) collective-permute-start(f32[256,256]{1,0:T(8,128)S(1)} %add_add_fusion.1), channel_id=1, source_target_pairs={{1,0},{3,2},{5,4},{7,6},{9,8},{11,10},{13,12},{15,14},{17,16},{19,... | collective-permute-start | bytes 786440 | tf_op jit(solution)/shard_map/ppermute | solution.py:270
  69.4 1.9 %collective-permute-start.22 = (f32[224,256]{1,0:T(8,128)S(1)}, f32[224,256]{1,0:T(8,128)S(1)}, u32[]{:S(2)}, u32[]{:S(2)}) collective-permute-start(f32[224,256]{1,0:T(8,128)S(1)} %get-tuple-element.60), channel_id=1, source_target_pairs={{0,8},{1,33},{2,10},{3,35},{4,12},{5,37},{6,14},{7,39},{8,16},{9,4... | collective-permute-start | bytes 688136 | tf_op jit(solution)/shard_map/ppermute | solution.py:36
  71.2 1.5 %collective-permute-start.23 = (f32[224,256]{1,0:T(8,128)S(1)}, f32[224,256]{1,0:T(8,128)S(1)}, u32[]{:S(2)}, u32[]{:S(2)}) collective-permute-start(f32[224,256]{1,0:T(8,128)S(1)} %get-tuple-element.60), channel_id=1, source_target_pairs={{0,24},{1,97},{2,26},{3,99},{4,28},{5,101},{6,30},{7,103},{8,0},{9... | collective-permute-start | bytes 688136 | tf_op jit(solution)/shard_map/ppermute | solution.py:36
  72.7 4.0 %collective-permute-done.22 = f32[224,256]{1,0:T(8,128)S(1)} collective-permute-done((f32[224,256]{1,0:T(8,128)S(1)}, f32[224,256]{1,0:T(8,128)S(1)}, u32[]{:S(2)}, u32[]{:S(2)}) %collective-permute-start.22) | collective-permute-done | bytes 229408 | tf_op jit(solution)/shard_map/ppermute | solution.py:36
  76.7 0.6 collective-permute-done.23
  77.3 0.9 collective-permute-start.24
  78.6 3.9 %collective-permute-start.29 = (f32[896,256]{1,0:T(8,128)S(1)}, f32[896,256]{1,0:T(8,128)S(1)}, u32[]{:S(2)}, u32[]{:S(2)}) collective-permute-start(f32[896,256]{1,0:T(8,128)S(1)} %bitcast.87), channel_id=1, source_target_pairs={{0,64},{1,17},{2,66},{3,19},{4,68},{5,21},{6,70},{7,23},{8,72},{9,... | collective-permute-start | bytes 2752520 | tf_op jit(solution)/shard_map/ppermute | solution.py:36
  83.2 8.7 %collective-permute-done.24 = f32[896,256]{1,0:T(8,128)S(1)} collective-permute-done((f32[896,256]{1,0:T(8,128)S(1)}, f32[896,256]{1,0:T(8,128)S(1)}, u32[]{:S(2)}, u32[]{:S(2)}) %collective-permute-start.24) | collective-permute-done | bytes 917536 | tf_op jit(solution)/shard_map/ppermute | solution.py:36
  91.9 3.0 %collective-permute-start.25 = (f32[64,512]{1,0:T(8,128)S(1)}, f32[64,512]{1,0:T(8,128)S(1)}, u32[]{:S(2)}, u32[]{:S(2)}) collective-permute-start(f32[64,512]{1,0:T(8,128)S(1)} %pad_maximum_fusion), channel_id=1, source_target_pairs={{0,4},{1,5},{2,6},{3,7},{4,0},{5,1},{6,2},{7,3},{8,12},{9,13},{10,... | collective-permute-start | bytes 393224 | tf_op jit(solution)/shard_map/ppermute | solution.py:41
  94.9 0.6 collective-permute-start.26
  95.5 2.6 %collective-permute-start.27 = (f32[64,512]{1,0:T(8,128)S(1)}, f32[64,512]{1,0:T(8,128)S(1)}, u32[]{:S(2)}, u32[]{:S(2)}) collective-permute-start(f32[64,512]{1,0:T(8,128)S(1)} %pad_maximum_fusion), channel_id=1, source_target_pairs={{0,6},{1,7},{2,0},{3,1},{4,2},{5,3},{6,4},{7,5},{8,14},{9,15},{10,... | collective-permute-start | bytes 393224 | tf_op jit(solution)/shard_map/ppermute | solution.py:41
  98.3 4.9 %collective-permute-done.29 = f32[896,256]{1,0:T(8,128)S(1)} collective-permute-done((f32[896,256]{1,0:T(8,128)S(1)}, f32[896,256]{1,0:T(8,128)S(1)}, u32[]{:S(2)}, u32[]{:S(2)}) %collective-permute-start.29) | collective-permute-done | bytes 917536 | tf_op jit(solution)/shard_map/ppermute | solution.py:36
  104.0 1.5 %collective-permute-done.28 = f32[256,512]{1,0:T(8,128)S(1)} collective-permute-done((f32[256,512]{1,0:T(8,128)S(1)}, f32[256,512]{1,0:T(8,128)S(1)}, u32[]{:S(2)}, u32[]{:S(2)}) %collective-permute-start.28) | collective-permute-done | bytes 524320 | tf_op jit(solution)/shard_map/ppermute | solution.py:45
  105.6 1.0 fusion.21
  (70 shorter events, 3.2 us)
Async XLA Ops:
  7.2 1.8 %collective-permute-start.1 = (f32[256,256]{1,0:T(8,128)}, f32[256,256]{1,0:T(8,128)S(1)}, u32[]{:S(2)}, u32[]{:S(2)}) collective-permute-start(f32[256,256]{1,0:T(8,128)} %get-tuple-element.30), channel_id=1, source_target_pairs={{0,1},{1,0},{2,3},{3,2},{4,5},{5,4},{6,7},{7,6},{8,9},{9,8},{10,11... | collective-permute-start | bytes 786440 | tf_op jit(solution)/shard_map/ppermute | solution.py:45
  7.3 16.9 %collective-permute-start = (f32[256,512]{1,0:T(8,128)}, f32[256,512]{1,0:T(8,128)S(1)}, u32[]{:S(2)}, u32[]{:S(2)}) collective-permute-start(f32[256,512]{1,0:T(8,128)} %get-tuple-element.29), channel_id=1, source_target_pairs={{0,1},{1,0},{2,3},{3,2},{4,5},{5,4},{6,7},{7,6},{8,9},{9,8},{10,11... | collective-permute-start | bytes 1572872 | tf_op jit(solution)/shard_map/ppermute | solution.py:45
  10.0 14.9 %copy-start.5 = (f32[256,512]{1,0:T(8,128)S(1)}, f32[256,512]{1,0:T(8,128)}, u32[]{:S(2)}) copy-start(f32[256,512]{1,0:T(8,128)} %get-tuple-element.28) | copy-start | bytes 1572868
  10.0 15.0 %collective-permute-start.2 = (f32[256,256]{1,0:T(8,128)S(1)}, f32[256,256]{1,0:T(8,128)S(1)}, u32[]{:S(2)}, u32[]{:S(2)}) collective-permute-start(f32[256,256]{1,0:T(8,128)S(1)} %add.271), channel_id=1, source_target_pairs={{3,7},{11,15},{19,23},{27,31},{35,39},{43,47},{51,55},{59,63},{67,... | collective-permute-start | bytes 786440 | tf_op jit(solution)/shard_map/ppermute | solution.py:257
  10.8 16.8 %collective-permute-start.3 = (f32[256,256]{1,0:T(8,128)S(1)}, f32[256,256]{1,0:T(8,128)S(1)}, u32[]{:S(2)}, u32[]{:S(2)}) collective-permute-start(f32[256,256]{1,0:T(8,128)S(1)} %add.271), channel_id=1, source_target_pairs={{1,7},{9,15},{17,23},{25,31},{33,39},{41,47},{49,55},{57,63},{65,7... | collective-permute-start | bytes 786440 | tf_op jit(solution)/shard_map/ppermute | solution.py:257
  11.5 16.1 %collective-permute-start.4 = (f32[256,256]{1,0:T(8,128)S(1)}, f32[256,256]{1,0:T(8,128)}, u32[]{:S(2)}, u32[]{:S(2)}) collective-permute-start(f32[256,256]{1,0:T(8,128)S(1)} %add.271), channel_id=1, source_target_pairs={{5,7},{13,15},{21,23},{29,31},{37,39},{45,47},{53,55},{61,63},{69,... | collective-permute-start | bytes 786440 | tf_op jit(solution)/shard_map/ppermute | solution.py:257
  20.9 22.7 %collective-permute-start.12 = (f32[896,256]{1,0:T(8,128)}, f32[896,256]{1,0:T(8,128)S(1)}, u32[]{:S(2)}, u32[]{:S(2)}) collective-permute-start(f32[896,256]{1,0:T(8,128)} %get-tuple-element.35), channel_id=1, source_target_pairs={{0,64},{1,17},{2,66},{3,19},{4,68},{5,21},{6,70},{7,23},{8,72},{9,... | collective-permute-start | bytes 2752520 | tf_op jit(solution)/shard_map/ppermute | solution.py:36
  24.2 21.8 %collective-permute-start.13 = (f32[896,256]{1,0:T(8,128)}, f32[896,256]{1,0:T(8,128)}, u32[]{:S(2)}, u32[]{:S(2)}) collective-permute-start(f32[896,256]{1,0:T(8,128)} %get-tuple-element.36), channel_id=1, source_target_pairs={{0,32},{1,9},{2,34},{3,11},{4,36},{5,13},{6,38},{7,15},{8,40},{9,1... | collective-permute-start | bytes 2752520 | tf_op jit(solution)/shard_map/ppermute | solution.py:36
  25.0 25.5 %copy-start.4 = (f32[896,256]{1,0:T(8,128)S(1)}, f32[896,256]{1,0:T(8,128)}, u32[]{:S(2)}) copy-start(f32[896,256]{1,0:T(8,128)} %get-tuple-element.34) | copy-start | bytes 2752516
  25.0 23.5 %collective-permute-start.14 = (f32[896,256]{1,0:T(8,128)}, f32[896,256]{1,0:T(8,128)}, u32[]{:S(2)}, u32[]{:S(2)}) collective-permute-start(f32[896,256]{1,0:T(8,128)} %get-tuple-element.37), channel_id=1, source_target_pairs={{0,96},{1,25},{2,98},{3,27},{4,100},{5,29},{6,102},{7,31},{8,104},... | collective-permute-start | bytes 2752520 | tf_op jit(solution)/shard_map/ppermute | solution.py:36
  29.4 6.6 %collective-permute-start.5 = (f32[64,512]{1,0:T(8,128)S(1)}, f32[64,512]{1,0:T(8,128)S(1)}, u32[]{:S(2)}, u32[]{:S(2)}) collective-permute-start(f32[64,512]{1,0:T(8,128)S(1)} %get-tuple-element.53), channel_id=1, source_target_pairs={{0,4},{1,5},{2,6},{3,7},{4,0},{5,1},{6,2},{7,3},{8,12},{9,13},{10,... | collective-permute-start | bytes 393224 | tf_op jit(solution)/shard_map/ppermute | solution.py:41
  32.5 8.5 %collective-permute-start.6 = (f32[64,512]{1,0:T(8,128)S(1)}, f32[64,512]{1,0:T(8,128)S(1)}, u32[]{:S(2)}, u32[]{:S(2)}) collective-permute-start(f32[64,512]{1,0:T(8,128)S(1)} %get-tuple-element.55), channel_id=1, source_target_pairs={{0,2},{1,3},{2,4},{3,5},{4,6},{5,7},{6,0},{7,1},{8,10},{9,11},{10,... | collective-permute-start | bytes 393224 | tf_op jit(solution)/shard_map/ppermute | solution.py:41
  35.9 6.9 %collective-permute-start.7 = (f32[64,512]{1,0:T(8,128)S(1)}, f32[64,512]{1,0:T(8,128)S(1)}, u32[]{:S(2)}, u32[]{:S(2)}) collective-permute-start(f32[64,512]{1,0:T(8,128)S(1)} %get-tuple-element.54), channel_id=1, source_target_pairs={{0,6},{1,7},{2,0},{3,1},{4,2},{5,3},{6,4},{7,5},{8,14},{9,15},{10,... | collective-permute-start | bytes 393224 | tf_op jit(solution)/shard_map/ppermute | solution.py:41
  41.0 11.2 %collective-permute-start.16 = (f32[64,256]{1,0:T(8,128)}, f32[64,256]{1,0:T(8,128)S(1)}, u32[]{:S(2)}, u32[]{:S(2)}) collective-permute-start(f32[64,256]{1,0:T(8,128)} %get-tuple-element.58), channel_id=1, source_target_pairs={{0,32},{1,9},{2,34},{3,11},{4,36},{5,13},{6,38},{7,15},{8,40},{9,1... | collective-permute-start | bytes 196616 | tf_op jit(solution)/shard_map/ppermute | solution.py:36
  42.9 24.1 %collective-permute-start.10 = (f32[256,256]{1,0:T(8,128)S(1)}, f32[256,256]{1,0:T(8,128)S(1)}, u32[]{:S(2)}, u32[]{:S(2)}) collective-permute-start(f32[256,256]{1,0:T(8,128)S(1)} %slice.62), channel_id=1, source_target_pairs={{7,3},{15,11},{23,19},{31,27},{39,35},{47,43},{55,51},{63,59},{71,... | collective-permute-start | bytes 786440 | tf_op jit(solution)/shard_map/ppermute | solution.py:268
  43.6 23.4 %collective-permute-start.8 = (f32[256,256]{1,0:T(8,128)S(1)}, f32[256,256]{1,0:T(8,128)S(1)}, u32[]{:S(2)}, u32[]{:S(2)}) collective-permute-start(f32[256,256]{1,0:T(8,128)S(1)} %slice.62), channel_id=1, source_target_pairs={{7,1},{15,9},{23,17},{31,25},{39,33},{47,41},{55,49},{63,57},{71,6... | collective-permute-start | bytes 786440 | tf_op jit(solution)/shard_map/ppermute | solution.py:268
  46.0 6.2 %collective-permute-start.15 = (f32[64,256]{1,0:T(8,128)}, f32[64,256]{1,0:T(8,128)S(1)}, u32[]{:S(2)}, u32[]{:S(2)}) collective-permute-start(f32[64,256]{1,0:T(8,128)} %get-tuple-element.56), channel_id=1, source_target_pairs={{0,64},{1,17},{2,66},{3,19},{4,68},{5,21},{6,70},{7,23},{8,72},{9,... | collective-permute-start | bytes 196616 | tf_op jit(solution)/shard_map/ppermute | solution.py:36
  48.5 4.5 %collective-permute-start.17 = (f32[64,256]{1,0:T(8,128)}, f32[64,256]{1,0:T(8,128)S(1)}, u32[]{:S(2)}, u32[]{:S(2)}) collective-permute-start(f32[64,256]{1,0:T(8,128)} %get-tuple-element.57), channel_id=1, source_target_pairs={{0,96},{1,25},{2,98},{3,27},{4,100},{5,29},{6,102},{7,31},{8,104},... | collective-permute-start | bytes 196616 | tf_op jit(solution)/shard_map/ppermute | solution.py:36
  52.2 8.1 %copy-start.3 = (f32[256,256]{1,0:T(8,128)S(1)}, f32[256,256]{1,0:T(8,128)}, u32[]{:S(2)}) copy-start(f32[256,256]{1,0:T(8,128)} %inverse_hbm.1) | copy-start | bytes 786436
  52.2 12.4 %copy-start.2 = (f32[256,256]{1,0:T(8,128)S(1)}, f32[256,256]{1,0:T(8,128)}, u32[]{:S(2)}) copy-start(f32[256,256]{1,0:T(8,128)} %param.14) | copy-start | bytes 786436
  53.1 8.0 %collective-permute-start.18 = (f32[224,256]{1,0:T(8,128)S(1)}, f32[224,256]{1,0:T(8,128)S(1)}, u32[]{:S(2)}, u32[]{:S(2)}) collective-permute-start(f32[224,256]{1,0:T(8,128)S(1)} %get-tuple-element.50), channel_id=1, source_target_pairs={{0,16},{1,65},{2,18},{3,67},{4,20},{5,69},{6,22},{7,71},{8,24},{9,... | collective-permute-start | bytes 688136 | tf_op jit(solution)/shard_map/ppermute | solution.py:36
  57.0 7.2 %collective-permute-start.19 = (f32[224,256]{1,0:T(8,128)S(1)}, f32[224,256]{1,0:T(8,128)S(1)}, u32[]{:S(2)}, u32[]{:S(2)}) collective-permute-start(f32[224,256]{1,0:T(8,128)S(1)} %get-tuple-element.52), channel_id=1, source_target_pairs={{0,8},{1,33},{2,10},{3,35},{4,12},{5,37},{6,14},{7,39},{8,16},{9,4... | collective-permute-start | bytes 688136 | tf_op jit(solution)/shard_map/ppermute | solution.py:36
  58.0 6.5 %collective-permute-start.20 = (f32[224,256]{1,0:T(8,128)S(1)}, f32[224,256]{1,0:T(8,128)S(1)}, u32[]{:S(2)}, u32[]{:S(2)}) collective-permute-start(f32[224,256]{1,0:T(8,128)S(1)} %get-tuple-element.51), channel_id=1, source_target_pairs={{0,24},{1,97},{2,26},{3,99},{4,28},{5,101},{6,30},{7,103},{8,0},{9... | collective-permute-start | bytes 688136 | tf_op jit(solution)/shard_map/ppermute | solution.py:36
  61.0 6.0 %collective-permute-start.9 = (f32[256,256]{1,0:T(8,128)S(1)}, f32[256,256]{1,0:T(8,128)S(1)}, u32[]{:S(2)}, u32[]{:S(2)}) collective-permute-start(f32[256,256]{1,0:T(8,128)S(1)} %slice.62), channel_id=1, source_target_pairs={{7,5},{15,13},{23,21},{31,29},{39,37},{47,45},{55,53},{63,61},{71,... | collective-permute-start | bytes 786440 | tf_op jit(solution)/shard_map/ppermute | solution.py:268
  64.9 7.8 %collective-permute-start.21 = (f32[224,256]{1,0:T(8,128)S(1)}, f32[224,256]{1,0:T(8,128)S(1)}, u32[]{:S(2)}, u32[]{:S(2)}) collective-permute-start(f32[224,256]{1,0:T(8,128)S(1)} %get-tuple-element.60), channel_id=1, source_target_pairs={{0,16},{1,65},{2,18},{3,67},{4,20},{5,69},{6,22},{7,71},{8,24},{9,... | collective-permute-start | bytes 688136 | tf_op jit(solution)/shard_map/ppermute | solution.py:36
  68.1 10.1 %collective-permute-start.11 = (f32[256,256]{1,0:T(8,128)S(1)}, f32[256,256]{1,0:T(8,128)S(1)}, u32[]{:S(2)}, u32[]{:S(2)}) collective-permute-start(f32[256,256]{1,0:T(8,128)S(1)} %add_add_fusion.1), channel_id=1, source_target_pairs={{1,0},{3,2},{5,4},{7,6},{9,8},{11,10},{13,12},{15,14},{17,16},{19,... | collective-permute-start | bytes 786440 | tf_op jit(solution)/shard_map/ppermute | solution.py:270
  69.4 7.3 %collective-permute-start.22 = (f32[224,256]{1,0:T(8,128)S(1)}, f32[224,256]{1,0:T(8,128)S(1)}, u32[]{:S(2)}, u32[]{:S(2)}) collective-permute-start(f32[224,256]{1,0:T(8,128)S(1)} %get-tuple-element.60), channel_id=1, source_target_pairs={{0,8},{1,33},{2,10},{3,35},{4,12},{5,37},{6,14},{7,39},{8,16},{9,4... | collective-permute-start | bytes 688136 | tf_op jit(solution)/shard_map/ppermute | solution.py:36
  71.2 6.0 %collective-permute-start.23 = (f32[224,256]{1,0:T(8,128)S(1)}, f32[224,256]{1,0:T(8,128)S(1)}, u32[]{:S(2)}, u32[]{:S(2)}) collective-permute-start(f32[224,256]{1,0:T(8,128)S(1)} %get-tuple-element.60), channel_id=1, source_target_pairs={{0,24},{1,97},{2,26},{3,99},{4,28},{5,101},{6,30},{7,103},{8,0},{9... | collective-permute-start | bytes 688136 | tf_op jit(solution)/shard_map/ppermute | solution.py:36
  77.3 14.7 %collective-permute-start.24 = (f32[896,256]{1,0:T(8,128)S(1)}, f32[896,256]{1,0:T(8,128)S(1)}, u32[]{:S(2)}, u32[]{:S(2)}) collective-permute-start(f32[896,256]{1,0:T(8,128)S(1)} %bitcast.86), channel_id=1, source_target_pairs={{0,32},{1,9},{2,34},{3,11},{4,36},{5,13},{6,38},{7,15},{8,40},{9,1... | collective-permute-start | bytes 2752520 | tf_op jit(solution)/shard_map/ppermute | solution.py:36
  78.6 24.6 %collective-permute-start.29 = (f32[896,256]{1,0:T(8,128)S(1)}, f32[896,256]{1,0:T(8,128)S(1)}, u32[]{:S(2)}, u32[]{:S(2)}) collective-permute-start(f32[896,256]{1,0:T(8,128)S(1)} %bitcast.87), channel_id=1, source_target_pairs={{0,64},{1,17},{2,66},{3,19},{4,68},{5,21},{6,70},{7,23},{8,72},{9,... | collective-permute-start | bytes 2752520 | tf_op jit(solution)/shard_map/ppermute | solution.py:36
  82.5 20.7 %collective-permute-start.30 = (f32[896,256]{1,0:T(8,128)S(1)}, f32[896,256]{1,0:T(8,128)S(1)}, u32[]{:S(2)}, u32[]{:S(2)}) collective-permute-start(f32[896,256]{1,0:T(8,128)S(1)} %bitcast.88), channel_id=1, source_target_pairs={{0,96},{1,25},{2,98},{3,27},{4,100},{5,29},{6,102},{7,31},{8,104},... | collective-permute-start | bytes 2752520 | tf_op jit(solution)/shard_map/ppermute | solution.py:36
  91.9 11.5 %collective-permute-start.25 = (f32[64,512]{1,0:T(8,128)S(1)}, f32[64,512]{1,0:T(8,128)S(1)}, u32[]{:S(2)}, u32[]{:S(2)}) collective-permute-start(f32[64,512]{1,0:T(8,128)S(1)} %pad_maximum_fusion), channel_id=1, source_target_pairs={{0,4},{1,5},{2,6},{3,7},{4,0},{5,1},{6,2},{7,3},{8,12},{9,13},{10,... | collective-permute-start | bytes 393224 | tf_op jit(solution)/shard_map/ppermute | solution.py:41
  94.9 8.5 %collective-permute-start.26 = (f32[64,512]{1,0:T(8,128)S(1)}, f32[64,512]{1,0:T(8,128)S(1)}, u32[]{:S(2)}, u32[]{:S(2)}) collective-permute-start(f32[64,512]{1,0:T(8,128)S(1)} %pad_maximum_fusion), channel_id=1, source_target_pairs={{0,2},{1,3},{2,4},{3,5},{4,6},{5,7},{6,0},{7,1},{8,10},{9,11},{10,... | collective-permute-start | bytes 393224 | tf_op jit(solution)/shard_map/ppermute | solution.py:41
  95.5 7.9 %collective-permute-start.27 = (f32[64,512]{1,0:T(8,128)S(1)}, f32[64,512]{1,0:T(8,128)S(1)}, u32[]{:S(2)}, u32[]{:S(2)}) collective-permute-start(f32[64,512]{1,0:T(8,128)S(1)} %pad_maximum_fusion), channel_id=1, source_target_pairs={{0,6},{1,7},{2,0},{3,1},{4,2},{5,3},{6,4},{7,5},{8,14},{9,15},{10,... | collective-permute-start | bytes 393224 | tf_op jit(solution)/shard_map/ppermute | solution.py:41
  103.5 2.0 %collective-permute-start.28 = (f32[256,512]{1,0:T(8,128)S(1)}, f32[256,512]{1,0:T(8,128)S(1)}, u32[]{:S(2)}, u32[]{:S(2)}) collective-permute-start(f32[256,512]{1,0:T(8,128)S(1)} %bitcast.91), channel_id=1, source_target_pairs={{0,1},{1,0},{2,3},{3,2},{4,5},{5,4},{6,7},{7,6},{8,9},{9,8},{10,11... | collective-permute-start | bytes 1572872 | tf_op jit(solution)/shard_map/ppermute | solution.py:45
  103.8 1.8 %copy-start.1 = (f32[7,4,64,256]{3,2,1,0:T(8,128)}, f32[7,4,64,256]{3,2,1,0:T(8,128)S(1)}, u32[]{:S(2)}) copy-start(f32[7,4,64,256]{3,2,1,0:T(8,128)S(1)} %constant_dynamic-update-slice_fusion.7) | copy-start | bytes 5505028
  103.8 2.8 %copy-start = (f32[7,4,64,256]{3,2,1,0:T(8,128)}, f32[7,4,64,256]{3,2,1,0:T(8,128)S(1)}, u32[]{:S(2)}) copy-start(f32[7,4,64,256]{3,2,1,0:T(8,128)S(1)} %constant_dynamic-update-slice_fusion.3) | copy-start | bytes 5505028
